TPU v7x, 256 devices: a whole 4x4x8 slice. The times are simulated.
256 devices in a mesh: wide: 128 (over y, z, x), cols: 2 (over core).
Axes of the slice: x: 4, y: 4, z: 8, core: 2. Of those that a mesh axis runs over, the one named last changes fastest.
Arguments:
- factor: float32 [262144, 256], P('wide', 'cols')
- gates: float32 [8, 128, 128], replicated, may hold values from -0.5 to 0.5
- gate_layout: int32 [2048], P('wide'), may hold values from 0 to 7
- jump_masks: int32 [3], replicated, may hold values from 1 to 127
- jump_rates: float32 [3], replicated, may hold values from 0.1 to 0.4
- sketch_perm: int32 [1024], replicated, may hold values from 0 to 1023, each once
- bases: float32 [8, 64, 64], replicated, may hold values from -0.75 to 0.75
- basis_index: int32 [128, 32], P('wide'), may hold values from 0 to 7
Outputs:
- new_factor: float32 [262144, 256], P('wide', 'cols')
- weights: float32 [128, 2048], P('wide', 'cols')
Inputs may be any that keep to these rules, and one draw needn't show every extreme that they name: `jump_masks`: nonzero bit masks over the high qubits. `sketch_perm`: each value appears once.
All inputs are finite; a program needn't handle non-finite values.
Results may differ from a plain program's by a relative error of at most 0.0003.
Values sent between devices are 32-bit elements; how exact they have to be, the bound alone decides.
No kernel may reach another device: no remote copies, remote signals or barrier semaphores. Data moves between devices by JAX's collectives and lax.ppermute only.
A program may use at most 64 MiB of HBM per device.

v0:
```python
import jax
import jax.numpy as jnp
from jax import lax
from jax.sharding import PartitionSpec as P

NS_ITERS = 7


HIGH = lax.Precision.HIGHEST


def apply_blocks(mats, index, data):
    chosen = jnp.take(mats, index, axis=0)
    return jnp.einsum("bij,bjc->bic", chosen, data, precision=HIGH)


def flip_rows(data, mask, count):
    shaped = data.reshape(count, data.shape[0] // count, data.shape[1])
    source = jnp.bitwise_xor(jnp.arange(count, dtype=jnp.int32), mask)
    return jnp.take(shaped, source, axis=0).reshape(data.shape)


def sketch_table(sketch_perm, rank):
    target = sketch_perm % rank
    sign = 1.0 - 2.0 * (sketch_perm // rank % 2).astype(jnp.float32)
    hit = target[:, None] == jnp.arange(rank, dtype=jnp.int32)[None, :]
    return jnp.where(hit, sign[:, None], jnp.zeros((), jnp.float32))


def mixed_stack(source, table, first, coefs, masks, count):
    rank = table.shape[1]
    width = source.shape[1]
    sources = []
    blocks = []
    for k in range(len(coefs)):
        flipped = source if k == 0 else flip_rows(source, masks[k - 1], count)
        sources.append(coefs[k] * flipped)
        blocks.append(lax.dynamic_slice_in_dim(table, k * rank + first, width, 0))
    joined = jnp.concatenate(sources, axis=1)
    table_rows = jnp.concatenate(blocks, axis=0)
    return jnp.dot(joined, table_rows, precision=HIGH, preferred_element_type=jnp.float32)


def newton_root(mat, eye, iters):
    fro = jnp.sqrt(jnp.sum(mat * mat))
    approx = mat / (fro + 1e-06)
    inverse = eye
    for step in range(iters):
        middle = 1.5 * eye - 0.5 * jnp.dot(inverse, approx, precision=HIGH)
        approx = jnp.dot(approx, middle, precision=HIGH)
        inverse = jnp.dot(middle, inverse, precision=HIGH)
    return (approx, inverse, fro)


def per_device(factor, gates, gate_layout, jump_masks, jump_rates, sketch_perm, bases, basis_index):
    rows, width = factor.shape
    order = gates.shape[1]
    count = lax.axis_size("wide")
    halves = lax.axis_size("cols")
    column_index = lax.axis_index("cols")
    rank = width * halves
    jumps = jump_rates.shape[0]
    gated = apply_blocks(gates, gate_layout, factor.reshape(rows // order, order, width)).reshape(
        rows, width
    )
    moved = lax.all_to_all(gated, "wide", split_axis=0, concat_axis=0, tiled=True)
    keep = 1.0 - 0.5 * jnp.sum(jump_rates)
    coefs = [keep] + [jnp.sqrt(jump_rates[k]) for k in range(jumps)]
    table = sketch_table(sketch_perm, rank)
    first = column_index * width
    terms = mixed_stack(moved, table, first, coefs, jump_masks, count)
    sketch_own = lax.psum_scatter(terms, "cols", scatter_dimension=1, tiled=True)
    sketch = lax.all_gather(sketch_own, "cols", axis=1, tiled=True)
    share = rows // halves
    mine = lax.dynamic_slice_in_dim(sketch, column_index * share, share, 0)
    gram_part = lax.dot_general(
        mine, mine, (((0,), (0,)), ((), ())), precision=HIGH, preferred_element_type=jnp.float32
    )
    gram = lax.psum(gram_part, ("wide", "cols"))
    eye = jnp.eye(rank, dtype=jnp.float32)
    unused, inverse, fro = newton_root(gram, eye, NS_ITERS)
    parts = []
    for k in range(jumps + 1):
        right = moved if k == 0 else flip_rows(moved, jump_masks[k - 1], count)
        parts.append(
            coefs[k]
            * lax.dot_general(
                sketch,
                right,
                (((0,), (0,)), ((), ())),
                precision=HIGH,
                preferred_element_type=jnp.float32,
            )
        )
    proj_own = jnp.concatenate(parts, axis=1)
    proj_sum = lax.psum(proj_own, "wide")
    coeff = lax.dot_general(
        inverse,
        proj_sum,
        (((0,), (0,)), ((), ())),
        precision=HIGH,
        preferred_element_type=jnp.float32,
    )
    core_part = lax.dot_general(
        coeff, coeff, (((1,), (1,)), ((), ())), precision=HIGH, preferred_element_type=jnp.float32
    )
    core = lax.psum(core_part, "cols")
    approx_two, unused_two, fro_two = newton_root(core, eye, NS_ITERS)
    root_own = jnp.sqrt(fro_two + 1e-06) * lax.dynamic_slice_in_dim(approx_two, first, width, 1)
    mixing_own = jnp.dot(inverse, root_own, precision=HIGH)
    new_own = jnp.dot(sketch, mixing_own, precision=HIGH)
    rot = bases.shape[1]
    rotated = apply_blocks(bases, basis_index.reshape(-1), new_own.reshape(rows // rot, rot, width))
    partial_value = (jnp.sum(rotated * rotated, axis=2) / rank).reshape(1, rows)
    weights = lax.psum_scatter(partial_value, "cols", scatter_dimension=1, tiled=True)
    return (new_own, weights)


def solution(mesh):
    return jax.shard_map(
        per_device,
        mesh=mesh,
        in_specs=(P("wide", "cols"), P(), P("wide"), P(), P(), P(), P(), P("wide", None)),
        out_specs=(P("wide", "cols"), P("wide", "cols")),
        check_vma=False,
    )
```

profile of v0, /device:TPU:1, one launch (start us, length us, event | category | flops | bytes accessed | tf_op | source)
XLA Modules:
  0.0 657.7 jit_solution(18310592391966807667)
XLA Ops:
  7.2 0.7 compare_select_fusion.5
  7.9 0.7 compare_and_fusion.4
  8.6 1.7 gather_fusion
  10.3 2.2 fusion.12
  12.5 16.3 %all-to-all-start = ((f32[128,16,128]{2,1,0:T(8,128)}), f32[128,16,128]{2,1,0:T(8,128)S(1)}, u32[]{:S(2)}, u32[]{:S(2)}) async-start(f32[128,16,128]{2,1,0:T(8,128)} %bitcast.1), calls=%async_computation | async-start | bytes 2097152 | tf_op jit(solution)/shard_map/all_to_all | solution.py:66
  28.9 0.7 fusion.47
  31.7 0.6 reduce_sum.36
  32.9 0.7 fusion.46
  33.6 0.6 compare_select_fusion.2
  34.3 1.2 compare_and_fusion.2
  35.5 1.3 compare_select_fusion
  36.7 1.8 compare_and_fusion
  38.9 0.7 constant_dynamic-slice_fusion.3
  39.6 16.5 %all-to-all-done = f32[128,16,128]{2,1,0:T(8,128)S(1)} async-done(((f32[128,16,128]{2,1,0:T(8,128)}), f32[128,16,128]{2,1,0:T(8,128)S(1)}, u32[]{:S(2)}, u32[]{:S(2)}) %all-to-all-start) | async-done | bytes 1048608 | tf_op jit(solution)/shard_map/all_to_all | solution.py:66
  56.1 0.8 gather_fusion.3
  56.8 0.9 broadcast_select_fusion.1
  57.7 1.0 copy-done.4
  58.7 1.0 broadcast_multiply_fusion.1
  59.7 0.8 gather_fusion.4
  60.7 1.0 copy-done.5
  61.7 1.0 broadcast_multiply_fusion
  62.7 0.8 gather_fusion.2
  63.9 0.8 copy-done.7
  64.7 0.6 copy-done.12
  65.7 4.9 fusion
  70.6 13.1 %reduce-scatter.5.cloned.1.call-done = f32[2048,128]{1,0:T(8,128)} async-done(((f32[2048,256]{1,0:T(8,128)}), f32[2048,128]{1,0:T(8,128)}) %reduce-scatter.5.cloned.1.call-update) | async-done | bytes 1048592 | tf_op jit(solution)/shard_map/reduce_scatter | solution.py:72
  83.8 19.0 %all-gather.2.cloned.1.call-done = f32[2048,256]{1,0:T(8,128)} async-done(((f32[2048,128]{1,0:T(8,128)}), f32[2048,256]{1,0:T(8,128)}) %all-gather.2.cloned.1.call-update) | async-done | bytes 2097168 | tf_op jit(solution)/shard_map/all_gather | solution.py:73
  102.7 4.1 fusion.10
  106.9 0.5 all-reduce.6.cloned.1.call-start
  107.4 5.4 convolution_multiply_fusion.16
  112.8 3.4 convolution_multiply_fusion.15
  116.3 3.4 convolution_multiply_fusion.17
  119.7 3.6 convolution_multiply_fusion.18
  123.3 0.8 pad_maximum_fusion
  124.2 234.4 %all-reduce.4.cloned.1.call-done = f32[256,256]{1,0:T(8,128)} async-done(((f32[256,256]{1,0:T(8,128)}), f32[256,256]{1,0:T(8,128)}) %all-reduce.4.cloned.1.call-update) | async-done | bytes 262160 | tf_op jit(solution)/shard_map/psum | solution.py:79
  358.6 1.6 multiply_reduce_fusion.1
  360.9 1.3 select_subtract_fusion.13
  362.5 1.3 fusion.31
  363.8 0.4 select_subtract_fusion.12
  365.0 0.4 select_subtract_fusion.11
  366.2 0.4 select_subtract_fusion.10
  367.3 0.4 select_subtract_fusion.9
  368.5 0.4 select_subtract_fusion.8
  369.7 0.4 select_subtract_fusion.7
  370.0 1.1 fusion.58
  371.1 206.0 %all-reduce.6.cloned.1.call-done = f32[256,512]{1,0:T(8,128)} async-done(((f32[256,512]{1,0:T(8,128)}), f32[256,512]{1,0:T(8,128)}) %all-reduce.6.cloned.1.call-update) | async-done | bytes 524304 | tf_op jit(solution)/shard_map/psum | solution.py:96
  577.2 1.7 fusion.59
  578.9 1.3 fusion.60
  580.6 1.6 gather_fusion.1
  582.2 30.0 %all-reduce.8.cloned.1.call-done = f32[256,256]{1,0:T(8,128)} async-done(((f32[256,256]{1,0:T(8,128)}), f32[256,256]{1,0:T(8,128)}) %all-reduce.8.cloned.1.call-update) | async-done | bytes 262160 | tf_op jit(solution)/shard_map/psum | solution.py:107
  612.2 1.6 multiply_reduce_fusion
  614.5 1.3 select_subtract_fusion.6
  616.0 1.3 fusion.32
  617.4 0.4 select_subtract_fusion.5
  622.0 0.4 select_subtract_fusion.1
  622.4 1.1 fusion.70
  623.9 1.3 select_subtract_fusion
  625.7 1.4 fusion.28
  627.1 1.8 fusion.72
  629.0 1.0 copy-done.9
  629.9 1.5 fusion.8
  631.5 2.0 div.43
  633.5 15.3 %reduce-scatter.7.cloned.1.call-done = f32[1024,1]{1,0:T(8,128)} async-done(((f32[2048,1]{1,0:T(8,128)}), f32[1024,1]{1,0:T(8,128)}) %reduce-scatter.7.cloned.1.call-update) | async-done | bytes 4112
  648.8 1.8 copy.11
  (85 shorter events, 11.1 us)
Async XLA Ops:
  7.2 3.1 copy-start
  10.3 18.6 %copy-start.16 = (f32[3]{0:T(128)S(1)}, f32[3]{0:T(128)}, u32[]{:S(2)}) copy-start(f32[3]{0:T(128)} %param.14) | copy-start | bytes 40
  10.3 22.6 %copy-start.17 = (s32[3]{0:T(128)S(1)}, s32[3]{0:T(128)}, u32[]{:S(2)}) copy-start(s32[3]{0:T(128)} %param.13) | copy-start | bytes 40
  10.3 28.2 %copy-start.15 = (s32[1024]{0:T(1024)S(1)}, s32[1024]{0:T(1024)}, u32[]{:S(2)}) copy-start(s32[1024]{0:T(1024)} %param.15) | copy-start | bytes 12292
  12.5 43.6 %all-to-all-start = ((f32[128,16,128]{2,1,0:T(8,128)}), f32[128,16,128]{2,1,0:T(8,128)S(1)}, u32[]{:S(2)}, u32[]{:S(2)}) async-start(f32[128,16,128]{2,1,0:T(8,128)} %bitcast.1), calls=%async_computation | async-start | bytes 2097152 | tf_op jit(solution)/shard_map/all_to_all | solution.py:66
  28.8 54.8 %reduce-scatter.5.cloned.1.call-start = ((), (), s32[]{:S(2)}) async-start(), calls=%async_computation.3 | async-start | bytes 3145728 | tf_op jit(solution)/shard_map/reduce_scatter | solution.py:72
  56.1 7.7 %copy-start.2 = (f32[128,16,128]{2,1,0:T(8,128)}, f32[128,16,128]{2,1,0:T(8,128)S(1)}, u32[]{:S(2)}) copy-start(f32[128,16,128]{2,1,0:T(8,128)S(1)} %all-to-all-done) | copy-start | bytes 3145732
  57.7 1.0 copy-start.4
  60.7 1.0 copy-start.5
  61.7 1.8 copy-start.18
  63.7 1.0 copy-start.7
  63.7 1.6 copy-start.12
  63.8 1.9 copy-start.13
  63.8 1.9 copy-start.14
  70.5 13.2 %copy-start.19 = (s32[1,32]{1,0:T(1,128)S(1)}, s32[1,32]{1,0:T(1,128)}, u32[]{:S(2)}) copy-start(s32[1,32]{1,0:T(1,128)} %param.17) | copy-start | bytes 388
  70.6 32.2 %all-gather.2.cloned.1.call-start = ((), (), s32[]{:S(2)}) async-start(), calls=%async_computation.4 | async-start | bytes 3145728 | tf_op jit(solution)/shard_map/all_gather | solution.py:73
  83.7 274.9 %all-reduce.4.cloned.1.call-start = ((), (), s32[]{:S(2)}) async-start(), calls=%async_computation.5 | async-start | bytes 524288 | tf_op jit(solution)/shard_map/psum | solution.py:79
  106.9 5.9 copy-start.1
  106.9 470.3 %all-reduce.6.cloned.1.call-start = ((), (), s32[]{:S(2)}) async-start(), calls=%async_computation.6 | async-start | bytes 1048576 | tf_op jit(solution)/shard_map/psum | solution.py:96
  107.4 5.4 copy-start.6
  112.8 3.5 copy-start.8
  116.3 3.5 copy-start.3
  124.2 488.0 %all-reduce.8.cloned.1.call-start = ((), (), s32[]{:S(2)}) async-start(), calls=%async_computation.7 | async-start | bytes 524288 | tf_op jit(solution)/shard_map/psum | solution.py:107
  369.6 210.9 %copy-start.11 = (f32[8,64,64]{2,1,0:T(8,128)S(1)}, f32[8,64,64]{2,1,0:T(8,128)}, u32[]{:S(2)}) copy-start(f32[8,64,64]{2,1,0:T(8,128)} %param.16) | copy-start | bytes 393220
  580.3 68.5 %reduce-scatter.7.cloned.1.call-start = ((), (), s32[]{:S(2)}) async-start(), calls=%async_computation.8 | async-start | bytes 1572864
  625.7 4.3 copy-start.10
  629.0 1.0 copy-start.9
Sparse Core Ops, SparseCore 0:
  70.7 12.9 reduce-scatter.4
  85.6 17.0 all-gather.1
  109.1 249.4 all-reduce.3
  365.3 211.7 all-reduce.5
  580.4 31.7 all-reduce.7
  633.6 15.1 reduce-scatter.6
where the time goes:
time: 666 us; the launch traced here: 658 us
  waiting for transfers between devices  534 us (80%)
  matrix products  55.9 us (8%)
  between operations  19.3 us (3%)
  starting transfers between devices  17.3 us (3%)
  local copies, waits for them, and re-layouts  16.1 us (2%)
  other arithmetic  14.9 us (2%)
    psum x1, waiting for transfers between devices, per_device(): gram = lax.psum(gram_part, ('wide', 'cols'))  234 us
    psum x1, waiting for transfers between devices, per_device(): proj_sum = lax.psum(proj_own, 'wide')  206 us
    psum x1, waiting for transfers between devices, per_device(): core = lax.psum(core_part, 'cols')  30 us
    all_gather x1, waiting for transfers between devices, per_device(): sketch = lax.all_gather(sketch_own, 'cols', axis=1, tiled=True)  19 us
    all_to_all x1, waiting for transfers between devices, per_device(): lax.all_to_all(gated, 'wide', split_axis=0, concat_axis=0, tiled=True)  16.5 us
    all_to_all x1, starting transfers between devices, per_device(): lax.all_to_all(gated, 'wide', split_axis=0, concat_axis=0, tiled=True)  16.3 us
    dot_general x4, matrix products, per_device(): lax.dot_general(sketch, right, (((0,), (0,)), ((), ())), precision=HIGH,...  15.9 us
    unnamed x7, waiting for transfers between devices  15.4 us
  transfers between devices with their start and end apart: 7, of which 7 were waited for; matrix products, arithmetic and copies ran while one was open for 6% of the time, Pallas kernels for 0%

commit v1 on v0

v1 whole, which is shorter than its diff:
```python
import jax
import jax.numpy as jnp
from jax import lax
from jax.experimental import pallas as pl
from jax.experimental.pallas import tpu as pltpu
from jax.sharding import PartitionSpec as P

NS_ITERS = 7
F32 = jnp.float32
BF16 = jnp.bfloat16
NN = (((1,), (0,)), ((), ()))
NT = (((1,), (1,)), ((), ()))


def split(x):
    hi = x.astype(BF16)
    return hi, (x - hi.astype(F32)).astype(BF16)


def dot(a, b, dims=NN):
    return lax.dot_general(a, b, dims, preferred_element_type=F32)


def mul3(a, b, dims=NN):
    return dot(a[0], b[0], dims) + (dot(a[1], b[0], dims) + dot(a[0], b[1], dims))


def gate_kernel(order, layout, gates, factor, out):
    def block(b, carry):
        rows = pl.ds(pl.multiple_of(b * order, order), order)
        out[rows, :] = mul3(split(gates[layout[b]]), split(factor[rows, :]))
        return carry

    lax.fori_loop(0, factor.shape[0] // order, block, 0)


def apply_gates(gates, layout, factor):
    order = gates.shape[1]
    return pl.pallas_call(
        lambda *refs: gate_kernel(order, *refs),
        out_shape=jax.ShapeDtypeStruct(factor.shape, F32),
        in_specs=[
            pl.BlockSpec(memory_space=pltpu.SMEM),
            pl.BlockSpec(memory_space=pltpu.VMEM),
            pl.BlockSpec(memory_space=pltpu.VMEM),
        ],
        out_specs=pl.BlockSpec(memory_space=pltpu.VMEM),
        name="gates",
    )(layout, gates, factor)


def stack_kernel(masks, rates, moved, table, sketch, proj, high, low):
    count, halves, lows, width = moved.shape
    rank = halves * width
    jumps = masks.shape[0]
    total = rates[0]
    for k in range(1, jumps):
        total = total + rates[k]
    coefs = [jnp.full((2 * lows, width), 1.0 - 0.5 * total, F32)]
    for k in range(jumps):
        coefs.append(jnp.sqrt(jnp.full((2 * lows, width), rates[k], F32)))

    def pair(p, carry):
        rows = pl.ds(pl.multiple_of(p * 2 * lows, 2 * lows), 2 * lows)
        for k in range(jumps + 1):
            flip = 0 if k == 0 else masks[k - 1]
            first, second = (2 * p) ^ flip, (2 * p + 1) ^ flip
            for c in range(halves):
                value = coefs[k] * jnp.concatenate([moved[first, c], moved[second, c]], axis=0)
                cols = slice(k * rank + c * width, k * rank + (c + 1) * width)
                high[rows, cols], low[rows, cols] = split(value)
        return carry

    lax.fori_loop(0, count // 2, pair, 0, unroll=4)
    value = dot(high[...], table[...]) + dot(low[...], table[...])
    sketch[...] = value
    left = split(value.T)
    for k in range(jumps + 1):
        cols = slice(k * rank, (k + 1) * rank)
        proj[:, cols] = mul3(left, (high[:, cols], low[:, cols]))


def stack_products(masks, rates, moved, table):
    count, halves, lows, width = moved.shape
    rows, rank = count * lows, halves * width
    columns = table.shape[0]
    vmem = pl.BlockSpec(memory_space=pltpu.VMEM)
    smem = pl.BlockSpec(memory_space=pltpu.SMEM)
    return pl.pallas_call(
        stack_kernel,
        out_shape=(
            jax.ShapeDtypeStruct((rows, rank), F32),
            jax.ShapeDtypeStruct((rank, columns), F32),
        ),
        in_specs=[smem, smem, vmem, vmem],
        out_specs=(vmem, vmem),
        scratch_shapes=[pltpu.VMEM((rows, columns), BF16), pltpu.VMEM((rows, columns), BF16)],
        compiler_params=pltpu.CompilerParams(vmem_limit_bytes=40 << 20),
        name="stack",
    )(masks, rates, moved, table)


def rotate_kernel(where, index, sketch, bases, sk_high, sk_low, rot_high, rot_low, rotated):
    halves, count, lows, rank = sketch.shape
    order = bases.shape[1]
    group = order // (halves * lows)
    blocks = rotated.shape[0] // order
    own = where[0]

    def block(b, carry):
        first = own * (count // halves) + b * group
        parts = []
        for g in range(group):
            for c in range(halves):
                parts.append(sketch[c, first + g])
        data = jnp.concatenate(parts, axis=0)
        rows = pl.ds(pl.multiple_of(b * order, order), order)
        rotated[rows, :] = mul3(split(bases[index[0, own * blocks + b]]), split(data))
        return carry

    lax.fori_loop(0, blocks, block, 0)
    rot_high[...], rot_low[...] = split(rotated[...].T)
    for c in range(halves):
        sk_high[c], sk_low[c] = split(sketch[c].reshape(count * lows, rank))


def rotate_sketch(where, index, sketch, bases):
    halves, count, lows, rank = sketch.shape
    rows = count * lows
    vmem = pl.BlockSpec(memory_space=pltpu.VMEM)
    smem = pl.BlockSpec(memory_space=pltpu.SMEM)
    return pl.pallas_call(
        rotate_kernel,
        out_shape=(
            jax.ShapeDtypeStruct((halves, rows, rank), BF16),
            jax.ShapeDtypeStruct((halves, rows, rank), BF16),
            jax.ShapeDtypeStruct((rank, rows), BF16),
            jax.ShapeDtypeStruct((rank, rows), BF16),
        ),
        in_specs=[smem, smem, vmem, vmem],
        out_specs=(vmem, vmem, vmem, vmem),
        scratch_shapes=[pltpu.VMEM((rows, rank), F32)],
        compiler_params=pltpu.CompilerParams(vmem_limit_bytes=40 << 20),
        name="rotate",
    )(where, index, sketch, bases)


def frobenius(mat):
    return jnp.sqrt(jnp.sum(jnp.sum(mat * mat, axis=0, keepdims=True), axis=1, keepdims=True))


def eye(n):
    return (
        lax.broadcasted_iota(jnp.int32, (n, n), 0) == lax.broadcasted_iota(jnp.int32, (n, n), 1)
    ).astype(F32)


def newton(mat, value):
    t = mat
    held = None
    for step in range(NS_ITERS):
        last = step == NS_ITERS - 1
        right = split(t)
        if step == 0:
            once = 1.5 * t - 0.5 * mul3(right, right)
            held = 1.5 * eye(t.shape[0]) - 0.5 * t if value is None else once
        else:
            if not last:
                once = 1.5 * t - 0.5 * mul3(right, right)
            held = 1.5 * held - 0.5 * mul3(split(held), right)
        if not last:
            t = 1.5 * once - 0.5 * mul3(split(once), right)
    return held


def output_kernel(where, proj, table, sk_high, sk_low, rot_high, rot_low, new, weights):
    rank = proj.shape[0]
    halves = sk_high.shape[0]
    width = rank // halves
    p = split(proj[...])
    gram = dot(p[0], table[...]) + dot(p[1], table[...])
    inverse = newton(gram / (frobenius(gram) + 1e-6), None)
    inv = split(inverse)
    coeff = split(mul3(inv, p))
    core = mul3(coeff, coeff, NT)
    shift = frobenius(core) + 1e-6
    root = split(newton(core / shift, "approx"))
    scale = jnp.sqrt(shift)
    mixing = scale * mul3(inv, root)
    turned = split(scale * mul3(root, inv))
    own = jnp.where(where[0] == 0, mixing[:, :width], mixing[:, width:])
    own = split(own)
    rot = mul3(turned, (rot_high[...], rot_low[...]))
    weights[...] = jnp.sum(rot * rot, axis=0, keepdims=True) / rank
    for c in range(halves):
        value = mul3((sk_high[c], sk_low[c]), own)
        new[:, c] = value.reshape(new.shape[0], new.shape[2], width)


def outputs(where, proj, table, sk_high, sk_low, rot_high, rot_low, lows):
    halves, rows, rank = sk_high.shape
    vmem = pl.BlockSpec(memory_space=pltpu.VMEM)
    smem = pl.BlockSpec(memory_space=pltpu.SMEM)
    return pl.pallas_call(
        output_kernel,
        out_shape=(
            jax.ShapeDtypeStruct((rows // lows, halves, lows, rank // halves), F32),
            jax.ShapeDtypeStruct((1, rows), F32),
        ),
        in_specs=[smem] + [vmem] * 6,
        out_specs=(vmem, vmem),
        compiler_params=pltpu.CompilerParams(vmem_limit_bytes=40 << 20),
        name="outputs",
    )(where, proj, table, sk_high, sk_low, rot_high, rot_low)


def sketch_table(sketch_perm, rank):
    target = sketch_perm % rank
    sign = 1.0 - 2.0 * (sketch_perm // rank % 2).astype(F32)
    hit = target[:, None] == jnp.arange(rank, dtype=jnp.int32)[None, :]
    return jnp.where(hit, sign[:, None], jnp.zeros((), F32)).astype(BF16)


def per_device(factor, gates, gate_layout, jump_masks, jump_rates, sketch_perm, bases, basis_index):
    rows, width = factor.shape
    count = lax.axis_size("wide")
    halves = lax.axis_size("cols")
    rank = width * halves
    lows = rows // (count * halves)
    where = lax.axis_index("cols").astype(jnp.int32).reshape(1)
    gated = apply_gates(gates, gate_layout, factor)
    pieces = gated.reshape(count * halves, lows, width)
    moved = lax.all_to_all(pieces, ("wide", "cols"), split_axis=0, concat_axis=0, tiled=True)
    moved = moved.reshape(count, halves, lows, width)
    table = sketch_table(sketch_perm, rank)
    sketch_own, proj_own = stack_products(jump_masks, jump_rates, moved, table)
    proj = lax.psum(proj_own, ("wide", "cols"))
    sketch = lax.all_gather(sketch_own, "cols", axis=0, tiled=False)
    sketch = sketch.reshape(halves, count, lows, rank)
    sk_high, sk_low, rot_high, rot_low = rotate_sketch(where, basis_index, sketch, bases)
    new, weights = outputs(where, proj, table, sk_high, sk_low, rot_high, rot_low, lows)
    return new.reshape(rows, width), weights


def solution(mesh):
    return jax.shard_map(
        per_device,
        mesh=mesh,
        in_specs=(P("wide", "cols"), P(), P("wide"), P(), P(), P(), P(), P("wide", None)),
        out_specs=(P("wide", "cols"), P("wide", "cols")),
        check_vma=False,
    )
```

time: 666 us -> 345 us (0.52); the launches traced: 658 us -> 344 us
  waiting for transfers between devices: 534 us -> 279 us
  matrix products: 55.9 us -> 0 us
  Pallas kernels: 0 us -> 29.1 us
  other arithmetic: 14.9 us -> 0.36 us
  local copies, waits for them, and re-layouts: 16.1 us -> 4.68 us
    psum x3 -> x1, waiting for transfers between devices: 470 us -> 237 us  [per_device(): proj = lax.psum(proj_own, ('wide', 'cols'))]
    dot_general x52 -> x0, matrix products: 55.9 us -> none  [the longest x4 15.9 us: per_device(): lax.dot_general(sketch, right, (((0,), (0,)), ((), ())), precision=HIGH,...]
    pallas_call x0 -> x4, Pallas kernels: none -> 29.1 us  [the longest x1 13 us: outputs(): pl.pallas_call(output_kernel, out_shape=(jax.ShapeDtypeStruct((rows // lo...]
    unnamed x7 -> x2, waiting for transfers between devices: 15.4 us -> 0.36 us
    all_to_all x1, waiting for transfers between devices: 16.5 us -> 30.6 us  [per_device(): lax.all_to_all(pieces, ('wide', 'cols'), split_axis=0, concat_axis=0, til...]
    reduce_scatter x1 -> x0, waiting for transfers between devices: 13.1 us -> none  [per_device(): lax.psum_scatter(terms, 'cols', scatter_dimension=1, tiled=True)]
    all_gather x1, waiting for transfers between devices: 19 us -> 10.6 us  [per_device(): sketch = lax.all_gather(sketch_own, 'cols', axis=0, tiled=False)]
  transfers between devices with their start and end apart: 7 -> 3, of which waited for: 7 -> 3; matrix products, arithmetic and copies ran while one was open for 6% -> 0% of each run, Pallas kernels for 0% -> 1%
where the time goes in v1:
time: 345 us; the launch traced here: 344 us
  waiting for transfers between devices  279 us (81%)
  Pallas kernels  29.1 us (8%)
  starting transfers between devices  15.9 us (5%)
  between operations  15.6 us (5%)
  local copies, waits for them, and re-layouts  4.68 us (1%)
    psum x1, waiting for transfers between devices, per_device(): proj = lax.psum(proj_own, ('wide', 'cols'))  237 us
    all_to_all x1, waiting for transfers between devices, per_device(): lax.all_to_all(pieces, ('wide', 'cols'), split_axis=0, concat_axis=0, til...  30.6 us
    all_to_all x1, starting transfers between devices, per_device(): lax.all_to_all(pieces, ('wide', 'cols'), split_axis=0, concat_axis=0, til...  15.7 us
    pallas_call x1, Pallas kernels, outputs(): pl.pallas_call(output_kernel, out_shape=(jax.ShapeDtypeStruct((rows // lo...  13 us
    all_gather x1, waiting for transfers between devices, per_device(): sketch = lax.all_gather(sketch_own, 'cols', axis=0, tiled=False)  10.6 us
    pallas_call x1, Pallas kernels, stack_products(): pl.pallas_call(stack_kernel, out_shape=(jax.ShapeDtypeStruct((rows, rank)...  6.96 us
  transfers between devices with their start and end apart: 3, of which 3 were waited for; matrix products, arithmetic and copies ran while one was open for 0% of the time, Pallas kernels for 1%

profile of v1, /device:TPU:1, one launch (start us, length us, event | category | flops | bytes accessed | tf_op | source)
XLA Modules:
  0.0 344.2 jit_solution(6177409346861635550)
XLA Ops:
  8.0 0.0 copy-start.8
  8.0 0.0 copy-start.6
  8.0 0.0 copy-start.5
  8.0 5.1 %gates.1 = f32[2048,128]{1,0:T(8,128)} custom-call(s32[16]{0:T(128)} %refs_0_.1, f32[8,128,128]{2,1,0:T(8,128)} %refs_1_.1, f32[2048,128]{1,0:T(8,128)} %refs_2_.1), custom_call_target="tpu_custom_call" | custom-call | tf_op jit(solution)/shard_map/gates/pallas_call | solution.py:39
  13.1 15.7 %all-to-all-start = ((f32[256,8,128]{2,1,0:T(8,128)}), f32[256,8,128]{2,1,0:T(8,128)S(1)}, u32[]{:S(2)}, u32[]{:S(2)}) async-start(f32[256,8,128]{2,1,0:T(8,128)} %bitcast.7), calls=%async_computation | async-start | bytes 2097152 | tf_op jit(solution)/shard_map/all_to_all | solution.py:233
  28.8 0.0 all-gather.3.cloned.1.call-start
  28.9 0.0 copy-done.8
  28.9 0.0 copy-start.4
  28.9 0.0 copy-start.7
  28.9 0.3 select_convert_fusion.table
  29.3 30.6 %all-to-all-done = f32[256,8,128]{2,1,0:T(8,128)S(1)} async-done(((f32[256,8,128]{2,1,0:T(8,128)}), f32[256,8,128]{2,1,0:T(8,128)S(1)}, u32[]{:S(2)}, u32[]{:S(2)}) %all-to-all-start) | async-done | bytes 1048608 | tf_op jit(solution)/shard_map/all_to_all | solution.py:233
  59.9 0.0 copy-done.6
  59.9 0.0 copy-done.5
  59.9 7.0 %stack.1 = (f32[1024,256]{1,0:T(8,128)}, f32[256,1024]{1,0:T(8,128)}) custom-call(s32[3]{0:T(128)S(1)} %copy-done.5, f32[3]{0:T(128)S(1)} %copy-done.6, f32[128,2,8,128]{3,2,1,0:T(8,128)S(1)} %bitcast.5, bf16[1024,256]{1,0:T(8,128)(2,1)S(1)} %select_convert_fusion.table), custom_call_target="tpu_custom_call" | custom-call | tf_op jit(solution)/shard_map/stack/pallas_call | solution.py:89
  66.9 0.0 all-gather.3.cloned.1.call-update
  66.9 0.2 all-reduce.2.cloned.1.call-start
  67.1 0.3 all-reduce.2.cloned.1.call-update
  67.5 10.6 %all-gather.3.cloned.1.call-done = f32[2048,256]{1,0:T(8,128)} async-done(((f32[1024,256]{1,0:T(8,128)}), f32[2048,256]{1,0:T(8,128)}) %all-gather.3.cloned.1.call-update) | async-done | bytes 2097168 | tf_op jit(solution)/shard_map/all_gather | solution.py:238
  78.1 0.0 copy-done.4
  78.1 0.0 copy-done.7
  78.1 0.0 copy-start
  78.1 1.6 copy-done
  79.7 4.1 %rotate.1 = (bf16[2,1024,256]{2,1,0:T(8,128)(2,1)S(1)}, bf16[2,1024,256]{2,1,0:T(8,128)(2,1)S(1)}, bf16[256,1024]{1,0:T(8,128)(2,1)S(1)}, bf16[256,1024]{1,0:T(8,128)(2,1)S(1)}) custom-call(s32[1]{0:T(128)} %bitcast.where, s32[1,32]{1,0:T(1,128)S(1)} %copy-done.7, f32[2,128,8,256]{3,2,1,0:T(8,128)S(1)} %bitcast.6, f32[8,64,64]{2,1,0:T(8,128)S(1)} %copy-done.4), custom_call_target="tpu_custom_call" | custom-call | tf_op jit(solution)/shard_map/rotate/pallas_call | solution.py:132
  83.8 0.0 copy-start.2
  83.8 0.8 copy-done.2
  84.6 236.9 %all-reduce.2.cloned.1.call-done.proj = f32[256,1024]{1,0:T(8,128)} async-done(((f32[256,1024]{1,0:T(8,128)}), f32[256,1024]{1,0:T(8,128)}) %all-reduce.2.cloned.1.call-update) | async-done | bytes 1048592 | tf_op jit(solution)/shard_map/psum | solution.py:237
  321.5 0.0 copy-start.1
  321.5 1.2 copy-done.1
  322.8 0.0 copy-start.3
  322.8 1.0 copy-done.3
  323.8 13.0 %outputs.1 = (f32[128,2,8,128]{3,2,1,0:T(8,128)}, f32[1,1024]{1,0:T(1,128)}) custom-call(s32[1]{0:T(128)} %bitcast.where, f32[256,1024]{1,0:T(8,128)S(1)} %copy-done.1, bf16[1024,256]{1,0:T(8,128)(2,1)S(1)} %select_convert_fusion.table, bf16[2,1024,256]{2,1,0:T(8,128)(2,1)S(1)} %get-tuple-element.12.sk_high, ...), custom_call_target="tpu_custom_call" | custom-call | tf_op jit(solution)/shard_map/outputs/pallas_call | solution.py:204
  (2 shorter events, 0.0 us)
Async XLA Ops:
  8.0 20.9 %copy-start.8 = (s32[1024]{0:T(1024)S(1)}, s32[1024]{0:T(1024)}, u32[]{:S(2)}) copy-start(s32[1024]{0:T(1024)} %param.13) | copy-start | bytes 12292
  8.0 51.9 %copy-start.6 = (f32[3]{0:T(128)S(1)}, f32[3]{0:T(128)}, u32[]{:S(2)}) copy-start(f32[3]{0:T(128)} %rates.1) | copy-start | bytes 40
  8.0 51.9 %copy-start.5 = (s32[3]{0:T(128)S(1)}, s32[3]{0:T(128)}, u32[]{:S(2)}) copy-start(s32[3]{0:T(128)} %masks.1) | copy-start | bytes 40
  13.1 46.8 %all-to-all-start = ((f32[256,8,128]{2,1,0:T(8,128)}), f32[256,8,128]{2,1,0:T(8,128)S(1)}, u32[]{:S(2)}, u32[]{:S(2)}) async-start(f32[256,8,128]{2,1,0:T(8,128)} %bitcast.7), calls=%async_computation | async-start | bytes 2097152 | tf_op jit(solution)/shard_map/all_to_all | solution.py:233
  28.8 49.3 %all-gather.3.cloned.1.call-start = ((), (), s32[]{:S(2)}) async-start(), calls=%async_computation.2 | async-start | bytes 3145728 | tf_op jit(solution)/shard_map/all_gather | solution.py:238
  28.9 49.2 %copy-start.4 = (f32[8,64,64]{2,1,0:T(8,128)S(1)}, f32[8,64,64]{2,1,0:T(8,128)}, u32[]{:S(2)}) copy-start(f32[8,64,64]{2,1,0:T(8,128)} %bases.1) | copy-start | bytes 393220
  28.9 49.2 %copy-start.7 = (s32[1,32]{1,0:T(1,128)S(1)}, s32[1,32]{1,0:T(1,128)}, u32[]{:S(2)}) copy-start(s32[1,32]{1,0:T(1,128)} %index.1) | copy-start | bytes 388
  66.9 254.6 %all-reduce.2.cloned.1.call-start = ((), (), s32[]{:S(2)}) async-start(), calls=%async_computation.1 | async-start | bytes 2097152 | tf_op jit(solution)/shard_map/psum | solution.py:237
  78.1 1.6 copy-start
  83.8 0.8 copy-start.2
  321.5 1.2 copy-start.1
  322.8 1.0 copy-start.3
Sparse Core Ops, SparseCore 0:
  67.0 11.0 all-gather.2
Sparse Core Ops, SparseCore 1:
  72.8 248.7 all-reduce.1

commit v2 on v1

v2 whole, which is shorter than its diff:
```python
import jax
import jax.numpy as jnp
from jax import lax
from jax.experimental import pallas as pl
from jax.experimental.pallas import tpu as pltpu
from jax.sharding import PartitionSpec as P

NS_ITERS = 7
F32 = jnp.float32
BF16 = jnp.bfloat16
NN = (((1,), (0,)), ((), ()))
NT = (((1,), (1,)), ((), ()))


def split(x):
    hi = x.astype(BF16)
    return hi, (x - hi.astype(F32)).astype(BF16)


def dot(a, b, dims=NN):
    return lax.dot_general(a, b, dims, preferred_element_type=F32)


def mul3(a, b, dims=NN):
    return dot(a[0], b[0], dims) + (dot(a[1], b[0], dims) + dot(a[0], b[1], dims))


def gate_kernel(order, where, layout, gates, factor, keep, send):
    lows = keep.shape[1]
    group = order // (2 * lows)
    mine = where[0] == 0
    for b in range(factor.shape[0] // order):
        high, low = split(factor[b * order : (b + 1) * order, :])
        left = jnp.concatenate(split(gates[layout[b]]), axis=1)
        right = jnp.concatenate(
            [
                jnp.concatenate([high, low], axis=1),
                jnp.concatenate([high, jnp.zeros_like(high)], axis=1),
            ],
            axis=0,
        )
        both = dot(left, right)
        value = both[:, : high.shape[1]] + both[:, high.shape[1] :]
        value = value.reshape(group, 2, lows, high.shape[1])
        hs = slice(b * group, (b + 1) * group)
        keep[hs] = jnp.where(mine, value[:, 0], value[:, 1])
        send[hs] = jnp.where(mine, value[:, 1], value[:, 0])


def apply_gates(where, gates, layout, factor, count):
    order = gates.shape[1]
    rows, width = factor.shape
    vmem = pl.BlockSpec(memory_space=pltpu.VMEM)
    smem = pl.BlockSpec(memory_space=pltpu.SMEM)
    half = jax.ShapeDtypeStruct((count, rows // (2 * count), width), F32)
    return pl.pallas_call(
        lambda *refs: gate_kernel(order, *refs),
        out_shape=(half, half),
        in_specs=[smem, smem, vmem, vmem],
        out_specs=(vmem, vmem),
        name="gates",
    )(where, layout, gates, factor)


def join_kernel(where, kept, received, out):
    width = kept.shape[2]
    first = pl.multiple_of(where[0] * width, width)
    second = pl.multiple_of((1 - where[0]) * width, width)
    out[:, :, pl.ds(first, width)] = kept[...]
    out[:, :, pl.ds(second, width)] = received[...]


def join_columns(where, kept, received):
    count, lows, width = kept.shape
    vmem = pl.BlockSpec(memory_space=pltpu.VMEM)
    return pl.pallas_call(
        join_kernel,
        out_shape=jax.ShapeDtypeStruct((count, lows, 2 * width), F32),
        in_specs=[pl.BlockSpec(memory_space=pltpu.SMEM), vmem, vmem],
        out_specs=vmem,
        name="join",
    )(where, kept, received)


def stack_kernel(where, masks, rates, moved, table, sketch, keep, send, high, low):
    count, lows, rank = moved.shape
    jumps = masks.shape[0]
    total = rates[0]
    for k in range(1, jumps):
        total = total + rates[k]
    coefs = [jnp.full((2 * lows, rank), 1.0 - 0.5 * total, F32)]
    for k in range(jumps):
        coefs.append(jnp.sqrt(jnp.full((2 * lows, rank), rates[k], F32)))

    def pair(p, carry):
        rows = pl.ds(pl.multiple_of(p * 2 * lows, 2 * lows), 2 * lows)
        for k in range(jumps + 1):
            flip = 0 if k == 0 else masks[k - 1]
            first, second = (2 * p) ^ flip, (2 * p + 1) ^ flip
            value = coefs[k] * jnp.concatenate([moved[first], moved[second]], axis=0)
            cols = slice(k * rank, (k + 1) * rank)
            high[rows, cols], low[rows, cols] = split(value)
        return carry

    lax.fori_loop(0, count // 2, pair, 0, unroll=4)
    value = dot(high[...], table[...]) + dot(low[...], table[...])
    sketch[...] = value.reshape(sketch.shape)
    left = split(value.T)
    mine = where[0] == 0
    half = rank // 2
    for k in range(jumps + 1):
        cols = slice(k * rank, (k + 1) * rank)
        part = mul3(left, (high[:, cols], low[:, cols]))
        for j in range(rank // 128):
            tiles = part[:, j * 128 : (j + 1) * 128]
            top = tiles[:half].reshape(half // 8, 8, 128)
            bottom = tiles[half:].reshape(half // 8, 8, 128)
            keep[:, k * (rank // 128) + j] = jnp.where(mine, top, bottom)
            send[:, k * (rank // 128) + j] = jnp.where(mine, bottom, top)


def stack_products(where, masks, rates, moved, table):
    count, lows, rank = moved.shape
    columns = table.shape[0]
    vmem = pl.BlockSpec(memory_space=pltpu.VMEM)
    smem = pl.BlockSpec(memory_space=pltpu.SMEM)
    half = jax.ShapeDtypeStruct((rank // 16, columns // 128, 8, 128), F32)
    return pl.pallas_call(
        stack_kernel,
        out_shape=(jax.ShapeDtypeStruct(moved.shape, F32), half, half),
        in_specs=[smem, smem, smem, vmem, vmem],
        out_specs=(vmem, vmem, vmem),
        scratch_shapes=[pltpu.VMEM((count * lows, columns), BF16)] * 2,
        compiler_params=pltpu.CompilerParams(vmem_limit_bytes=40 << 20),
        name="stack",
    )(where, masks, rates, moved, table)


def spread_kernel(parts, out):
    out[...] = jnp.broadcast_to(jnp.sum(parts[...], axis=0, keepdims=True), out.shape)


def sum_wide(part, beside):
    vmem = pl.BlockSpec(memory_space=pltpu.VMEM)
    pieces = lax.all_to_all(part, "wide", split_axis=0, concat_axis=0, tiled=True)
    pieces, beside = lax.optimization_barrier((pieces, beside))
    copies = pl.pallas_call(
        spread_kernel,
        out_shape=jax.ShapeDtypeStruct(part.shape, F32),
        in_specs=[vmem],
        out_specs=vmem,
        name="spread",
    )(pieces)
    total = lax.all_to_all(copies, "wide", split_axis=0, concat_axis=0, tiled=True)
    return total, beside


def rotate_kernel(where, index, own, other, bases, sk_high, sk_low, rot_high, rot_low, rotated):
    count, lows, rank = own.shape
    order = bases.shape[1]
    group = order // (2 * lows)
    blocks = rotated.shape[0] // order
    core = where[0]
    mine = core == 0
    for b in range(blocks):
        parts = []
        for g in range(group):
            w = core * (count // 2) + b * group + g
            first, second = own[w], other[w]
            parts.append(jnp.where(mine, first, second))
            parts.append(jnp.where(mine, second, first))
        data = jnp.concatenate(parts, axis=0)
        value = mul3(split(bases[index[0, core * blocks + b]]), split(data))
        rotated[b * order : (b + 1) * order, :] = value
    rot_high[...], rot_low[...] = split(rotated[...].T)
    sk_high[core], sk_low[core] = split(own[...].reshape(count * lows, rank))
    sk_high[1 - core], sk_low[1 - core] = split(other[...].reshape(count * lows, rank))


def rotate_sketch(where, index, own, other, bases):
    count, lows, rank = own.shape
    rows = count * lows
    vmem = pl.BlockSpec(memory_space=pltpu.VMEM)
    smem = pl.BlockSpec(memory_space=pltpu.SMEM)
    return pl.pallas_call(
        rotate_kernel,
        out_shape=(
            jax.ShapeDtypeStruct((2, rows, rank), BF16),
            jax.ShapeDtypeStruct((2, rows, rank), BF16),
            jax.ShapeDtypeStruct((rank, rows), BF16),
            jax.ShapeDtypeStruct((rank, rows), BF16),
        ),
        in_specs=[smem, smem, vmem, vmem, vmem],
        out_specs=(vmem, vmem, vmem, vmem),
        scratch_shapes=[pltpu.VMEM((rows, rank), F32)],
        compiler_params=pltpu.CompilerParams(vmem_limit_bytes=40 << 20),
        name="rotate",
    )(where, index, own, other, bases)


def frobenius(mat):
    return jnp.sqrt(jnp.sum(jnp.sum(mat * mat, axis=0, keepdims=True), axis=1, keepdims=True))


def eye(n):
    return (
        lax.broadcasted_iota(jnp.int32, (n, n), 0) == lax.broadcasted_iota(jnp.int32, (n, n), 1)
    ).astype(F32)


def newton(mat, value):
    t = mat
    held = None
    for step in range(NS_ITERS):
        last = step == NS_ITERS - 1
        right = split(t)
        if step == 0:
            once = 1.5 * t - 0.5 * mul3(right, right)
            held = 1.5 * eye(t.shape[0]) - 0.5 * t if value is None else once
        else:
            if not last:
                once = 1.5 * t - 0.5 * mul3(right, right)
            held = 1.5 * held - 0.5 * mul3(split(held), right)
        if not last:
            t = 1.5 * once - 0.5 * mul3(split(once), right)
    return held


def output_kernel(
    where, mine, other, table, sk_high, sk_low, rot_high, rot_low, new, weights, proj
):
    rank = proj.shape[0]
    halves = sk_high.shape[0]
    width = rank // halves
    first = pl.ds(pl.multiple_of(where[0] * width, width), width)
    second = pl.ds(pl.multiple_of((1 - where[0]) * width, width), width)
    for j in range(mine.shape[1]):
        cols = slice(j * 128, (j + 1) * 128)
        proj[first, cols] = mine[:, j].reshape(width, 128)
        proj[second, cols] = other[:, j].reshape(width, 128)
    p = split(proj[...])
    gram = dot(p[0], table[...]) + dot(p[1], table[...])
    inverse = newton(gram / (frobenius(gram) + 1e-6), None)
    inv = split(inverse)
    coeff = split(mul3(inv, p))
    core = mul3(coeff, coeff, NT)
    shift = frobenius(core) + 1e-6
    root = split(newton(core / shift, "approx"))
    scale = jnp.sqrt(shift)
    mixing = scale * mul3(inv, root)
    turned = split(scale * mul3(root, inv))
    own = jnp.where(where[0] == 0, mixing[:, :width], mixing[:, width:])
    own = split(own)
    rot = mul3(turned, (rot_high[...], rot_low[...]))
    weights[...] = jnp.sum(rot * rot, axis=0, keepdims=True) / rank
    for c in range(halves):
        value = mul3((sk_high[c], sk_low[c]), own)
        new[:, c] = value.reshape(new.shape[0], new.shape[2], width)


def outputs(where, mine, other, table, sk_high, sk_low, rot_high, rot_low, lows):
    halves, rows, rank = sk_high.shape
    vmem = pl.BlockSpec(memory_space=pltpu.VMEM)
    smem = pl.BlockSpec(memory_space=pltpu.SMEM)
    return pl.pallas_call(
        output_kernel,
        out_shape=(
            jax.ShapeDtypeStruct((rows // lows, halves, lows, rank // halves), F32),
            jax.ShapeDtypeStruct((1, rows), F32),
        ),
        in_specs=[smem] + [vmem] * 7,
        out_specs=(vmem, vmem),
        scratch_shapes=[pltpu.VMEM((rank, table.shape[0]), F32)],
        compiler_params=pltpu.CompilerParams(vmem_limit_bytes=40 << 20),
        name="outputs",
    )(where, mine, other, table, sk_high, sk_low, rot_high, rot_low)


def sketch_table(sketch_perm, rank):
    target = sketch_perm % rank
    sign = 1.0 - 2.0 * (sketch_perm // rank % 2).astype(F32)
    hit = target[:, None] == jnp.arange(rank, dtype=jnp.int32)[None, :]
    return jnp.where(hit, sign[:, None], jnp.zeros((), F32)).astype(BF16)


def swap(value):
    return lax.ppermute(value, "cols", [(0, 1), (1, 0)])


def per_device(factor, gates, gate_layout, jump_masks, jump_rates, sketch_perm, bases, basis_index):
    rows, width = factor.shape
    count = lax.axis_size("wide")
    rank = width * lax.axis_size("cols")
    lows = rows // (2 * count)
    where = lax.axis_index("cols").astype(jnp.int32).reshape(1)
    kept, sent = apply_gates(where, gates, gate_layout, factor, count)
    pieces = join_columns(where, kept, swap(sent))
    moved = lax.all_to_all(pieces, "wide", split_axis=0, concat_axis=0, tiled=True)
    table = sketch_table(sketch_perm, rank)
    sketch, keep, send = stack_products(where, jump_masks, jump_rates, moved, table)
    part = keep + swap(send)
    total, other = sum_wide(part.reshape(-1, 8, 128), swap(sketch))
    turned = rotate_sketch(where, basis_index, sketch, other, bases)
    total, turned = lax.optimization_barrier((total.reshape(part.shape), turned))
    new, weights = outputs(where, total, swap(total), table, *turned, lows)
    return new.reshape(rows, width), weights


def solution(mesh):
    return jax.shard_map(
        per_device,
        mesh=mesh,
        in_specs=(P("wide", "cols"), P(), P("wide"), P(), P(), P(), P(), P("wide", None)),
        out_specs=(P("wide", "cols"), P("wide", "cols")),
        check_vma=False,
    )
```

time: 345 us -> 137 us (0.40)
  waiting for transfers between devices: 279 us -> 58.8 us
  starting transfers between devices: 15.9 us -> 40.6 us
  between operations: 15.6 us -> 0.78 us
    psum x1 -> x0, waiting for transfers between devices: 237 us -> none  [per_device(): proj = lax.psum(proj_own, ('wide', 'cols'))]
    all_to_all x1 -> x3, waiting for transfers between devices: 30.6 us -> 54 us  [the longest x1 27 us: per_device(): lax.all_to_all(pieces, 'wide', split_axis=0, concat_axis=0, tiled=True)]
    all_to_all x1 -> x3, starting transfers between devices: 15.7 us -> 29.4 us  [the longest x1 13.9 us: per_device(): lax.all_to_all(pieces, 'wide', split_axis=0, concat_axis=0, tiled=True)]
    ppermute x0 -> x4, starting transfers between devices: none -> 11.2 us  [swap(): return lax.ppermute(value, 'cols', [(0, 1), (1, 0)])]
    all_gather x1 -> x0, waiting for transfers between devices: 10.6 us -> none  [per_device(): sketch = lax.all_gather(sketch_own, 'cols', axis=0, tiled=False)]
    ppermute x0 -> x4, waiting for transfers between devices: none -> 4.72 us  [swap(): return lax.ppermute(value, 'cols', [(0, 1), (1, 0)])]
    unnamed x18 -> x30, local copies, waits for them, and re-layouts: 4.68 us -> 7.76 us
    pallas_call x3 -> x5, Pallas kernels: 16.1 us -> 14.6 us  [the longest x1 5.73 us: stack_products(): pl.pallas_call(stack_kernel, out_shape=(jax.ShapeDtypeStruct(moved.shape,...]
  transfers between devices with their start and end apart: 3 -> 7, of which waited for: 3 -> 6; matrix products, arithmetic and copies ran while one was open for 0% -> 1% of each run, Pallas kernels for 1% -> 1%
where the time goes in v2:
time: 137 us
  waiting for transfers between devices  58.8 us (43%)
  starting transfers between devices  40.6 us (30%)
  Pallas kernels  27.7 us (20%)
  local copies, waits for them, and re-layouts  7.76 us (6%)
    all_to_all x1, waiting for transfers between devices, per_device(): lax.all_to_all(pieces, 'wide', split_axis=0, concat_axis=0, tiled=True)  27 us
    all_to_all x1, waiting for transfers between devices, sum_wide(): lax.all_to_all(part, 'wide', split_axis=0, concat_axis=0, tiled=True)  17.1 us
    all_to_all x1, starting transfers between devices, per_device(): lax.all_to_all(pieces, 'wide', split_axis=0, concat_axis=0, tiled=True)  13.9 us
    pallas_call x1, Pallas kernels, outputs(): pl.pallas_call(output_kernel, out_shape=(jax.ShapeDtypeStruct((rows // lo...  13.1 us
    ppermute x4, starting transfers between devices, swap(): return lax.ppermute(value, 'cols', [(0, 1), (1, 0)])  11.2 us
    all_to_all x1, waiting for transfers between devices, sum_wide(): lax.all_to_all(copies, 'wide', split_axis=0, concat_axis=0, tiled=True)  9.9 us
    all_to_all x1, starting transfers between devices, sum_wide(): lax.all_to_all(copies, 'wide', split_axis=0, concat_axis=0, tiled=True)  8.51 us
    unnamed x30, local copies, waits for them, and re-layouts  7.76 us
  transfers between devices with their start and end apart: 7, of which 6 were waited for; matrix products, arithmetic and copies ran while one was open for 1% of the time, Pallas kernels for 1%

profile of v2, /device:TPU:1, one launch (start us, length us, event | category | flops | bytes accessed | tf_op | source)
XLA Modules:
  0.0 136.8 jit_solution(2748222950207901720)
XLA Ops:
  0.6 2.8 %gates.1 = (f32[128,8,128]{2,1,0:T(8,128)}, f32[128,8,128]{2,1,0:T(8,128)}) custom-call(s32[1]{0:T(128)} %bitcast.refs_0_.where, s32[16]{0:T(128)} %refs_1_.1, f32[8,128,128]{2,1,0:T(8,128)} %refs_2_.1, f32[2048,128]{1,0:T(8,128)} %refs_3_.1), custom_call_target="tpu_custom_call" | custom-call | tf_op jit(solution)/shard_map/gates/pallas_call | solution.py:56
  3.5 3.2 %collective-permute-start = (f32[128,8,128]{2,1,0:T(8,128)}, f32[128,8,128]{2,1,0:T(8,128)S(1)}, u32[]{:S(2)}, u32[]{:S(2)}) collective-permute-start(f32[128,8,128]{2,1,0:T(8,128)} %get-tuple-element.21), channel_id=1, source_target_pairs={{0,1},{1,0},{2,3},{3,2},{4,5},{5,4},{6,7},{7,6},{8,9},{9,8},{10,11... | collective-permute-start | bytes 1572872 | tf_op jit(solution)/shard_map/ppermute | solution.py:287
  6.7 1.7 %collective-permute-done.received = f32[128,8,128]{2,1,0:T(8,128)S(1)} collective-permute-done((f32[128,8,128]{2,1,0:T(8,128)}, f32[128,8,128]{2,1,0:T(8,128)S(1)}, u32[]{:S(2)}, u32[]{:S(2)}) %collective-permute-start) | collective-permute-done | bytes 524320 | tf_op jit(solution)/shard_map/ppermute | solution.py:287
  8.4 0.0 copy-start.13
  8.4 0.8 copy-done.13
  9.3 2.3 %join.1 = f32[128,8,256]{2,1,0:T(8,128)} custom-call(s32[1]{0:T(128)} %bitcast.refs_0_.where, f32[128,8,128]{2,1,0:T(8,128)} %get-tuple-element.20.kept, f32[128,8,128]{2,1,0:T(8,128)} %copy-done.13), custom_call_target="tpu_custom_call" | custom-call | tf_op jit(solution)/shard_map/join/pallas_call | solution.py:76
  11.5 0.0 copy-start.14
  11.5 13.9 %all-to-all-start = ((f32[128,8,256]{2,1,0:T(8,128)}), f32[128,8,256]{2,1,0:T(8,128)S(1)}, u32[]{:S(2)}, u32[]{:S(2)}) async-start(f32[128,8,256]{2,1,0:T(8,128)} %join.1), calls=%async_computation | async-start | bytes 2097152 | tf_op jit(solution)/shard_map/all_to_all | solution.py:298
  25.4 0.0 copy-done.14
  25.5 0.0 copy-start.9
  25.5 0.0 copy-start.10
  25.5 0.3 select_convert_fusion.table
  25.8 27.0 %all-to-all-done.moved = f32[128,8,256]{2,1,0:T(8,128)S(1)} async-done(((f32[128,8,256]{2,1,0:T(8,128)}), f32[128,8,256]{2,1,0:T(8,128)S(1)}, u32[]{:S(2)}, u32[]{:S(2)}) %all-to-all-start) | async-done | bytes 1048608 | tf_op jit(solution)/shard_map/all_to_all | solution.py:298
  52.8 0.0 copy-done.9
  52.8 0.0 copy-done.10
  52.8 5.7 %stack.1 = (f32[128,8,256]{2,1,0:T(8,128)S(1)}, f32[16,8,8,128]{3,2,1,0:T(8,128)S(1)}, f32[16,8,8,128]{3,2,1,0:T(8,128)S(1)}) custom-call(s32[1]{0:T(128)} %bitcast.refs_0_.where, s32[3]{0:T(128)S(1)} %copy-done.9, f32[3]{0:T(128)S(1)} %copy-done.10, f32[128,8,256]{2,1,0:T(8,128)S(1)} %all-to-all-done.moved, bf16[1024,256]{1,0:T(8,128)(2,1)S(1)} %select_convert_fusion.table), custom_call_target="tpu_custom_call" | custom-call | tf_op jit(solution)/shard_map/stack/pallas_call | solution.py:128
  58.6 0.0 copy-start
  58.6 3.5 %collective-permute-start.1 = (f32[16,8,8,128]{3,2,1,0:T(8,128)S(1)}, f32[16,8,8,128]{3,2,1,0:T(8,128)S(1)}, u32[]{:S(2)}, u32[]{:S(2)}) collective-permute-start(f32[16,8,8,128]{3,2,1,0:T(8,128)S(1)} %get-tuple-element.23), channel_id=1, source_target_pairs={{0,1},{1,0},{2,3},{3,2},{4,5},{5,4},{6,7},{7,6},{8,9},{9,8},{10,11... | collective-permute-start | bytes 1572872 | tf_op jit(solution)/shard_map/ppermute | solution.py:287
  62.2 0.1 collective-permute-start.2
  62.3 1.4 %collective-permute-done.1 = f32[16,8,8,128]{3,2,1,0:T(8,128)S(1)} collective-permute-done((f32[16,8,8,128]{3,2,1,0:T(8,128)S(1)}, f32[16,8,8,128]{3,2,1,0:T(8,128)S(1)}, u32[]{:S(2)}, u32[]{:S(2)}) %collective-permute-start.1) | collective-permute-done | bytes 524320 | tf_op jit(solution)/shard_map/ppermute | solution.py:287
  63.7 0.8 add.16
  64.5 0.0 copy-done
  64.5 7.0 %all-to-all-start.1 = ((f32[128,8,128]{2,1,0:T(8,128)}), f32[128,8,128]{2,1,0:T(8,128)S(1)}, u32[]{:S(2)}, u32[]{:S(2)}) async-start(f32[128,8,128]{2,1,0:T(8,128)} %bitcast.1), calls=%async_computation.1 | async-start | bytes 1048576 | tf_op jit(solution)/shard_map/all_to_all | solution.py:145
  71.5 0.0 collective-permute-done.2.other
  71.5 0.0 copy-start.2
  71.6 17.1 %all-to-all-done.1.parts = f32[128,8,128]{2,1,0:T(8,128)S(1)} async-done(((f32[128,8,128]{2,1,0:T(8,128)}), f32[128,8,128]{2,1,0:T(8,128)S(1)}, u32[]{:S(2)}, u32[]{:S(2)}) %all-to-all-start.1) | async-done | bytes 524320 | tf_op jit(solution)/shard_map/all_to_all | solution.py:145
  88.7 0.0 copy-start.12
  88.7 0.8 copy-done.12
  89.5 2.0 %spread.1 = f32[128,8,128]{2,1,0:T(8,128)} custom-call(f32[128,8,128]{2,1,0:T(8,128)} %copy-done.12), custom_call_target="tpu_custom_call" | custom-call | tf_op jit(solution)/shard_map/spread/pallas_call | solution.py:147
  91.5 0.0 copy-start.8
  91.5 0.0 copy-start.11
  91.5 0.0 copy-done.2
  91.5 8.5 %all-to-all-start.2 = ((f32[128,8,128]{2,1,0:T(8,128)}), f32[128,8,128]{2,1,0:T(8,128)S(1)}, u32[]{:S(2)}, u32[]{:S(2)}) async-start(f32[128,8,128]{2,1,0:T(8,128)} %spread.1), calls=%async_computation.2 | async-start | bytes 1048576 | tf_op jit(solution)/shard_map/all_to_all | solution.py:154
  100.0 0.0 copy-done.8
  100.0 0.0 copy-done.11
  100.0 0.0 copy-start.1
  100.0 1.2 copy-done.1
  101.2 0.0 copy-start.3
  101.2 1.2 copy-done.3
  102.5 1.8 %rotate.1 = (bf16[2,1024,256]{2,1,0:T(8,128)(2,1)S(1)}, bf16[2,1024,256]{2,1,0:T(8,128)(2,1)S(1)}, bf16[256,1024]{1,0:T(8,128)(2,1)S(1)}, bf16[256,1024]{1,0:T(8,128)(2,1)S(1)}) custom-call(s32[1]{0:T(128)} %bitcast.refs_0_.where, s32[1,32]{1,0:T(1,128)S(1)} %copy-done.11, f32[128,8,256]{2,1,0:T(8,128)S(1)} %copy-done.1, f32[128,8,256]{2,1,0:T(8,128)S(1)} %copy-done.3, ...), custom_call_target="tpu_custom_call" | custom-call | tf_op jit(solution)/shard_map/rotate/pallas_call | solution.py:185
  104.3 0.0 copy-start.4
  104.3 0.8 copy-done.4
  105.1 0.0 copy-start.6
  105.1 0.8 copy-done.6
  105.9 9.9 %all-to-all-done.2 = f32[128,8,128]{2,1,0:T(8,128)S(1)} async-done(((f32[128,8,128]{2,1,0:T(8,128)}), f32[128,8,128]{2,1,0:T(8,128)S(1)}, u32[]{:S(2)}, u32[]{:S(2)}) %all-to-all-start.2) | async-done | bytes 524320 | tf_op jit(solution)/shard_map/all_to_all | solution.py:154
  115.8 4.3 %collective-permute-start.3 = (f32[16,8,8,128]{3,2,1,0:T(8,128)S(1)}, f32[16,8,8,128]{3,2,1,0:T(8,128)S(1)}, u32[]{:S(2)}, u32[]{:S(2)}) collective-permute-start(f32[16,8,8,128]{3,2,1,0:T(8,128)S(1)} %bitcast.4), channel_id=1, source_target_pairs={{0,1},{1,0},{2,3},{3,2},{4,5},{5,4},{6,7},{7,6},{8,9},{9,8},{10,11... | collective-permute-start | bytes 1572872 | tf_op jit(solution)/shard_map/ppermute | solution.py:287
  120.1 1.5 %collective-permute-done.3.other = f32[16,8,8,128]{3,2,1,0:T(8,128)S(1)} collective-permute-done((f32[16,8,8,128]{3,2,1,0:T(8,128)S(1)}, f32[16,8,8,128]{3,2,1,0:T(8,128)S(1)}, u32[]{:S(2)}, u32[]{:S(2)}) %collective-permute-start.3) | collective-permute-done | bytes 524320 | tf_op jit(solution)/shard_map/ppermute | solution.py:287
  121.6 0.0 copy-start.5
  121.6 1.0 copy-done.5
  122.7 0.0 copy-start.7
  122.7 1.0 copy-done.7
  123.7 13.1 %outputs.1 = (f32[128,2,8,128]{3,2,1,0:T(8,128)}, f32[1,1024]{1,0:T(1,128)}) custom-call(s32[1]{0:T(128)} %bitcast.refs_0_.where, f32[16,8,8,128]{3,2,1,0:T(8,128)S(1)} %bitcast.5, f32[16,8,8,128]{3,2,1,0:T(8,128)S(1)} %collective-permute-done.3.other, bf16[1024,256]{1,0:T(8,128)(2,1)S(1)} %select_convert_fusion.table, ...), custom_call_target="tpu_custom_call" | custom-call | tf_op jit(solution)/shard_map/outputs/pallas_call | solution.py:265
  (2 shorter events, 0.0 us)
Async XLA Ops:
  3.5 5.0 %collective-permute-start = (f32[128,8,128]{2,1,0:T(8,128)}, f32[128,8,128]{2,1,0:T(8,128)S(1)}, u32[]{:S(2)}, u32[]{:S(2)}) collective-permute-start(f32[128,8,128]{2,1,0:T(8,128)} %get-tuple-element.21), channel_id=1, source_target_pairs={{0,1},{1,0},{2,3},{3,2},{4,5},{5,4},{6,7},{7,6},{8,9},{9,8},{10,11... | collective-permute-start | bytes 1572872 | tf_op jit(solution)/shard_map/ppermute | solution.py:287
  8.4 0.8 copy-start.13
  11.5 13.9 %copy-start.14 = (s32[1024]{0:T(1024)S(1)}, s32[1024]{0:T(1024)}, u32[]{:S(2)}) copy-start(s32[1024]{0:T(1024)} %param.13) | copy-start | bytes 12292
  11.5 41.3 %all-to-all-start = ((f32[128,8,256]{2,1,0:T(8,128)}), f32[128,8,256]{2,1,0:T(8,128)S(1)}, u32[]{:S(2)}, u32[]{:S(2)}) async-start(f32[128,8,256]{2,1,0:T(8,128)} %join.1), calls=%async_computation | async-start | bytes 2097152 | tf_op jit(solution)/shard_map/all_to_all | solution.py:298
  25.5 27.4 %copy-start.9 = (s32[3]{0:T(128)S(1)}, s32[3]{0:T(128)}, u32[]{:S(2)}) copy-start(s32[3]{0:T(128)} %masks.1) | copy-start | bytes 40
  25.5 27.4 %copy-start.10 = (f32[3]{0:T(128)S(1)}, f32[3]{0:T(128)}, u32[]{:S(2)}) copy-start(f32[3]{0:T(128)} %rates.1) | copy-start | bytes 40
  58.6 6.0 %copy-start = (f32[128,8,256]{2,1,0:T(8,128)}, f32[128,8,256]{2,1,0:T(8,128)S(1)}, u32[]{:S(2)}) copy-start(f32[128,8,256]{2,1,0:T(8,128)S(1)} %get-tuple-element.24.own) | copy-start | bytes 3145732
  58.6 5.1 %collective-permute-start.1 = (f32[16,8,8,128]{3,2,1,0:T(8,128)S(1)}, f32[16,8,8,128]{3,2,1,0:T(8,128)S(1)}, u32[]{:S(2)}, u32[]{:S(2)}) collective-permute-start(f32[16,8,8,128]{3,2,1,0:T(8,128)S(1)} %get-tuple-element.23), channel_id=1, source_target_pairs={{0,1},{1,0},{2,3},{3,2},{4,5},{5,4},{6,7},{7,6},{8,9},{9,8},{10,11... | collective-permute-start | bytes 1572872 | tf_op jit(solution)/shard_map/ppermute | solution.py:287
  62.2 9.4 %collective-permute-start.2 = (f32[128,8,256]{2,1,0:T(8,128)S(1)}, f32[128,8,256]{2,1,0:T(8,128)S(1)}, u32[]{:S(2)}, u32[]{:S(2)}) collective-permute-start(f32[128,8,256]{2,1,0:T(8,128)S(1)} %get-tuple-element.24.own), channel_id=1, source_target_pairs={{0,1},{1,0},{2,3},{3,2},{4,5},{5,4},{6,7},{7,6},{8,9},{9,8},{10,11... | collective-permute-start | bytes 3145736 | tf_op jit(solution)/shard_map/ppermute | solution.py:287
  64.5 24.1 %all-to-all-start.1 = ((f32[128,8,128]{2,1,0:T(8,128)}), f32[128,8,128]{2,1,0:T(8,128)S(1)}, u32[]{:S(2)}, u32[]{:S(2)}) async-start(f32[128,8,128]{2,1,0:T(8,128)} %bitcast.1), calls=%async_computation.1 | async-start | bytes 1048576 | tf_op jit(solution)/shard_map/all_to_all | solution.py:145
  71.5 19.9 %copy-start.2 = (f32[128,8,256]{2,1,0:T(8,128)}, f32[128,8,256]{2,1,0:T(8,128)S(1)}, u32[]{:S(2)}) copy-start(f32[128,8,256]{2,1,0:T(8,128)S(1)} %collective-permute-done.2.other) | copy-start | bytes 3145732
  88.7 0.8 copy-start.12
  91.5 8.5 %copy-start.8 = (f32[8,64,64]{2,1,0:T(8,128)S(1)}, f32[8,64,64]{2,1,0:T(8,128)}, u32[]{:S(2)}) copy-start(f32[8,64,64]{2,1,0:T(8,128)} %bases.1) | copy-start | bytes 393220
  91.5 8.5 %copy-start.11 = (s32[1,32]{1,0:T(1,128)S(1)}, s32[1,32]{1,0:T(1,128)}, u32[]{:S(2)}) copy-start(s32[1,32]{1,0:T(1,128)} %index.1) | copy-start | bytes 388
  91.5 24.3 %all-to-all-start.2 = ((f32[128,8,128]{2,1,0:T(8,128)}), f32[128,8,128]{2,1,0:T(8,128)S(1)}, u32[]{:S(2)}, u32[]{:S(2)}) async-start(f32[128,8,128]{2,1,0:T(8,128)} %spread.1), calls=%async_computation.2 | async-start | bytes 1048576 | tf_op jit(solution)/shard_map/all_to_all | solution.py:154
  100.0 1.2 copy-start.1
  101.2 1.2 copy-start.3
  104.3 0.8 copy-start.4
  105.1 0.8 copy-start.6
  115.8 5.9 %collective-permute-start.3 = (f32[16,8,8,128]{3,2,1,0:T(8,128)S(1)}, f32[16,8,8,128]{3,2,1,0:T(8,128)S(1)}, u32[]{:S(2)}, u32[]{:S(2)}) collective-permute-start(f32[16,8,8,128]{3,2,1,0:T(8,128)S(1)} %bitcast.4), channel_id=1, source_target_pairs={{0,1},{1,0},{2,3},{3,2},{4,5},{5,4},{6,7},{7,6},{8,9},{9,8},{10,11... | collective-permute-start | bytes 1572872 | tf_op jit(solution)/shard_map/ppermute | solution.py:287
  121.6 1.0 copy-start.5
  122.7 1.0 copy-start.7

commit v3 on v2

--- a/solution.py
+++ b/solution.py
@@ -22,16 +22,23 @@
 
 
 def mul3(a, b, dims=NN):
-    return dot(a[0], b[0], dims) + (dot(a[1], b[0], dims) + dot(a[0], b[1], dims))
+    left = jnp.concatenate([a[0], a[1], a[0]], axis=dims[0][0][0])
+    right = jnp.concatenate([b[0], b[0], b[1]], axis=dims[0][1][0])
+    return dot(left, right, dims)
+
+
+def params(mib):
+    return pltpu.CompilerParams(vmem_limit_bytes=mib << 20)
 
 
 def gate_kernel(order, where, layout, gates, factor, keep, send):
-    lows = keep.shape[1]
+    lows, width = send.shape[1:]
     group = order // (2 * lows)
+    blocks = factor.shape[0] // order
     mine = where[0] == 0
-    for b in range(factor.shape[0] // order):
+    for b in range(blocks):
         high, low = split(factor[b * order : (b + 1) * order, :])
-        left = jnp.concatenate(split(gates[layout[b]]), axis=1)
+        left = jnp.concatenate(split(gates[layout[pl.program_id(0) * blocks + b]]), axis=1)
         right = jnp.concatenate(
             [
                 jnp.concatenate([high, low], axis=1),
@@ -40,66 +47,83 @@
             axis=0,
         )
         both = dot(left, right)
-        value = both[:, : high.shape[1]] + both[:, high.shape[1] :]
-        value = value.reshape(group, 2, lows, high.shape[1])
+        value = both[:, :width] + both[:, width:]
+        value = value.reshape(group, 2, lows, width)
         hs = slice(b * group, (b + 1) * group)
-        keep[hs] = jnp.where(mine, value[:, 0], value[:, 1])
+        keep[hs, 0] = jnp.where(mine, value[:, 0], value[:, 1])
         send[hs] = jnp.where(mine, value[:, 1], value[:, 0])
 
 
 def apply_gates(where, gates, layout, factor, count):
     order = gates.shape[1]
     rows, width = factor.shape
-    vmem = pl.BlockSpec(memory_space=pltpu.VMEM)
-    smem = pl.BlockSpec(memory_space=pltpu.SMEM)
-    half = jax.ShapeDtypeStruct((count, rows // (2 * count), width), F32)
+    lows = rows // (2 * count)
+    steps = 2
     return pl.pallas_call(
         lambda *refs: gate_kernel(order, *refs),
-        out_shape=(half, half),
-        in_specs=[smem, smem, vmem, vmem],
-        out_specs=(vmem, vmem),
+        out_shape=(
+            jax.ShapeDtypeStruct((count, 2, lows, width), F32),
+            jax.ShapeDtypeStruct((count, lows, width), F32),
+        ),
+        grid_spec=pltpu.PrefetchScalarGridSpec(
+            num_scalar_prefetch=2,
+            grid=(steps,),
+            in_specs=[
+                pl.BlockSpec(gates.shape, lambda i, where, layout: (0, 0, 0)),
+                pl.BlockSpec((rows // steps, width), lambda i, where, layout: (i, 0)),
+            ],
+            out_specs=(
+                pl.BlockSpec(
+                    (count // steps, 1, lows, width), lambda i, where, layout: (i, where[0], 0, 0)
+                ),
+                pl.BlockSpec((count // steps, lows, width), lambda i, where, layout: (i, 0, 0)),
+            ),
+        ),
+        compiler_params=params(8),
         name="gates",
     )(where, layout, gates, factor)
 
 
-def join_kernel(where, kept, received, out):
-    width = kept.shape[2]
-    first = pl.multiple_of(where[0] * width, width)
-    second = pl.multiple_of((1 - where[0]) * width, width)
-    out[:, :, pl.ds(first, width)] = kept[...]
-    out[:, :, pl.ds(second, width)] = received[...]
-
-
-def join_columns(where, kept, received):
-    count, lows, width = kept.shape
-    vmem = pl.BlockSpec(memory_space=pltpu.VMEM)
+def join_kernel(where, received, kept, joined, sem):
+    copy = pltpu.make_async_copy(received, joined.at[:, 1 - where[0]], sem)
+    copy.start()
+    copy.wait()
+
+
+def join_columns(where, received, kept):
+    away = pl.BlockSpec(memory_space=pl.ANY)
     return pl.pallas_call(
         join_kernel,
-        out_shape=jax.ShapeDtypeStruct((count, lows, 2 * width), F32),
-        in_specs=[pl.BlockSpec(memory_space=pltpu.SMEM), vmem, vmem],
-        out_specs=vmem,
+        out_shape=jax.ShapeDtypeStruct(kept.shape, F32),
+        in_specs=[pl.BlockSpec(memory_space=pltpu.SMEM), away, away],
+        out_specs=away,
+        scratch_shapes=[pltpu.SemaphoreType.DMA(())],
+        input_output_aliases={2: 0},
+        compiler_params=params(1),
         name="join",
-    )(where, kept, received)
+    )(where, received, kept)
 
 
 def stack_kernel(where, masks, rates, moved, table, sketch, keep, send, high, low):
-    count, lows, rank = moved.shape
+    count, halves, lows, width = moved.shape
+    rank = halves * width
     jumps = masks.shape[0]
     total = rates[0]
     for k in range(1, jumps):
         total = total + rates[k]
-    coefs = [jnp.full((2 * lows, rank), 1.0 - 0.5 * total, F32)]
+    coefs = [jnp.full((2 * lows, width), 1.0 - 0.5 * total, F32)]
     for k in range(jumps):
-        coefs.append(jnp.sqrt(jnp.full((2 * lows, rank), rates[k], F32)))
+        coefs.append(jnp.sqrt(jnp.full((2 * lows, width), rates[k], F32)))
 
     def pair(p, carry):
         rows = pl.ds(pl.multiple_of(p * 2 * lows, 2 * lows), 2 * lows)
         for k in range(jumps + 1):
             flip = 0 if k == 0 else masks[k - 1]
             first, second = (2 * p) ^ flip, (2 * p + 1) ^ flip
-            value = coefs[k] * jnp.concatenate([moved[first], moved[second]], axis=0)
-            cols = slice(k * rank, (k + 1) * rank)
-            high[rows, cols], low[rows, cols] = split(value)
+            for c in range(halves):
+                value = coefs[k] * jnp.concatenate([moved[first, c], moved[second, c]], axis=0)
+                cols = slice(k * rank + c * width, k * rank + (c + 1) * width)
+                high[rows, cols], low[rows, cols] = split(value)
         return carry
 
     lax.fori_loop(0, count // 2, pair, 0, unroll=4)
@@ -120,39 +144,64 @@
 
 
 def stack_products(where, masks, rates, moved, table):
-    count, lows, rank = moved.shape
+    count, halves, lows, width = moved.shape
+    rank = halves * width
     columns = table.shape[0]
     vmem = pl.BlockSpec(memory_space=pltpu.VMEM)
     smem = pl.BlockSpec(memory_space=pltpu.SMEM)
     half = jax.ShapeDtypeStruct((rank // 16, columns // 128, 8, 128), F32)
     return pl.pallas_call(
         stack_kernel,
-        out_shape=(jax.ShapeDtypeStruct(moved.shape, F32), half, half),
+        out_shape=(jax.ShapeDtypeStruct((count, lows, rank), F32), half, half),
         in_specs=[smem, smem, smem, vmem, vmem],
         out_specs=(vmem, vmem, vmem),
         scratch_shapes=[pltpu.VMEM((count * lows, columns), BF16)] * 2,
-        compiler_params=pltpu.CompilerParams(vmem_limit_bytes=40 << 20),
+        compiler_params=params(20),
         name="stack",
     )(where, masks, rates, moved, table)
 
 
+SIDES = (4, 8, 4)
+
+
+def groups(count):
+    ny, nz, nx = SIDES
+    assert ny * nz * nx == count
+    at = lambda y, z, x: (y * nz + z) * nx + x
+    planes = [[at(y, z, x) for y in range(ny) for x in range(nx)] for z in range(nz)]
+    lines = [[at(y, z, x) for z in range(nz)] for y in range(ny) for x in range(nx)]
+    return planes, lines
+
+
 def spread_kernel(parts, out):
     out[...] = jnp.broadcast_to(jnp.sum(parts[...], axis=0, keepdims=True), out.shape)
 
 
-def sum_wide(part, beside):
+def sum_and_spread(parts, copies):
     vmem = pl.BlockSpec(memory_space=pltpu.VMEM)
-    pieces = lax.all_to_all(part, "wide", split_axis=0, concat_axis=0, tiled=True)
-    pieces, beside = lax.optimization_barrier((pieces, beside))
-    copies = pl.pallas_call(
+    return pl.pallas_call(
         spread_kernel,
-        out_shape=jax.ShapeDtypeStruct(part.shape, F32),
+        out_shape=jax.ShapeDtypeStruct((copies,) + parts.shape[1:], F32),
         in_specs=[vmem],
         out_specs=vmem,
+        compiler_params=params(4),
         name="spread",
-    )(pieces)
-    total = lax.all_to_all(copies, "wide", split_axis=0, concat_axis=0, tiled=True)
-    return total, beside
+    )(parts)
+
+
+def exchange(pieces, members):
+    return lax.all_to_all(
+        pieces, "wide", split_axis=0, concat_axis=0, axis_index_groups=members, tiled=True
+    )
+
+
+def sum_wide(part, beside):
+    planes, lines = groups(lax.axis_size("wide"))
+    assert len(planes[0]) == part.shape[0]
+    pieces = exchange(part, planes)
+    pieces, beside = lax.optimization_barrier((pieces, beside))
+    pieces = exchange(sum_and_spread(pieces, len(lines[0])), lines)
+    return exchange(sum_and_spread(pieces, len(planes[0])), planes), beside
 
 
 def rotate_kernel(where, index, own, other, bases, sk_high, sk_low, rot_high, rot_low, rotated):
@@ -193,7 +242,7 @@
         in_specs=[smem, smem, vmem, vmem, vmem],
         out_specs=(vmem, vmem, vmem, vmem),
         scratch_shapes=[pltpu.VMEM((rows, rank), F32)],
-        compiler_params=pltpu.CompilerParams(vmem_limit_bytes=40 << 20),
+        compiler_params=params(12),
         name="rotate",
     )(where, index, own, other, bases)
 
@@ -271,7 +320,7 @@
         in_specs=[smem] + [vmem] * 7,
         out_specs=(vmem, vmem),
         scratch_shapes=[pltpu.VMEM((rank, table.shape[0]), F32)],
-        compiler_params=pltpu.CompilerParams(vmem_limit_bytes=40 << 20),
+        compiler_params=params(20),
         name="outputs",
     )(where, mine, other, table, sk_high, sk_low, rot_high, rot_low)
 
@@ -291,18 +340,17 @@
     rows, width = factor.shape
     count = lax.axis_size("wide")
     rank = width * lax.axis_size("cols")
-    lows = rows // (2 * count)
     where = lax.axis_index("cols").astype(jnp.int32).reshape(1)
     kept, sent = apply_gates(where, gates, gate_layout, factor, count)
-    pieces = join_columns(where, kept, swap(sent))
+    pieces = join_columns(where, swap(sent), kept)
     moved = lax.all_to_all(pieces, "wide", split_axis=0, concat_axis=0, tiled=True)
     table = sketch_table(sketch_perm, rank)
     sketch, keep, send = stack_products(where, jump_masks, jump_rates, moved, table)
     part = keep + swap(send)
-    total, other = sum_wide(part.reshape(-1, 8, 128), swap(sketch))
+    total, other = sum_wide(part, swap(sketch))
     turned = rotate_sketch(where, basis_index, sketch, other, bases)
-    total, turned = lax.optimization_barrier((total.reshape(part.shape), turned))
-    new, weights = outputs(where, total, swap(total), table, *turned, lows)
+    total, turned = lax.optimization_barrier((total, turned))
+    new, weights = outputs(where, total, swap(total), table, *turned, moved.shape[2])
     return new.reshape(rows, width), weights
 
 

time: 137 us -> 127 us (0.927)
  blocking collectives: 0 us -> 26.9 us
  waiting for transfers between devices: 58.8 us -> 36.2 us
  starting transfers between devices: 40.6 us -> 29 us
  Pallas kernels: 27.7 us -> 23.9 us
    all_to_all x0 -> x2, blocking collectives: none -> 26.9 us  [exchange(): lax.all_to_all(pieces, 'wide', split_axis=0, concat_axis=0, axis_index_gr...]
    all_to_all x2 -> x1, waiting for transfers between devices: 27 us -> 3.21 us  [exchange(): lax.all_to_all(pieces, 'wide', split_axis=0, concat_axis=0, axis_index_gr...]
    all_to_all x2 -> x1, starting transfers between devices: 15.5 us -> 4.21 us  [exchange(): lax.all_to_all(pieces, 'wide', split_axis=0, concat_axis=0, axis_index_gr...]
    pallas_call x4 -> x5, Pallas kernels: 12.8 us -> 9.61 us  [the longest x1 6 us: stack_products(): pl.pallas_call(stack_kernel, out_shape=(jax.ShapeDtypeStruct((count, lows...]
    unnamed x30 -> x32, local copies, waits for them, and re-layouts: 7.76 us -> 9.08 us
  transfers between devices with their start and end apart: 7 -> 6, of which waited for: 6 -> 5; matrix products, arithmetic and copies ran while one was open for 1% -> 0% of each run, Pallas kernels for 1% -> 1%
where the time goes in v3:
time: 127 us; the launch traced here: 126 us
  waiting for transfers between devices  36.2 us (29%)
  starting transfers between devices  29 us (23%)
  blocking collectives  26.9 us (21%)
  Pallas kernels  23.9 us (19%)
  local copies, waits for them, and re-layouts  9.08 us (7%)
    all_to_all x1, waiting for transfers between devices, per_device(): lax.all_to_all(pieces, 'wide', split_axis=0, concat_axis=0, tiled=True)  27 us
    all_to_all x2, blocking collectives, exchange(): lax.all_to_all(pieces, 'wide', split_axis=0, concat_axis=0, axis_index_gr...  26.9 us
    all_to_all x1, starting transfers between devices, per_device(): lax.all_to_all(pieces, 'wide', split_axis=0, concat_axis=0, tiled=True)  13.8 us
    pallas_call x1, Pallas kernels, outputs(): pl.pallas_call(output_kernel, out_shape=(jax.ShapeDtypeStruct((rows // lo...  12.6 us
    ppermute x4, starting transfers between devices, swap(): return lax.ppermute(value, 'cols', [(0, 1), (1, 0)])  11 us
    unnamed x32, local copies, waits for them, and re-layouts  9.08 us
    ppermute x4, waiting for transfers between devices, swap(): return lax.ppermute(value, 'cols', [(0, 1), (1, 0)])  6.01 us
    pallas_call x1, Pallas kernels, stack_products(): pl.pallas_call(stack_kernel, out_shape=(jax.ShapeDtypeStruct((count, lows...  6 us
  transfers between devices with their start and end apart: 6, of which 5 were waited for; matrix products, arithmetic and copies ran while one was open for 0% of the time, Pallas kernels for 1%

profile of v3, /device:TPU:1, one launch (start us, length us, event | category | flops | bytes accessed | tf_op | source)
XLA Modules:
  0.0 126.4 jit_solution(14957366026410319589)
XLA Ops:
  0.6 0.0 copy-start.13
  0.6 0.6 copy-done.13
  1.3 0.0 copy-start
  1.3 1.2 copy-done
  2.5 0.0 copy-start.9
  2.5 1.0 copy-done.9
  3.6 1.9 %gates.1 = (f32[128,2,8,128]{3,2,1,0:T(8,128)}, f32[128,8,128]{2,1,0:T(8,128)S(1)}) custom-call(s32[1]{0:T(128)} %bitcast.refs_0_.where, s32[16]{0:T(128)S(1)} %copy-done.13, f32[8,128,128]{2,1,0:T(8,128)S(1)} %copy-done.9, f32[2048,128]{1,0:T(8,128)S(1)} %copy-done), custom_call_target="tpu_custom_call" | custom-call | tf_op jit(solution)/shard_map/gates/pallas_call | solution.py:62
  5.5 3.2 %collective-permute-start = (f32[128,8,128]{2,1,0:T(8,128)S(1)}, f32[128,8,128]{2,1,0:T(8,128)S(1)}, u32[]{:S(2)}, u32[]{:S(2)}) collective-permute-start(f32[128,8,128]{2,1,0:T(8,128)S(1)} %get-tuple-element.20), channel_id=1, source_target_pairs={{0,1},{1,0},{2,3},{3,2},{4,5},{5,4},{6,7},{7,6},{8,9},{9,8},{10,11... | collective-permute-start | bytes 1572872 | tf_op jit(solution)/shard_map/ppermute | solution.py:336
  8.7 1.5 %collective-permute-done.received = f32[128,8,128]{2,1,0:T(8,128)S(1)} collective-permute-done((f32[128,8,128]{2,1,0:T(8,128)S(1)}, f32[128,8,128]{2,1,0:T(8,128)S(1)}, u32[]{:S(2)}, u32[]{:S(2)}) %collective-permute-start) | collective-permute-done | bytes 524320 | tf_op jit(solution)/shard_map/ppermute | solution.py:336
  10.2 0.8 join.1
  11.1 0.0 copy-start.15
  11.1 13.8 %all-to-all-start = ((f32[128,2,8,128]{3,2,1,0:T(8,128)}), f32[128,2,8,128]{3,2,1,0:T(8,128)S(1)}, u32[]{:S(2)}, u32[]{:S(2)}) async-start(f32[128,2,8,128]{3,2,1,0:T(8,128)} %join.1), calls=%async_computation | async-start | bytes 2097152 | tf_op jit(solution)/shard_map/all_to_all | solution.py:346
  24.9 0.0 copy-done.15
  24.9 0.0 copy-start.11
  24.9 0.0 copy-start.12
  24.9 0.3 select_convert_fusion.table
  25.3 27.0 %all-to-all-done.moved = f32[128,2,8,128]{3,2,1,0:T(8,128)S(1)} async-done(((f32[128,2,8,128]{3,2,1,0:T(8,128)}), f32[128,2,8,128]{3,2,1,0:T(8,128)S(1)}, u32[]{:S(2)}, u32[]{:S(2)}) %all-to-all-start) | async-done | bytes 1048608 | tf_op jit(solution)/shard_map/all_to_all | solution.py:346
  52.3 0.0 copy-done.11
  52.3 0.0 copy-done.12
  52.3 6.0 %stack.1 = (f32[128,8,256]{2,1,0:T(8,128)S(1)}, f32[16,8,8,128]{3,2,1,0:T(8,128)S(1)}, f32[16,8,8,128]{3,2,1,0:T(8,128)S(1)}) custom-call(s32[1]{0:T(128)} %bitcast.refs_0_.where, s32[3]{0:T(128)S(1)} %copy-done.11, f32[3]{0:T(128)S(1)} %copy-done.12, f32[128,2,8,128]{3,2,1,0:T(8,128)S(1)} %all-to-all-done.moved, bf16[1024,256]{1,0:T(8,128)(2,1)S(1)} %select_convert_fusion.table), custom_call_target="tpu_custom_call" | custom-call | tf_op jit(solution)/shard_map/stack/pallas_call | solution.py:153
  58.3 0.0 copy-start.1
  58.3 3.5 %collective-permute-start.2 = (f32[128,8,256]{2,1,0:T(8,128)S(1)}, f32[128,8,256]{2,1,0:T(8,128)S(1)}, u32[]{:S(2)}, u32[]{:S(2)}) collective-permute-start(f32[128,8,256]{2,1,0:T(8,128)S(1)} %get-tuple-element.24.own), channel_id=1, source_target_pairs={{0,1},{1,0},{2,3},{3,2},{4,5},{5,4},{6,7},{7,6},{8,9},{9,8},{10,11... | collective-permute-start | bytes 3145736 | tf_op jit(solution)/shard_map/ppermute | solution.py:336
  61.8 0.1 collective-permute-start.1
  61.9 2.9 %collective-permute-done.1 = f32[16,8,8,128]{3,2,1,0:T(8,128)S(1)} collective-permute-done((f32[16,8,8,128]{3,2,1,0:T(8,128)S(1)}, f32[16,8,8,128]{3,2,1,0:T(8,128)S(1)}, u32[]{:S(2)}, u32[]{:S(2)}) %collective-permute-start.1) | collective-permute-done | bytes 524320 | tf_op jit(solution)/shard_map/ppermute | solution.py:336
  64.9 0.1 add.16
  65.0 15.0 %all_to_all.20.parts = f32[16,8,8,128]{3,2,1,0:T(8,128)S(1)} all-to-all(f32[16,8,8,128]{3,2,1,0:T(8,128)S(1)} %add.16), channel_id=1, replica_groups={{0,2,4,6,64,66,68,70,128,130,132,134,192,194,196,198},{8,10,12,14,72,74..., dimensions={0} | all-to-all | bytes 1048576 | tf_op jit(solution)/shard_map/all_to_all | solution.py:193
  79.9 0.0 copy-done.1
  79.9 0.0 collective-permute-done.2.other
  79.9 0.0 copy-start.3
  80.0 11.9 %all_to_all.21.parts = f32[8,8,8,128]{3,2,1,0:T(8,128)S(1)} all-to-all(f32[8,8,8,128]{3,2,1,0:T(8,128)S(1)} %spread.2), channel_id=1, replica_groups={{0,8,16,24,32,40,48,56},{2,10,18,26,34,42,50,58},{4,12,20,28,36,44,52,6..., dimensions={0} | all-to-all | bytes 524288 | tf_op jit(solution)/shard_map/all_to_all | solution.py:193
  91.9 0.0 copy-done.3
  91.9 0.9 spread.3
  92.8 0.0 copy-start.10
  92.8 0.0 copy-start.14
  92.8 4.2 %all-to-all-start.3 = ((f32[16,8,8,128]{3,2,1,0:T(8,128)}), f32[16,8,8,128]{3,2,1,0:T(8,128)S(1)}, u32[]{:S(2)}, u32[]{:S(2)}) async-start(f32[16,8,8,128]{3,2,1,0:T(8,128)} %spread.3), calls=%async_computation.3 | async-start | bytes 1048576 | tf_op jit(solution)/shard_map/all_to_all | solution.py:193
  97.0 0.0 copy-done.10
  97.0 0.0 copy-done.14
  97.1 0.0 copy-start.2
  97.1 1.2 copy-done.2
  98.3 0.0 copy-start.4
  98.3 1.2 copy-done.4
  99.5 1.7 %rotate.1 = (bf16[2,1024,256]{2,1,0:T(8,128)(2,1)S(1)}, bf16[2,1024,256]{2,1,0:T(8,128)(2,1)S(1)}, bf16[256,1024]{1,0:T(8,128)(2,1)S(1)}, bf16[256,1024]{1,0:T(8,128)(2,1)S(1)}) custom-call(s32[1]{0:T(128)} %bitcast.refs_0_.where, s32[1,32]{1,0:T(1,128)S(1)} %copy-done.14, f32[128,8,256]{2,1,0:T(8,128)S(1)} %copy-done.2, f32[128,8,256]{2,1,0:T(8,128)S(1)} %copy-done.4, ...), custom_call_target="tpu_custom_call" | custom-call | tf_op jit(solution)/shard_map/rotate/pallas_call | solution.py:234
  101.2 0.0 copy-start.5
  101.2 0.8 copy-done.5
  102.0 0.0 copy-start.7
  102.0 0.8 copy-done.7
  102.8 3.2 %all-to-all-done.3.mine = f32[16,8,8,128]{3,2,1,0:T(8,128)S(1)} async-done(((f32[16,8,8,128]{3,2,1,0:T(8,128)}), f32[16,8,8,128]{3,2,1,0:T(8,128)S(1)}, u32[]{:S(2)}, u32[]{:S(2)}) %all-to-all-start.3) | async-done | bytes 524320 | tf_op jit(solution)/shard_map/all_to_all | solution.py:193
  106.0 4.1 %collective-permute-start.3 = (f32[16,8,8,128]{3,2,1,0:T(8,128)S(1)}, f32[16,8,8,128]{3,2,1,0:T(8,128)S(1)}, u32[]{:S(2)}, u32[]{:S(2)}) collective-permute-start(f32[16,8,8,128]{3,2,1,0:T(8,128)S(1)} %all-to-all-done.3.mine), channel_id=1, source_target_pairs={{0,1},{1,0},{2,3},{3,2},{4,5},{5,4},{6,7},{7,6},{8,9},{9,8},{10,11... | collective-permute-start | bytes 1572872 | tf_op jit(solution)/shard_map/ppermute | solution.py:336
  110.1 1.5 %collective-permute-done.3.other = f32[16,8,8,128]{3,2,1,0:T(8,128)S(1)} collective-permute-done((f32[16,8,8,128]{3,2,1,0:T(8,128)S(1)}, f32[16,8,8,128]{3,2,1,0:T(8,128)S(1)}, u32[]{:S(2)}, u32[]{:S(2)}) %collective-permute-start.3) | collective-permute-done | bytes 524320 | tf_op jit(solution)/shard_map/ppermute | solution.py:336
  111.7 0.0 copy-start.6
  111.7 1.0 copy-done.6
  112.7 0.0 copy-start.8
  112.7 1.0 copy-done.8
  113.8 12.6 %outputs.1 = (f32[128,2,8,128]{3,2,1,0:T(8,128)}, f32[1,1024]{1,0:T(1,128)}) custom-call(s32[1]{0:T(128)} %bitcast.refs_0_.where, f32[16,8,8,128]{3,2,1,0:T(8,128)S(1)} %all-to-all-done.3.mine, f32[16,8,8,128]{3,2,1,0:T(8,128)S(1)} %collective-permute-done.3.other, bf16[1024,256]{1,0:T(8,128)(2,1)S(1)} %select_convert_fusion.table, ...), custom_call_target="tpu_custom_call" | custom-call | tf_op jit(solution)/shard_map/outputs/pallas_call | solution.py:314
  (3 shorter events, 0.1 us)
Async XLA Ops:
  0.6 0.7 copy-start.13
  1.3 1.2 copy-start
  2.5 1.0 copy-start.9
  5.5 4.8 %collective-permute-start = (f32[128,8,128]{2,1,0:T(8,128)S(1)}, f32[128,8,128]{2,1,0:T(8,128)S(1)}, u32[]{:S(2)}, u32[]{:S(2)}) collective-permute-start(f32[128,8,128]{2,1,0:T(8,128)S(1)} %get-tuple-element.20), channel_id=1, source_target_pairs={{0,1},{1,0},{2,3},{3,2},{4,5},{5,4},{6,7},{7,6},{8,9},{9,8},{10,11... | collective-permute-start | bytes 1572872 | tf_op jit(solution)/shard_map/ppermute | solution.py:336
  11.1 13.8 %copy-start.15 = (s32[1024]{0:T(1024)S(1)}, s32[1024]{0:T(1024)}, u32[]{:S(2)}) copy-start(s32[1024]{0:T(1024)} %param.13) | copy-start | bytes 12292
  11.1 41.2 %all-to-all-start = ((f32[128,2,8,128]{3,2,1,0:T(8,128)}), f32[128,2,8,128]{3,2,1,0:T(8,128)S(1)}, u32[]{:S(2)}, u32[]{:S(2)}) async-start(f32[128,2,8,128]{3,2,1,0:T(8,128)} %join.1), calls=%async_computation | async-start | bytes 2097152 | tf_op jit(solution)/shard_map/all_to_all | solution.py:346
  24.9 27.4 %copy-start.11 = (s32[3]{0:T(128)S(1)}, s32[3]{0:T(128)}, u32[]{:S(2)}) copy-start(s32[3]{0:T(128)} %masks.1) | copy-start | bytes 40
  24.9 27.4 %copy-start.12 = (f32[3]{0:T(128)S(1)}, f32[3]{0:T(128)}, u32[]{:S(2)}) copy-start(f32[3]{0:T(128)} %rates.1) | copy-start | bytes 40
  58.3 21.7 %copy-start.1 = (f32[128,8,256]{2,1,0:T(8,128)}, f32[128,8,256]{2,1,0:T(8,128)S(1)}, u32[]{:S(2)}) copy-start(f32[128,8,256]{2,1,0:T(8,128)S(1)} %get-tuple-element.24.own) | copy-start | bytes 3145732
  58.3 21.6 %collective-permute-start.2 = (f32[128,8,256]{2,1,0:T(8,128)S(1)}, f32[128,8,256]{2,1,0:T(8,128)S(1)}, u32[]{:S(2)}, u32[]{:S(2)}) collective-permute-start(f32[128,8,256]{2,1,0:T(8,128)S(1)} %get-tuple-element.24.own), channel_id=1, source_target_pairs={{0,1},{1,0},{2,3},{3,2},{4,5},{5,4},{6,7},{7,6},{8,9},{9,8},{10,11... | collective-permute-start | bytes 3145736 | tf_op jit(solution)/shard_map/ppermute | solution.py:336
  61.8 3.0 %collective-permute-start.1 = (f32[16,8,8,128]{3,2,1,0:T(8,128)S(1)}, f32[16,8,8,128]{3,2,1,0:T(8,128)S(1)}, u32[]{:S(2)}, u32[]{:S(2)}) collective-permute-start(f32[16,8,8,128]{3,2,1,0:T(8,128)S(1)} %get-tuple-element.23), channel_id=1, source_target_pairs={{0,1},{1,0},{2,3},{3,2},{4,5},{5,4},{6,7},{7,6},{8,9},{9,8},{10,11... | collective-permute-start | bytes 1572872 | tf_op jit(solution)/shard_map/ppermute | solution.py:336
  79.9 12.0 %copy-start.3 = (f32[128,8,256]{2,1,0:T(8,128)}, f32[128,8,256]{2,1,0:T(8,128)S(1)}, u32[]{:S(2)}) copy-start(f32[128,8,256]{2,1,0:T(8,128)S(1)} %collective-permute-done.2.other) | copy-start | bytes 3145732
  92.8 4.2 %copy-start.10 = (f32[8,64,64]{2,1,0:T(8,128)S(1)}, f32[8,64,64]{2,1,0:T(8,128)}, u32[]{:S(2)}) copy-start(f32[8,64,64]{2,1,0:T(8,128)} %bases.1) | copy-start | bytes 393220
  92.8 4.2 %copy-start.14 = (s32[1,32]{1,0:T(1,128)S(1)}, s32[1,32]{1,0:T(1,128)}, u32[]{:S(2)}) copy-start(s32[1,32]{1,0:T(1,128)} %index.1) | copy-start | bytes 388
  92.8 13.2 %all-to-all-start.3 = ((f32[16,8,8,128]{3,2,1,0:T(8,128)}), f32[16,8,8,128]{3,2,1,0:T(8,128)S(1)}, u32[]{:S(2)}, u32[]{:S(2)}) async-start(f32[16,8,8,128]{3,2,1,0:T(8,128)} %spread.3), calls=%async_computation.3 | async-start | bytes 1048576 | tf_op jit(solution)/shard_map/all_to_all | solution.py:193
  97.1 1.2 copy-start.2
  98.3 1.2 copy-start.4
  101.2 0.8 copy-start.5
  102.0 0.8 copy-start.7
  106.0 5.6 %collective-permute-start.3 = (f32[16,8,8,128]{3,2,1,0:T(8,128)S(1)}, f32[16,8,8,128]{3,2,1,0:T(8,128)S(1)}, u32[]{:S(2)}, u32[]{:S(2)}) collective-permute-start(f32[16,8,8,128]{3,2,1,0:T(8,128)S(1)} %all-to-all-done.3.mine), channel_id=1, source_target_pairs={{0,1},{1,0},{2,3},{3,2},{4,5},{5,4},{6,7},{7,6},{8,9},{9,8},{10,11... | collective-permute-start | bytes 1572872 | tf_op jit(solution)/shard_map/ppermute | solution.py:336
  111.7 1.0 copy-start.6
  112.7 1.0 copy-start.8

commit v4 on v3

v4 whole, which is shorter than its diff:
```python
import jax
import jax.numpy as jnp
from jax import lax
from jax.experimental import pallas as pl
from jax.experimental.pallas import tpu as pltpu
from jax.sharding import PartitionSpec as P

NS_ITERS = 7
F32 = jnp.float32
BF16 = jnp.bfloat16
NN = (((1,), (0,)), ((), ()))
NT = (((1,), (1,)), ((), ()))


def split(x):
    hi = x.astype(BF16)
    return hi, (x - hi.astype(F32)).astype(BF16)


def dot(a, b, dims=NN):
    return lax.dot_general(a, b, dims, preferred_element_type=F32)


def halves_of(x):
    half = x.shape[0] // 2
    return x[:half], x[half:]


def mul3(a, b, dims=NN):
    left = jnp.concatenate([a[0], a[1], a[0]], axis=dims[0][0][0])
    right = jnp.concatenate([b[0], b[0], b[1]], axis=dims[0][1][0])
    return jnp.concatenate([dot(rows, right, dims) for rows in halves_of(left)], axis=0)


def params(mib):
    return pltpu.CompilerParams(vmem_limit_bytes=mib << 20)


def gate_kernel(order, layout, gates, factor, out, mats, source, result, sems):
    steps = sems.shape[1] - 1
    chunk = factor.shape[0] // steps
    width = factor.shape[1]
    rows = [pl.ds(i * chunk, chunk) for i in range(steps)]
    first = pltpu.make_async_copy(gates, mats, sems.at[0, steps])
    first.start()
    arrive = []
    leave = []
    for i in range(steps):
        arrive.append(pltpu.make_async_copy(factor.at[rows[i]], source.at[rows[i]], sems.at[0, i]))
        arrive[i].start()
        leave.append(pltpu.make_async_copy(result.at[rows[i]], out.at[rows[i]], sems.at[1, i]))
    first.wait()
    for i in range(steps):
        arrive[i].wait()
        for b in range(i * chunk // order, (i + 1) * chunk // order):
            block = slice(b * order, (b + 1) * order)
            high, low = split(source[block, :])
            left = jnp.concatenate(split(mats[layout[b]]), axis=1)
            right = jnp.concatenate(
                [
                    jnp.concatenate([high, low], axis=1),
                    jnp.concatenate([high, jnp.zeros_like(high)], axis=1),
                ],
                axis=0,
            )
            both = dot(left, right)
            result[block, :] = both[:, :width] + both[:, width:]
        leave[i].start()
    for copy in leave:
        copy.wait()


def apply_gates(gates, layout, factor):
    order = gates.shape[1]
    away = pl.BlockSpec(memory_space=pltpu.HBM)
    steps = 4
    return pl.pallas_call(
        lambda *refs: gate_kernel(order, *refs),
        out_shape=jax.ShapeDtypeStruct(factor.shape, F32),
        in_specs=[pl.BlockSpec(memory_space=pltpu.SMEM), away, away],
        out_specs=away,
        scratch_shapes=[
            pltpu.VMEM(gates.shape, F32),
            pltpu.VMEM(factor.shape, F32),
            pltpu.VMEM(factor.shape, F32),
            pltpu.SemaphoreType.DMA((2, steps + 1)),
        ],
        compiler_params=params(8),
        name="gates",
    )(layout, gates, factor)


def stack_kernel(where, masks, rates, moved, table, sketch, keep, send, high, low):
    count, halves, lows, width = moved.shape
    rank = halves * width
    jumps = masks.shape[0]
    total = rates[0]
    for k in range(1, jumps):
        total = total + rates[k]
    coefs = [jnp.full((2 * lows, width), 1.0 - 0.5 * total, F32)]
    for k in range(jumps):
        coefs.append(jnp.sqrt(jnp.full((2 * lows, width), rates[k], F32)))

    value = [jnp.zeros((count * lows // 2, rank), F32)] * 2
    for k in range(jumps + 1):
        flip = 0 if k == 0 else masks[k - 1]
        cols = slice(k * rank, (k + 1) * rank)
        for p in range(count // 2):
            first, second = (2 * p) ^ flip, (2 * p + 1) ^ flip
            rows = slice(p * 2 * lows, (p + 1) * 2 * lows)
            for c in range(halves):
                pair = coefs[k] * jnp.concatenate([moved[first, c], moved[second, c]], axis=0)
                part = slice(k * rank + c * width, k * rank + (c + 1) * width)
                high[rows, part], low[rows, part] = split(pair)
        left = jnp.concatenate([high[:, cols], low[:, cols]], axis=1)
        right = jnp.concatenate([table[cols, :]] * 2, axis=0)
        value = [v + dot(rows, right) for v, rows in zip(value, halves_of(left))]
    value = jnp.concatenate(value, axis=0)
    sketch[...] = value.reshape(sketch.shape)
    left = split(value.T)
    mine = where[0] == 0
    half = rank // 2
    for k in range(jumps + 1):
        cols = slice(k * rank, (k + 1) * rank)
        part = mul3(left, (high[:, cols], low[:, cols]))
        for j in range(rank // 128):
            tiles = part[:, j * 128 : (j + 1) * 128]
            top = tiles[:half].reshape(half // 8, 8, 128)
            bottom = tiles[half:].reshape(half // 8, 8, 128)
            keep[:, k * (rank // 128) + j] = jnp.where(mine, top, bottom)
            send[:, k * (rank // 128) + j] = jnp.where(mine, bottom, top)


def stack_products(where, masks, rates, moved, table):
    count, halves, lows, width = moved.shape
    rank = halves * width
    columns = table.shape[0]
    vmem = pl.BlockSpec(memory_space=pltpu.VMEM)
    smem = pl.BlockSpec(memory_space=pltpu.SMEM)
    half = jax.ShapeDtypeStruct((rank // 16, columns // 128, 8, 128), F32)
    return pl.pallas_call(
        stack_kernel,
        out_shape=(jax.ShapeDtypeStruct((count, lows, rank), F32), half, half),
        in_specs=[smem, smem, smem, vmem, vmem],
        out_specs=(vmem, vmem, vmem),
        scratch_shapes=[pltpu.VMEM((count * lows, columns), BF16)] * 2,
        compiler_params=params(20),
        name="stack",
    )(where, masks, rates, moved, table)


SIDES = (4, 8, 4)


def groups(count):
    ny, nz, nx = SIDES
    assert ny * nz * nx == count
    at = lambda y, z, x: (y * nz + z) * nx + x
    planes = [[at(y, z, x) for y in range(ny) for x in range(nx)] for z in range(nz)]
    lines = [[at(y, z, x) for z in range(nz)] for y in range(ny) for x in range(nx)]
    return planes, lines


def spread_kernel(parts, out):
    out[...] = jnp.broadcast_to(jnp.sum(parts[...], axis=0, keepdims=True), out.shape)


def sum_and_spread(parts, copies):
    vmem = pl.BlockSpec(memory_space=pltpu.VMEM)
    return pl.pallas_call(
        spread_kernel,
        out_shape=jax.ShapeDtypeStruct((copies,) + parts.shape[1:], F32),
        in_specs=[vmem],
        out_specs=vmem,
        compiler_params=params(4),
        name="spread",
    )(parts)


def exchange(pieces, members):
    return lax.all_to_all(
        pieces, "wide", split_axis=0, concat_axis=0, axis_index_groups=members, tiled=True
    )


def sum_wide(part, beside):
    planes, lines = groups(lax.axis_size("wide"))
    assert len(planes[0]) == part.shape[0]
    pieces = exchange(part, planes)
    pieces, beside = lax.optimization_barrier((pieces, beside))
    pieces = exchange(sum_and_spread(pieces, len(lines[0])), lines)
    return exchange(sum_and_spread(pieces, len(planes[0])), planes), beside


def rotate_kernel(where, index, own, other, bases, sk, rot, rotated, sk_near, rot_near, sems):
    count, lows, rank = own.shape
    order = bases.shape[1]
    group = order // (2 * lows)
    blocks = rotated.shape[0] // order
    core = where[0]
    mine = core == 0
    for part, value in enumerate(split(own[...].reshape(count * lows, rank))):
        sk_near[part, core] = value
    for part, value in enumerate(split(other[...].reshape(count * lows, rank))):
        sk_near[part, 1 - core] = value
    leave = pltpu.make_async_copy(sk_near, sk, sems.at[0])
    leave.start()
    for b in range(blocks):
        parts = []
        for g in range(group):
            w = core * (count // 2) + b * group + g
            first, second = own[w], other[w]
            parts.append(jnp.where(mine, first, second))
            parts.append(jnp.where(mine, second, first))
        data = jnp.concatenate(parts, axis=0)
        value = mul3(split(bases[index[0, core * blocks + b]]), split(data))
        rotated[b * order : (b + 1) * order, :] = value
    rot_near[0], rot_near[1] = split(rotated[...].T)
    last = pltpu.make_async_copy(rot_near, rot, sems.at[1])
    last.start()
    leave.wait()
    last.wait()


def rotate_sketch(where, index, own, other, bases):
    count, lows, rank = own.shape
    rows = count * lows
    vmem = pl.BlockSpec(memory_space=pltpu.VMEM)
    smem = pl.BlockSpec(memory_space=pltpu.SMEM)
    away = pl.BlockSpec(memory_space=pltpu.HBM)
    shapes = ((2, 2, rows, rank), (2, rank, rows))
    return pl.pallas_call(
        rotate_kernel,
        out_shape=tuple(jax.ShapeDtypeStruct(shape, BF16) for shape in shapes),
        in_specs=[smem, smem, vmem, vmem, vmem],
        out_specs=(away, away),
        scratch_shapes=[pltpu.VMEM((rows, rank), F32)]
        + [pltpu.VMEM(shape, BF16) for shape in shapes]
        + [pltpu.SemaphoreType.DMA((2,))],
        compiler_params=params(16),
        name="rotate",
    )(where, index, own, other, bases)


def frobenius(mat):
    return jnp.sqrt(jnp.sum(jnp.sum(mat * mat, axis=0, keepdims=True), axis=1, keepdims=True))


def eye(n):
    return (
        lax.broadcasted_iota(jnp.int32, (n, n), 0) == lax.broadcasted_iota(jnp.int32, (n, n), 1)
    ).astype(F32)


def newton(mat, value):
    t = mat
    held = None
    for step in range(NS_ITERS):
        last = step == NS_ITERS - 1
        right = split(t)
        if step == 0:
            once = 1.5 * t - 0.5 * mul3(right, right)
            held = 1.5 * eye(t.shape[0]) - 0.5 * t if value is None else once
        else:
            if not last:
                once = 1.5 * t - 0.5 * mul3(right, right)
            held = 1.5 * held - 0.5 * mul3(split(held), right)
        if not last:
            t = 1.5 * once - 0.5 * mul3(split(once), right)
    return held


def output_kernel(where, mine, other, table, sk, rot, new, weights, proj, sk_near, rot_near, sems):
    rank = proj.shape[0]
    halves = sk.shape[1]
    width = rank // halves
    copies = [
        pltpu.make_async_copy(rot, rot_near, sems.at[0]),
        pltpu.make_async_copy(sk, sk_near, sems.at[1]),
    ]
    for copy in copies:
        copy.start()
    first = pl.ds(pl.multiple_of(where[0] * width, width), width)
    second = pl.ds(pl.multiple_of((1 - where[0]) * width, width), width)
    for j in range(mine.shape[1]):
        cols = slice(j * 128, (j + 1) * 128)
        proj[first, cols] = mine[:, j].reshape(width, 128)
        proj[second, cols] = other[:, j].reshape(width, 128)
    p = split(proj[...])
    left = jnp.concatenate(p, axis=1)
    right = jnp.concatenate([table[...]] * 2, axis=0)
    gram = jnp.concatenate([dot(rows, right) for rows in halves_of(left)], axis=0)
    inverse = newton(gram / (frobenius(gram) + 1e-6), None)
    inv = split(inverse)
    coeff = split(mul3(inv, p))
    core = mul3(coeff, coeff, NT)
    shift = frobenius(core) + 1e-6
    root = split(newton(core / shift, "approx"))
    scale = jnp.sqrt(shift)
    mixing = scale * mul3(inv, root)
    turned = split(scale * mul3(root, inv))
    own = split(jnp.where(where[0] == 0, mixing[:, :width], mixing[:, width:]))
    copies[1].wait()
    for c in range(halves):
        value = mul3((sk_near[0, c], sk_near[1, c]), own)
        new[:, c] = value.reshape(new.shape[0], new.shape[2], width)
    copies[0].wait()
    turn = mul3(turned, (rot_near[0], rot_near[1]))
    weights[...] = jnp.sum(turn * turn, axis=0, keepdims=True) / rank


def outputs(where, mine, other, table, sk, rot, lows):
    halves, rows, rank = sk.shape[1:]
    vmem = pl.BlockSpec(memory_space=pltpu.VMEM)
    smem = pl.BlockSpec(memory_space=pltpu.SMEM)
    away = pl.BlockSpec(memory_space=pltpu.HBM)
    return pl.pallas_call(
        output_kernel,
        out_shape=(
            jax.ShapeDtypeStruct((rows // lows, halves, lows, rank // halves), F32),
            jax.ShapeDtypeStruct((1, rows), F32),
        ),
        in_specs=[smem] + [vmem] * 3 + [away] * 2,
        out_specs=(vmem, vmem),
        scratch_shapes=[
            pltpu.VMEM((rank, table.shape[0]), F32),
            pltpu.VMEM(sk.shape, BF16),
            pltpu.VMEM(rot.shape, BF16),
            pltpu.SemaphoreType.DMA((2,)),
        ],
        compiler_params=params(20),
        name="outputs",
    )(where, mine, other, table, sk, rot)


def sketch_table(sketch_perm, rank):
    target = sketch_perm % rank
    sign = 1.0 - 2.0 * (sketch_perm // rank % 2).astype(F32)
    hit = target[:, None] == jnp.arange(rank, dtype=jnp.int32)[None, :]
    return jnp.where(hit, sign[:, None], jnp.zeros((), F32)).astype(BF16)


def swap(value):
    return lax.ppermute(value, "cols", [(0, 1), (1, 0)])


def per_device(factor, gates, gate_layout, jump_masks, jump_rates, sketch_perm, bases, basis_index):
    rows, width = factor.shape
    count = lax.axis_size("wide")
    rank = width * lax.axis_size("cols")
    where = lax.axis_index("cols").astype(jnp.int32).reshape(1)
    gated = apply_gates(gates, gate_layout, factor).reshape(2 * count, -1, width)
    moved = lax.all_to_all(gated, ("wide", "cols"), split_axis=0, concat_axis=0, tiled=True)
    moved = moved.reshape(count, 2, -1, width)
    table = sketch_table(sketch_perm, rank)
    sketch, keep, send = stack_products(where, jump_masks, jump_rates, moved, table)
    part = keep + swap(send)
    part, sketch = lax.optimization_barrier((part, sketch))
    total, other = sum_wide(part, swap(sketch))
    turned = rotate_sketch(where, basis_index, sketch, other, bases)
    total, turned = lax.optimization_barrier((total, turned))
    new, weights = outputs(where, total, swap(total), table, *turned, moved.shape[2])
    return new.reshape(rows, width), weights


def solution(mesh):
    return jax.shard_map(
        per_device,
        mesh=mesh,
        in_specs=(P("wide", "cols"), P(), P("wide"), P(), P(), P(), P(), P("wide", None)),
        out_specs=(P("wide", "cols"), P("wide", "cols")),
        check_vma=False,
    )
```

time: 127 us -> 120 us (0.945)
  starting transfers between devices: 29 us -> 24.7 us
  Pallas kernels: 23.9 us -> 20.7 us
    ppermute x4 -> x3, starting transfers between devices: 11 us -> 5.26 us  [swap(): return lax.ppermute(value, 'cols', [(0, 1), (1, 0)])]
    all_to_all x1, waiting for transfers between devices: 27 us -> 30.7 us  [per_device(): lax.all_to_all(gated, ('wide', 'cols'), split_axis=0, concat_axis=0, tile...]
    ppermute x4 -> x3, waiting for transfers between devices: 6.01 us -> 3.08 us  [swap(): return lax.ppermute(value, 'cols', [(0, 1), (1, 0)])]
    pallas_call x1, Pallas kernels: 6 us -> 3.8 us  [stack_products(): pl.pallas_call(stack_kernel, out_shape=(jax.ShapeDtypeStruct((count, lows...]
    all_to_all x1, starting transfers between devices: 13.8 us -> 15.7 us  [per_device(): lax.all_to_all(gated, ('wide', 'cols'), split_axis=0, concat_axis=0, tile...]
    unnamed x32 -> x28, local copies, waits for them, and re-layouts: 9.08 us -> 8.57 us
    pallas_call x3 -> x2, Pallas kernels: 4.4 us -> 4.36 us  [the longest x1 2.41 us: apply_gates(): pl.pallas_call(lambda *refs: gate_kernel(order, *refs), out_shape=jax.Sha...]
  transfers between devices with their start and end apart: 6 -> 5, of which waited for: 5 -> 4; matrix products, arithmetic and copies ran while one was open for 0% -> 0% of each run, Pallas kernels for 1% -> 2%
where the time goes in v4:
time: 120 us
  waiting for transfers between devices  37.4 us (31%)
  blocking collectives  26.9 us (22%)
  starting transfers between devices  24.7 us (21%)
  Pallas kernels  20.7 us (17%)
  local copies, waits for them, and re-layouts  8.57 us (7%)
    all_to_all x1, waiting for transfers between devices, per_device(): lax.all_to_all(gated, ('wide', 'cols'), split_axis=0, concat_axis=0, tile...  30.7 us
    all_to_all x2, blocking collectives, exchange(): lax.all_to_all(pieces, 'wide', split_axis=0, concat_axis=0, axis_index_gr...  26.9 us
    all_to_all x1, starting transfers between devices, per_device(): lax.all_to_all(gated, ('wide', 'cols'), split_axis=0, concat_axis=0, tile...  15.7 us
    pallas_call x1, Pallas kernels, outputs(): pl.pallas_call(output_kernel, out_shape=(jax.ShapeDtypeStruct((rows // lo...  11.6 us
    unnamed x28, local copies, waits for them, and re-layouts  8.57 us
    ppermute x3, starting transfers between devices, swap(): return lax.ppermute(value, 'cols', [(0, 1), (1, 0)])  5.26 us
    pallas_call x1, Pallas kernels, stack_products(): pl.pallas_call(stack_kernel, out_shape=(jax.ShapeDtypeStruct((count, lows...  3.8 us
    all_to_all x1, starting transfers between devices, exchange(): lax.all_to_all(pieces, 'wide', split_axis=0, concat_axis=0, axis_index_gr...  3.77 us
  transfers between devices with their start and end apart: 5, of which 4 were waited for; matrix products, arithmetic and copies ran while one was open for 0% of the time, Pallas kernels for 2%

profile of v4, /device:TPU:1, one launch (start us, length us, event | category | flops | bytes accessed | tf_op | source)
XLA Modules:
  0.0 119.6 jit_solution(12862007278119232003)
XLA Ops:
  0.6 0.0 copy-start.2
  0.6 1.2 %copy-done.2 = f32[2048,128]{1,0:T(8,128)S(1)} copy-done((f32[2048,128]{1,0:T(8,128)S(1)}, f32[2048,128]{1,0:T(8,128)}, u32[]{:S(2)}) %copy-start.2) | copy-done | bytes 1048600
  1.9 0.0 copy-start.7
  1.9 1.0 copy-done.7
  2.9 0.0 copy-start.11
  2.9 0.7 copy-done.11
  3.6 0.0 copy-start.13
  3.6 0.0 copy-start.9
  3.6 0.0 copy-start.10
  3.6 2.4 %gates.1 = f32[2048,128]{1,0:T(8,128)} custom-call(s32[16]{0:T(128)S(1)} %copy-done.11, f32[8,128,128]{2,1,0:T(8,128)S(1)} %copy-done.7, f32[2048,128]{1,0:T(8,128)S(1)} %copy-done.2), custom_call_target="tpu_custom_call" | custom-call | tf_op jit(solution)/shard_map/gates/pallas_call | solution.py:77
  6.0 15.7 %all-to-all-start = ((f32[256,8,128]{2,1,0:T(8,128)}), f32[256,8,128]{2,1,0:T(8,128)S(1)}, u32[]{:S(2)}, u32[]{:S(2)}) async-start(f32[256,8,128]{2,1,0:T(8,128)} %bitcast.1), calls=%async_computation | async-start | bytes 2097152 | tf_op jit(solution)/shard_map/all_to_all | solution.py:353
  21.7 0.0 copy-done.13
  21.7 0.3 select_convert_fusion.table
  22.0 30.7 %all-to-all-done = f32[256,8,128]{2,1,0:T(8,128)S(1)} async-done(((f32[256,8,128]{2,1,0:T(8,128)}), f32[256,8,128]{2,1,0:T(8,128)S(1)}, u32[]{:S(2)}, u32[]{:S(2)}) %all-to-all-start) | async-done | bytes 1048608 | tf_op jit(solution)/shard_map/all_to_all | solution.py:353
  52.7 0.0 copy-done.9
  52.8 0.0 copy-done.10
  52.8 3.8 %stack.1 = (f32[128,8,256]{2,1,0:T(8,128)S(1)}, f32[16,8,8,128]{3,2,1,0:T(8,128)S(1)}, f32[16,8,8,128]{3,2,1,0:T(8,128)S(1)}) custom-call(s32[1]{0:T(128)} %bitcast.where, s32[3]{0:T(128)S(1)} %copy-done.9, f32[3]{0:T(128)S(1)} %copy-done.10, f32[128,2,8,128]{3,2,1,0:T(8,128)S(1)} %bitcast.4, bf16[1024,256]{1,0:T(8,128)(2,1)S(1)} %select_convert_fusion.table), custom_call_target="tpu_custom_call" | custom-call | tf_op jit(solution)/shard_map/stack/pallas_call | solution.py:141
  56.6 0.0 copy-start.3
  56.6 0.8 collective-permute-start
  57.3 1.5 %collective-permute-done = f32[16,8,8,128]{3,2,1,0:T(8,128)S(1)} collective-permute-done((f32[16,8,8,128]{3,2,1,0:T(8,128)S(1)}, f32[16,8,8,128]{3,2,1,0:T(8,128)S(1)}, u32[]{:S(2)}, u32[]{:S(2)}) %collective-permute-start) | collective-permute-done | bytes 524320 | tf_op jit(solution)/shard_map/ppermute | solution.py:344
  58.9 0.1 add.16
  58.9 0.0 copy-start.8
  59.0 0.0 copy-start.12
  59.0 0.5 collective-permute-start.1
  59.4 14.6 %all_to_all.20.parts = f32[16,8,8,128]{3,2,1,0:T(8,128)S(1)} all-to-all(f32[16,8,8,128]{3,2,1,0:T(8,128)S(1)} %add.16), channel_id=1, replica_groups={{0,2,4,6,64,66,68,70,128,130,132,134,192,194,196,198},{8,10,12,14,72,74..., dimensions={0} | all-to-all | bytes 1048576 | tf_op jit(solution)/shard_map/all_to_all | solution.py:181
  74.0 0.0 collective-permute-done.1.other
  74.0 0.0 copy-start.5
  74.0 1.0 copy-done.5
  75.0 12.3 %all_to_all.21.parts = f32[8,8,8,128]{3,2,1,0:T(8,128)S(1)} all-to-all(f32[8,8,8,128]{3,2,1,0:T(8,128)S(1)} %spread.2), channel_id=1, replica_groups={{0,8,16,24,32,40,48,56},{2,10,18,26,34,42,50,58},{4,12,20,28,36,44,52,6..., dimensions={0} | all-to-all | bytes 524288 | tf_op jit(solution)/shard_map/all_to_all | solution.py:181
  87.4 0.0 copy-done.3
  87.4 0.9 spread.3
  88.2 3.8 %all-to-all-start.3 = ((f32[16,8,8,128]{3,2,1,0:T(8,128)}), f32[16,8,8,128]{3,2,1,0:T(8,128)S(1)}, u32[]{:S(2)}, u32[]{:S(2)}) async-start(f32[16,8,8,128]{3,2,1,0:T(8,128)} %spread.3), calls=%async_computation.3 | async-start | bytes 1048576 | tf_op jit(solution)/shard_map/all_to_all | solution.py:181
  92.0 0.0 copy-done.8
  92.0 0.0 copy-done.12
  92.0 0.0 copy-start.4
  92.0 1.2 %copy-done.4 = f32[128,8,256]{2,1,0:T(8,128)S(1)} copy-done((f32[128,8,256]{2,1,0:T(8,128)S(1)}, f32[128,8,256]{2,1,0:T(8,128)}, u32[]{:S(2)}) %copy-start.4) | copy-done | bytes 1048600
  93.3 0.0 copy-start.6
  93.3 1.2 %copy-done.6 = f32[128,8,256]{2,1,0:T(8,128)S(1)} copy-done((f32[128,8,256]{2,1,0:T(8,128)S(1)}, f32[128,8,256]{2,1,0:T(8,128)}, u32[]{:S(2)}) %copy-start.6) | copy-done | bytes 1048600
  94.5 1.9 %rotate.1 = (bf16[2,2,1024,256]{3,2,1,0:T(8,128)(2,1)S(1)}, bf16[2,256,1024]{2,1,0:T(8,128)(2,1)S(1)}) custom-call(s32[1]{0:T(128)} %bitcast.where, s32[1,32]{1,0:T(1,128)S(1)} %copy-done.12, f32[128,8,256]{2,1,0:T(8,128)S(1)} %copy-done.4, f32[128,8,256]{2,1,0:T(8,128)S(1)} %copy-done.6, f32[8,64,64]{2,1,0:T(8,128)S(1)} %copy-done.8), custom_call_target="tpu_custom_call" | custom-call | tf_op jit(solution)/shard_map/rotate/pallas_call | solution.py:232
  96.4 0.0 copy-start
  96.4 1.0 copy-done
  97.4 3.6 %all-to-all-done.3.mine = f32[16,8,8,128]{3,2,1,0:T(8,128)S(1)} async-done(((f32[16,8,8,128]{3,2,1,0:T(8,128)}), f32[16,8,8,128]{3,2,1,0:T(8,128)S(1)}, u32[]{:S(2)}, u32[]{:S(2)}) %all-to-all-start.3) | async-done | bytes 524320 | tf_op jit(solution)/shard_map/all_to_all | solution.py:181
  101.0 4.0 %collective-permute-start.2 = (f32[16,8,8,128]{3,2,1,0:T(8,128)S(1)}, f32[16,8,8,128]{3,2,1,0:T(8,128)S(1)}, u32[]{:S(2)}, u32[]{:S(2)}) collective-permute-start(f32[16,8,8,128]{3,2,1,0:T(8,128)S(1)} %all-to-all-done.3.mine), channel_id=1, source_target_pairs={{0,1},{1,0},{2,3},{3,2},{4,5},{5,4},{6,7},{7,6},{8,9},{9,8},{10,11... | collective-permute-start | bytes 1572872 | tf_op jit(solution)/shard_map/ppermute | solution.py:344
  105.0 1.5 %collective-permute-done.2.other = f32[16,8,8,128]{3,2,1,0:T(8,128)S(1)} collective-permute-done((f32[16,8,8,128]{3,2,1,0:T(8,128)S(1)}, f32[16,8,8,128]{3,2,1,0:T(8,128)S(1)}, u32[]{:S(2)}, u32[]{:S(2)}) %collective-permute-start.2) | collective-permute-done | bytes 524320 | tf_op jit(solution)/shard_map/ppermute | solution.py:344
  106.6 0.0 copy-start.1
  106.6 1.2 %copy-done.1 = bf16[2,256,1024]{2,1,0:T(8,128)(2,1)S(1)} copy-done((bf16[2,256,1024]{2,1,0:T(8,128)(2,1)S(1)}, bf16[2,256,1024]{2,1,0:T(8,128)(2,1)}, u32[]{:S(2)}) %copy-start.1) | copy-done | bytes 1048600
  107.8 11.6 %outputs.1 = (f32[128,2,8,128]{3,2,1,0:T(8,128)}, f32[1,1024]{1,0:T(1,128)}) custom-call(s32[1]{0:T(128)} %bitcast.where, f32[16,8,8,128]{3,2,1,0:T(8,128)S(1)} %all-to-all-done.3.mine, f32[16,8,8,128]{3,2,1,0:T(8,128)S(1)} %collective-permute-done.2.other, bf16[1024,256]{1,0:T(8,128)(2,1)S(1)} %select_convert_fusion.table, ...), custom_call_target="tpu_custom_call" | custom-call | tf_op jit(solution)/shard_map/outputs/pallas_call | solution.py:317
  (3 shorter events, 0.1 us)
Async XLA Ops:
  0.6 1.2 %copy-start.2 = (f32[2048,128]{1,0:T(8,128)S(1)}, f32[2048,128]{1,0:T(8,128)}, u32[]{:S(2)}) copy-start(f32[2048,128]{1,0:T(8,128)} %refs_2_.1) | copy-start | bytes 3145732
  1.9 1.0 copy-start.7
  2.9 0.7 copy-start.11
  3.6 18.1 %copy-start.13 = (s32[1024]{0:T(1024)S(1)}, s32[1024]{0:T(1024)}, u32[]{:S(2)}) copy-start(s32[1024]{0:T(1024)} %param.13) | copy-start | bytes 12292
  3.6 49.2 %copy-start.9 = (s32[3]{0:T(128)S(1)}, s32[3]{0:T(128)}, u32[]{:S(2)}) copy-start(s32[3]{0:T(128)} %masks.1) | copy-start | bytes 40
  3.6 49.2 %copy-start.10 = (f32[3]{0:T(128)S(1)}, f32[3]{0:T(128)}, u32[]{:S(2)}) copy-start(f32[3]{0:T(128)} %rates.1) | copy-start | bytes 40
  6.0 46.8 %all-to-all-start = ((f32[256,8,128]{2,1,0:T(8,128)}), f32[256,8,128]{2,1,0:T(8,128)S(1)}, u32[]{:S(2)}, u32[]{:S(2)}) async-start(f32[256,8,128]{2,1,0:T(8,128)} %bitcast.1), calls=%async_computation | async-start | bytes 2097152 | tf_op jit(solution)/shard_map/all_to_all | solution.py:353
  56.6 30.8 %copy-start.3 = (f32[128,8,256]{2,1,0:T(8,128)}, f32[128,8,256]{2,1,0:T(8,128)S(1)}, u32[]{:S(2)}) copy-start(f32[128,8,256]{2,1,0:T(8,128)S(1)} %get-tuple-element.20.own) | copy-start | bytes 3145732
  56.6 2.3 %collective-permute-start = (f32[16,8,8,128]{3,2,1,0:T(8,128)S(1)}, f32[16,8,8,128]{3,2,1,0:T(8,128)S(1)}, u32[]{:S(2)}, u32[]{:S(2)}) collective-permute-start(f32[16,8,8,128]{3,2,1,0:T(8,128)S(1)} %get-tuple-element.17), channel_id=1, source_target_pairs={{0,1},{1,0},{2,3},{3,2},{4,5},{5,4},{6,7},{7,6},{8,9},{9,8},{10,11... | collective-permute-start | bytes 1572872 | tf_op jit(solution)/shard_map/ppermute | solution.py:344
  58.9 33.1 %copy-start.8 = (f32[8,64,64]{2,1,0:T(8,128)S(1)}, f32[8,64,64]{2,1,0:T(8,128)}, u32[]{:S(2)}) copy-start(f32[8,64,64]{2,1,0:T(8,128)} %bases.1) | copy-start | bytes 393220
  59.0 33.1 %copy-start.12 = (s32[1,32]{1,0:T(1,128)S(1)}, s32[1,32]{1,0:T(1,128)}, u32[]{:S(2)}) copy-start(s32[1,32]{1,0:T(1,128)} %index.1) | copy-start | bytes 388
  59.0 15.0 %collective-permute-start.1 = (f32[128,8,256]{2,1,0:T(8,128)S(1)}, f32[128,8,256]{2,1,0:T(8,128)S(1)}, u32[]{:S(2)}, u32[]{:S(2)}) collective-permute-start(f32[128,8,256]{2,1,0:T(8,128)S(1)} %get-tuple-element.20.own), channel_id=1, source_target_pairs={{0,1},{1,0},{2,3},{3,2},{4,5},{5,4},{6,7},{7,6},{8,9},{9,8},{10,11... | collective-permute-start | bytes 3145736 | tf_op jit(solution)/shard_map/ppermute | solution.py:344
  74.0 1.0 copy-start.5
  88.2 12.8 %all-to-all-start.3 = ((f32[16,8,8,128]{3,2,1,0:T(8,128)}), f32[16,8,8,128]{3,2,1,0:T(8,128)S(1)}, u32[]{:S(2)}, u32[]{:S(2)}) async-start(f32[16,8,8,128]{3,2,1,0:T(8,128)} %spread.3), calls=%async_computation.3 | async-start | bytes 1048576 | tf_op jit(solution)/shard_map/all_to_all | solution.py:181
  92.0 1.2 %copy-start.4 = (f32[128,8,256]{2,1,0:T(8,128)S(1)}, f32[128,8,256]{2,1,0:T(8,128)}, u32[]{:S(2)}) copy-start(f32[128,8,256]{2,1,0:T(8,128)} %copy-done.3) | copy-start | bytes 3145732
  93.3 1.2 %copy-start.6 = (f32[128,8,256]{2,1,0:T(8,128)S(1)}, f32[128,8,256]{2,1,0:T(8,128)}, u32[]{:S(2)}) copy-start(f32[128,8,256]{2,1,0:T(8,128)} %copy-done.5) | copy-start | bytes 3145732
  96.4 1.0 copy-start
  101.0 5.6 %collective-permute-start.2 = (f32[16,8,8,128]{3,2,1,0:T(8,128)S(1)}, f32[16,8,8,128]{3,2,1,0:T(8,128)S(1)}, u32[]{:S(2)}, u32[]{:S(2)}) collective-permute-start(f32[16,8,8,128]{3,2,1,0:T(8,128)S(1)} %all-to-all-done.3.mine), channel_id=1, source_target_pairs={{0,1},{1,0},{2,3},{3,2},{4,5},{5,4},{6,7},{7,6},{8,9},{9,8},{10,11... | collective-permute-start | bytes 1572872 | tf_op jit(solution)/shard_map/ppermute | solution.py:344
  106.6 1.2 %copy-start.1 = (bf16[2,256,1024]{2,1,0:T(8,128)(2,1)S(1)}, bf16[2,256,1024]{2,1,0:T(8,128)(2,1)}, u32[]{:S(2)}) copy-start(bf16[2,256,1024]{2,1,0:T(8,128)(2,1)} %copy-done) | copy-start | bytes 3145732

commit v5 on v4

--- a/solution.py
+++ b/solution.py
@@ -32,8 +32,11 @@
     return jnp.concatenate([dot(rows, right, dims) for rows in halves_of(left)], axis=0)
 
 
+WHOLE = 60
+
+
 def params(mib):
-    return pltpu.CompilerParams(vmem_limit_bytes=mib << 20)
+    return pltpu.CompilerParams(vmem_limit_bytes=int(mib * 2**20))
 
 
 def gate_kernel(order, layout, gates, factor, out, mats, source, result, sems):
@@ -85,7 +88,7 @@
             pltpu.VMEM(factor.shape, F32),
             pltpu.SemaphoreType.DMA((2, steps + 1)),
         ],
-        compiler_params=params(8),
+        compiler_params=params(WHOLE),
         name="gates",
     )(layout, gates, factor)
 
@@ -192,18 +195,33 @@
     return exchange(sum_and_spread(pieces, len(planes[0])), planes), beside
 
 
-def rotate_kernel(where, index, own, other, bases, sk, rot, rotated, sk_near, rot_near, sems):
+PADDED = 16
+
+
+def rotate_kernel(
+    where, index, own_away, other_away, mats_away, kept,
+    own, other, mats, rotated, near, sems,
+):
     count, lows, rank = own.shape
-    order = bases.shape[1]
+    order = mats.shape[1]
     group = order // (2 * lows)
     blocks = rotated.shape[0] // order
     core = where[0]
     mine = core == 0
+    arrive = [
+        pltpu.make_async_copy(own_away, own, sems.at[0]),
+        pltpu.make_async_copy(other_away, other, sems.at[1]),
+        pltpu.make_async_copy(mats_away, mats, sems.at[2]),
+    ]
+    for copy in arrive:
+        copy.start()
+    for copy in arrive:
+        copy.wait()
     for part, value in enumerate(split(own[...].reshape(count * lows, rank))):
-        sk_near[part, core] = value
+        near[part, core] = value
     for part, value in enumerate(split(other[...].reshape(count * lows, rank))):
-        sk_near[part, 1 - core] = value
-    leave = pltpu.make_async_copy(sk_near, sk, sems.at[0])
+        near[part, 1 - core] = value
+    leave = pltpu.make_async_copy(near.at[:, :2], kept.at[:, :2], sems.at[3])
     leave.start()
     for b in range(blocks):
         parts = []
@@ -213,10 +231,13 @@
             parts.append(jnp.where(mine, first, second))
             parts.append(jnp.where(mine, second, first))
         data = jnp.concatenate(parts, axis=0)
-        value = mul3(split(bases[index[0, core * blocks + b]]), split(data))
+        value = mul3(split(mats[index[0, core * blocks + b]]), split(data))
         rotated[b * order : (b + 1) * order, :] = value
-    rot_near[0], rot_near[1] = split(rotated[...].T)
-    last = pltpu.make_async_copy(rot_near, rot, sems.at[1])
+    for q in range(rotated.shape[0] // rank):
+        rows = slice(q * rank, (q + 1) * rank)
+        for part, value in enumerate(split(rotated[rows, :].T)):
+            near[part, 2, rows] = value
+    last = pltpu.make_async_copy(near.at[:, 2], kept.at[:, 2], sems.at[4])
     last.start()
     leave.wait()
     last.wait()
@@ -225,19 +246,22 @@
 def rotate_sketch(where, index, own, other, bases):
     count, lows, rank = own.shape
     rows = count * lows
-    vmem = pl.BlockSpec(memory_space=pltpu.VMEM)
     smem = pl.BlockSpec(memory_space=pltpu.SMEM)
-    away = pl.BlockSpec(memory_space=pltpu.HBM)
-    shapes = ((2, 2, rows, rank), (2, rank, rows))
+    away = pl.BlockSpec(memory_space=pl.ANY)
     return pl.pallas_call(
         rotate_kernel,
-        out_shape=tuple(jax.ShapeDtypeStruct(shape, BF16) for shape in shapes),
-        in_specs=[smem, smem, vmem, vmem, vmem],
-        out_specs=(away, away),
-        scratch_shapes=[pltpu.VMEM((rows, rank), F32)]
-        + [pltpu.VMEM(shape, BF16) for shape in shapes]
-        + [pltpu.SemaphoreType.DMA((2,))],
-        compiler_params=params(16),
+        out_shape=jax.ShapeDtypeStruct((2, PADDED, rows, rank), BF16),
+        in_specs=[smem, smem, away, away, away],
+        out_specs=away,
+        scratch_shapes=[
+            pltpu.VMEM(own.shape, F32),
+            pltpu.VMEM(own.shape, F32),
+            pltpu.VMEM(bases.shape, F32),
+            pltpu.VMEM((rows, rank), F32),
+            pltpu.VMEM((2, 3, rows, rank), BF16),
+            pltpu.SemaphoreType.DMA((5,)),
+        ],
+        compiler_params=params(WHOLE),
         name="rotate",
     )(where, index, own, other, bases)
 
@@ -270,16 +294,12 @@
     return held
 
 
-def output_kernel(where, mine, other, table, sk, rot, new, weights, proj, sk_near, rot_near, sems):
+def output_kernel(where, mine, other, table, away, new, weights, proj, kept, new_near, sems):
     rank = proj.shape[0]
-    halves = sk.shape[1]
+    halves = new.shape[1]
     width = rank // halves
-    copies = [
-        pltpu.make_async_copy(rot, rot_near, sems.at[0]),
-        pltpu.make_async_copy(sk, sk_near, sems.at[1]),
-    ]
-    for copy in copies:
-        copy.start()
+    fetch = pltpu.make_async_copy(away.at[:, : kept.shape[1]], kept, sems.at[2])
+    fetch.start()
     first = pl.ds(pl.multiple_of(where[0] * width, width), width)
     second = pl.ds(pl.multiple_of((1 - where[0]) * width, width), width)
     for j in range(mine.shape[1]):
@@ -289,7 +309,7 @@
     p = split(proj[...])
     left = jnp.concatenate(p, axis=1)
     right = jnp.concatenate([table[...]] * 2, axis=0)
-    gram = jnp.concatenate([dot(rows, right) for rows in halves_of(left)], axis=0)
+    gram = jnp.concatenate([dot(part, right) for part in halves_of(left)], axis=0)
     inverse = newton(gram / (frobenius(gram) + 1e-6), None)
     inv = split(inverse)
     coeff = split(mul3(inv, p))
@@ -299,38 +319,54 @@
     scale = jnp.sqrt(shift)
     mixing = scale * mul3(inv, root)
     turned = split(scale * mul3(root, inv))
-    own = split(jnp.where(where[0] == 0, mixing[:, :width], mixing[:, width:]))
-    copies[1].wait()
+    high, low = split(jnp.where(where[0] == 0, mixing[:, :width], mixing[:, width:]))
+    right = jnp.concatenate(
+        [
+            jnp.concatenate([high, low], axis=1),
+            jnp.concatenate([high, jnp.zeros_like(high)], axis=1),
+        ],
+        axis=0,
+    )
+    fetch.wait()
+    leave = []
     for c in range(halves):
-        value = mul3((sk_near[0, c], sk_near[1, c]), own)
-        new[:, c] = value.reshape(new.shape[0], new.shape[2], width)
-    copies[0].wait()
-    turn = mul3(turned, (rot_near[0], rot_near[1]))
-    weights[...] = jnp.sum(turn * turn, axis=0, keepdims=True) / rank
-
-
-def outputs(where, mine, other, table, sk, rot, lows):
-    halves, rows, rank = sk.shape[1:]
+        left = jnp.concatenate([kept[0, c], kept[1, c]], axis=1)
+        both = jnp.concatenate([dot(part, right) for part in halves_of(left)], axis=0)
+        value = both[:, :width] + both[:, width:]
+        new_near[c] = value.reshape(new_near.shape[1:])
+        leave.append(pltpu.make_async_copy(new_near.at[c], new.at[:, c], sems.at[c]))
+        leave[c].start()
+    for q in range(kept.shape[2] // rank):
+        rows = slice(q * rank, (q + 1) * rank)
+        turn = mul3(turned, (kept[0, 2, rows], kept[1, 2, rows]))
+        weights[:, rows] = jnp.sum(turn * turn, axis=0, keepdims=True) / rank
+    for copy in leave:
+        copy.wait()
+
+
+def outputs(where, mine, other, table, kept, lows):
+    rows, rank = kept.shape[2:]
+    width = rank // 2
+    smem = pl.BlockSpec(memory_space=pltpu.SMEM)
     vmem = pl.BlockSpec(memory_space=pltpu.VMEM)
-    smem = pl.BlockSpec(memory_space=pltpu.SMEM)
-    away = pl.BlockSpec(memory_space=pltpu.HBM)
+    away = pl.BlockSpec(memory_space=pl.ANY)
     return pl.pallas_call(
         output_kernel,
         out_shape=(
-            jax.ShapeDtypeStruct((rows // lows, halves, lows, rank // halves), F32),
+            jax.ShapeDtypeStruct((rows // lows, 2, lows, width), F32),
             jax.ShapeDtypeStruct((1, rows), F32),
         ),
-        in_specs=[smem] + [vmem] * 3 + [away] * 2,
-        out_specs=(vmem, vmem),
+        in_specs=[smem] + [vmem] * 3 + [away],
+        out_specs=(away, vmem),
         scratch_shapes=[
             pltpu.VMEM((rank, table.shape[0]), F32),
-            pltpu.VMEM(sk.shape, BF16),
-            pltpu.VMEM(rot.shape, BF16),
-            pltpu.SemaphoreType.DMA((2,)),
+            pltpu.VMEM((2, 3, rows, rank), BF16),
+            pltpu.VMEM((2, rows // lows, lows, width), F32),
+            pltpu.SemaphoreType.DMA((3,)),
         ],
-        compiler_params=params(20),
+        compiler_params=params(48),
         name="outputs",
-    )(where, mine, other, table, sk, rot)
+    )(where, mine, other, table, kept)
 
 
 def sketch_table(sketch_perm, rank):
@@ -359,7 +395,7 @@
     total, other = sum_wide(part, swap(sketch))
     turned = rotate_sketch(where, basis_index, sketch, other, bases)
     total, turned = lax.optimization_barrier((total, turned))
-    new, weights = outputs(where, total, swap(total), table, *turned, moved.shape[2])
+    new, weights = outputs(where, total, swap(total), table, turned, moved.shape[2])
     return new.reshape(rows, width), weights
 
 

time: 120 us -> 117 us (0.975)
  local copies, waits for them, and re-layouts: 8.57 us -> 1.32 us
  Pallas kernels: 20.7 us -> 24.5 us
  other arithmetic: 0.44 us -> 1.82 us
    unnamed x28 -> x8, local copies, waits for them, and re-layouts: 8.57 us -> 1.32 us
    pallas_call x1, Pallas kernels: 1.94 us -> 4.93 us  [rotate_sketch(): pl.pallas_call(rotate_kernel, out_shape=jax.ShapeDtypeStruct((2, PADDED,...]
    all_to_all x1, waiting for transfers between devices: 30.7 us -> 29.3 us  [per_device(): lax.all_to_all(gated, ('wide', 'cols'), split_axis=0, concat_axis=0, tile...]
  transfers between devices with their start and end apart: 5 -> 5, of which waited for: 4 -> 4; matrix products, arithmetic and copies ran while one was open for 0% -> 1% of each run, Pallas kernels for 2% -> 4%
where the time goes in v5:
time: 117 us
  waiting for transfers between devices  36.4 us (31%)
  blocking collectives  26.9 us (23%)
  starting transfers between devices  24.7 us (21%)
  Pallas kernels  24.5 us (21%)
  other arithmetic  1.82 us (2%)
  local copies, waits for them, and re-layouts  1.32 us (1%)
    all_to_all x1, waiting for transfers between devices, per_device(): lax.all_to_all(gated, ('wide', 'cols'), split_axis=0, concat_axis=0, tile...  29.3 us
    all_to_all x2, blocking collectives, exchange(): lax.all_to_all(pieces, 'wide', split_axis=0, concat_axis=0, axis_index_gr...  26.9 us
    all_to_all x1, starting transfers between devices, per_device(): lax.all_to_all(gated, ('wide', 'cols'), split_axis=0, concat_axis=0, tile...  15.7 us
    pallas_call x1, Pallas kernels, outputs(): pl.pallas_call(output_kernel, out_shape=(jax.ShapeDtypeStruct((rows // lo...  11.3 us
    ppermute x3, starting transfers between devices, swap(): return lax.ppermute(value, 'cols', [(0, 1), (1, 0)])  5.26 us
    pallas_call x1, Pallas kernels, rotate_sketch(): pl.pallas_call(rotate_kernel, out_shape=jax.ShapeDtypeStruct((2, PADDED,...  4.93 us
    all_to_all x1, waiting for transfers between devices, exchange(): lax.all_to_all(pieces, 'wide', split_axis=0, concat_axis=0, axis_index_gr...  4.03 us
    pallas_call x1, Pallas kernels, stack_products(): pl.pallas_call(stack_kernel, out_shape=(jax.ShapeDtypeStruct((count, lows...  3.8 us
  transfers between devices with their start and end apart: 5, of which 4 were waited for; matrix products, arithmetic and copies ran while one was open for 1% of the time, Pallas kernels for 4%

profile of v5, /device:TPU:1, one launch (start us, length us, event | category | flops | bytes accessed | tf_op | source)
XLA Modules:
  0.0 116.6 jit_solution(10026059391790923078)
XLA Ops:
  0.6 3.5 %gates.1 = f32[2048,128]{1,0:T(8,128)} custom-call(s32[16]{0:T(128)} %refs_0_.1, f32[8,128,128]{2,1,0:T(8,128)} %refs_1_.1, f32[2048,128]{1,0:T(8,128)} %refs_2_.1), custom_call_target="tpu_custom_call" | custom-call | tf_op jit(solution)/shard_map/gates/pallas_call | solution.py:80
  4.2 15.7 %all-to-all-start = ((f32[256,8,128]{2,1,0:T(8,128)}), f32[256,8,128]{2,1,0:T(8,128)S(1)}, u32[]{:S(2)}, u32[]{:S(2)}) async-start(f32[256,8,128]{2,1,0:T(8,128)} %bitcast.5), calls=%async_computation | async-start | bytes 2097152 | tf_op jit(solution)/shard_map/all_to_all | solution.py:389
  19.8 0.7 fusion.3
  20.6 0.7 add_select_fusion.2
  21.2 0.3 select_convert_fusion.table
  21.6 29.3 %all-to-all-done = f32[256,8,128]{2,1,0:T(8,128)S(1)} async-done(((f32[256,8,128]{2,1,0:T(8,128)}), f32[256,8,128]{2,1,0:T(8,128)S(1)}, u32[]{:S(2)}, u32[]{:S(2)}) %all-to-all-start) | async-done | bytes 1048608 | tf_op jit(solution)/shard_map/all_to_all | solution.py:389
  50.9 0.0 copy-start.1
  50.9 0.7 copy-done.1
  51.6 0.0 copy-start.2
  51.6 0.7 copy-done.2
  52.2 3.8 %stack.1 = (f32[128,8,256]{2,1,0:T(8,128)S(1)}, f32[16,8,8,128]{3,2,1,0:T(8,128)S(1)}, f32[16,8,8,128]{3,2,1,0:T(8,128)S(1)}) custom-call(s32[1]{0:T(128)} %bitcast.where, s32[3]{0:T(128)S(1)} %copy-done.1, f32[3]{0:T(128)S(1)} %copy-done.2, f32[128,2,8,128]{3,2,1,0:T(8,128)S(1)} %bitcast.4, bf16[1024,256]{1,0:T(8,128)(2,1)S(1)} %select_convert_fusion.table), custom_call_target="tpu_custom_call" | custom-call | tf_op jit(solution)/shard_map/stack/pallas_call | solution.py:144
  56.1 0.0 copy-start
  56.1 0.8 collective-permute-start
  56.8 1.5 %collective-permute-done = f32[16,8,8,128]{3,2,1,0:T(8,128)S(1)} collective-permute-done((f32[16,8,8,128]{3,2,1,0:T(8,128)S(1)}, f32[16,8,8,128]{3,2,1,0:T(8,128)S(1)}, u32[]{:S(2)}, u32[]{:S(2)}) %collective-permute-start) | collective-permute-done | bytes 524320 | tf_op jit(solution)/shard_map/ppermute | solution.py:380
  58.4 0.1 add.16
  58.4 0.5 collective-permute-start.1
  58.9 14.6 %all_to_all.20.parts = f32[16,8,8,128]{3,2,1,0:T(8,128)S(1)} all-to-all(f32[16,8,8,128]{3,2,1,0:T(8,128)S(1)} %add.16), channel_id=1, replica_groups={{0,2,4,6,64,66,68,70,128,130,132,134,192,194,196,198},{8,10,12,14,72,74..., dimensions={0} | all-to-all | bytes 1048576 | tf_op jit(solution)/shard_map/all_to_all | solution.py:184
  73.5 0.0 collective-permute-done.1.other_away
  73.5 0.0 copy-start.3
  73.5 12.3 %all_to_all.21.parts = f32[8,8,8,128]{3,2,1,0:T(8,128)S(1)} all-to-all(f32[8,8,8,128]{3,2,1,0:T(8,128)S(1)} %spread.2), channel_id=1, replica_groups={{0,8,16,24,32,40,48,56},{2,10,18,26,34,42,50,58},{4,12,20,28,36,44,52,6..., dimensions={0} | all-to-all | bytes 524288 | tf_op jit(solution)/shard_map/all_to_all | solution.py:184
  85.8 0.9 spread.3
  86.7 3.8 %all-to-all-start.3 = ((f32[16,8,8,128]{3,2,1,0:T(8,128)}), f32[16,8,8,128]{3,2,1,0:T(8,128)S(1)}, u32[]{:S(2)}, u32[]{:S(2)}) async-start(f32[16,8,8,128]{3,2,1,0:T(8,128)} %spread.3), calls=%async_computation.3 | async-start | bytes 1048576 | tf_op jit(solution)/shard_map/all_to_all | solution.py:184
  90.5 0.0 copy-done
  90.5 0.0 copy-done.3
  90.5 4.9 %rotate.1.away = bf16[2,16,1024,256]{3,2,1,0:T(8,128)(2,1)} custom-call(s32[1]{0:T(128)} %bitcast.where, s32[1,32]{1,0:T(1,128)} %index.1, f32[128,8,256]{2,1,0:T(8,128)} %copy-done, f32[128,8,256]{2,1,0:T(8,128)} %copy-done.3, f32[8,64,64]{2,1,0:T(8,128)} %mats_away.1), custom_call_target="tpu_custom_call" | custom-call | tf_op jit(solution)/shard_map/rotate/pallas_call | solution.py:251
  95.5 4.0 %all-to-all-done.3.mine = f32[16,8,8,128]{3,2,1,0:T(8,128)S(1)} async-done(((f32[16,8,8,128]{3,2,1,0:T(8,128)}), f32[16,8,8,128]{3,2,1,0:T(8,128)S(1)}, u32[]{:S(2)}, u32[]{:S(2)}) %all-to-all-start.3) | async-done | bytes 524320 | tf_op jit(solution)/shard_map/all_to_all | solution.py:184
  99.5 4.0 %collective-permute-start.2 = (f32[16,8,8,128]{3,2,1,0:T(8,128)S(1)}, f32[16,8,8,128]{3,2,1,0:T(8,128)S(1)}, u32[]{:S(2)}, u32[]{:S(2)}) collective-permute-start(f32[16,8,8,128]{3,2,1,0:T(8,128)S(1)} %all-to-all-done.3.mine), channel_id=1, source_target_pairs={{0,1},{1,0},{2,3},{3,2},{4,5},{5,4},{6,7},{7,6},{8,9},{9,8},{10,11... | collective-permute-start | bytes 1572872 | tf_op jit(solution)/shard_map/ppermute | solution.py:380
  103.5 1.5 %collective-permute-done.2.other = f32[16,8,8,128]{3,2,1,0:T(8,128)S(1)} collective-permute-done((f32[16,8,8,128]{3,2,1,0:T(8,128)S(1)}, f32[16,8,8,128]{3,2,1,0:T(8,128)S(1)}, u32[]{:S(2)}, u32[]{:S(2)}) %collective-permute-start.2) | collective-permute-done | bytes 524320 | tf_op jit(solution)/shard_map/ppermute | solution.py:380
  105.1 11.3 %outputs.1 = (f32[128,2,8,128]{3,2,1,0:T(8,128)}, f32[1,1024]{1,0:T(1,128)}) custom-call(s32[1]{0:T(128)} %bitcast.where, f32[16,8,8,128]{3,2,1,0:T(8,128)S(1)} %all-to-all-done.3.mine, f32[16,8,8,128]{3,2,1,0:T(8,128)S(1)} %collective-permute-done.2.other, bf16[1024,256]{1,0:T(8,128)(2,1)S(1)} %select_convert_fusion.table, ...), custom_call_target="tpu_custom_call" | custom-call | tf_op jit(solution)/shard_map/outputs/pallas_call | solution.py:353
  (1 shorter events, 0.0 us)
Async XLA Ops:
  4.2 46.8 %all-to-all-start = ((f32[256,8,128]{2,1,0:T(8,128)}), f32[256,8,128]{2,1,0:T(8,128)S(1)}, u32[]{:S(2)}, u32[]{:S(2)}) async-start(f32[256,8,128]{2,1,0:T(8,128)} %bitcast.5), calls=%async_computation | async-start | bytes 2097152 | tf_op jit(solution)/shard_map/all_to_all | solution.py:389
  50.9 0.7 copy-start.1
  51.6 0.7 copy-start.2
  56.1 34.4 %copy-start = (f32[128,8,256]{2,1,0:T(8,128)}, f32[128,8,256]{2,1,0:T(8,128)S(1)}, u32[]{:S(2)}) copy-start(f32[128,8,256]{2,1,0:T(8,128)S(1)} %get-tuple-element.17.own_away) | copy-start | bytes 3145732
  56.1 2.3 %collective-permute-start = (f32[16,8,8,128]{3,2,1,0:T(8,128)S(1)}, f32[16,8,8,128]{3,2,1,0:T(8,128)S(1)}, u32[]{:S(2)}, u32[]{:S(2)}) collective-permute-start(f32[16,8,8,128]{3,2,1,0:T(8,128)S(1)} %get-tuple-element.14), channel_id=1, source_target_pairs={{0,1},{1,0},{2,3},{3,2},{4,5},{5,4},{6,7},{7,6},{8,9},{9,8},{10,11... | collective-permute-start | bytes 1572872 | tf_op jit(solution)/shard_map/ppermute | solution.py:380
  58.4 15.0 %collective-permute-start.1 = (f32[128,8,256]{2,1,0:T(8,128)S(1)}, f32[128,8,256]{2,1,0:T(8,128)S(1)}, u32[]{:S(2)}, u32[]{:S(2)}) collective-permute-start(f32[128,8,256]{2,1,0:T(8,128)S(1)} %get-tuple-element.17.own_away), channel_id=1, source_target_pairs={{0,1},{1,0},{2,3},{3,2},{4,5},{5,4},{6,7},{7,6},{8,9},{9,8},{10,11... | collective-permute-start | bytes 3145736 | tf_op jit(solution)/shard_map/ppermute | solution.py:380
  73.5 17.0 %copy-start.3 = (f32[128,8,256]{2,1,0:T(8,128)}, f32[128,8,256]{2,1,0:T(8,128)S(1)}, u32[]{:S(2)}) copy-start(f32[128,8,256]{2,1,0:T(8,128)S(1)} %collective-permute-done.1.other_away) | copy-start | bytes 3145732
  86.7 12.8 %all-to-all-start.3 = ((f32[16,8,8,128]{3,2,1,0:T(8,128)}), f32[16,8,8,128]{3,2,1,0:T(8,128)S(1)}, u32[]{:S(2)}, u32[]{:S(2)}) async-start(f32[16,8,8,128]{3,2,1,0:T(8,128)} %spread.3), calls=%async_computation.3 | async-start | bytes 1048576 | tf_op jit(solution)/shard_map/all_to_all | solution.py:184
  99.5 5.6 %collective-permute-start.2 = (f32[16,8,8,128]{3,2,1,0:T(8,128)S(1)}, f32[16,8,8,128]{3,2,1,0:T(8,128)S(1)}, u32[]{:S(2)}, u32[]{:S(2)}) collective-permute-start(f32[16,8,8,128]{3,2,1,0:T(8,128)S(1)} %all-to-all-done.3.mine), channel_id=1, source_target_pairs={{0,1},{1,0},{2,3},{3,2},{4,5},{5,4},{6,7},{7,6},{8,9},{9,8},{10,11... | collective-permute-start | bytes 1572872 | tf_op jit(solution)/shard_map/ppermute | solution.py:380

commit v6 on v5

--- a/solution.py
+++ b/solution.py
@@ -93,20 +93,13 @@
     )(layout, gates, factor)
 
 
-def stack_kernel(where, masks, rates, moved, table, sketch, keep, send, high, low):
+def stack_kernel(where, flips, coefs, moved, table, sketch, keep, send, high, low):
     count, halves, lows, width = moved.shape
     rank = halves * width
-    jumps = masks.shape[0]
-    total = rates[0]
-    for k in range(1, jumps):
-        total = total + rates[k]
-    coefs = [jnp.full((2 * lows, width), 1.0 - 0.5 * total, F32)]
-    for k in range(jumps):
-        coefs.append(jnp.sqrt(jnp.full((2 * lows, width), rates[k], F32)))
-
     value = [jnp.zeros((count * lows // 2, rank), F32)] * 2
-    for k in range(jumps + 1):
-        flip = 0 if k == 0 else masks[k - 1]
+    terms = flips.shape[0]
+    for k in range(terms):
+        flip = flips[k]
         cols = slice(k * rank, (k + 1) * rank)
         for p in range(count // 2):
             first, second = (2 * p) ^ flip, (2 * p + 1) ^ flip
@@ -123,7 +116,7 @@
     left = split(value.T)
     mine = where[0] == 0
     half = rank // 2
-    for k in range(jumps + 1):
+    for k in range(terms):
         cols = slice(k * rank, (k + 1) * rank)
         part = mul3(left, (high[:, cols], low[:, cols]))
         for j in range(rank // 128):
@@ -134,7 +127,7 @@
             send[:, k * (rank // 128) + j] = jnp.where(mine, bottom, top)
 
 
-def stack_products(where, masks, rates, moved, table):
+def stack_products(where, flips, coefs, moved, table):
     count, halves, lows, width = moved.shape
     rank = halves * width
     columns = table.shape[0]
@@ -149,7 +142,7 @@
         scratch_shapes=[pltpu.VMEM((count * lows, columns), BF16)] * 2,
         compiler_params=params(20),
         name="stack",
-    )(where, masks, rates, moved, table)
+    )(where, flips, coefs, moved, table)
 
 
 SIDES = (4, 8, 4)
@@ -389,7 +382,9 @@
     moved = lax.all_to_all(gated, ("wide", "cols"), split_axis=0, concat_axis=0, tiled=True)
     moved = moved.reshape(count, 2, -1, width)
     table = sketch_table(sketch_perm, rank)
-    sketch, keep, send = stack_products(where, jump_masks, jump_rates, moved, table)
+    flips = jnp.concatenate([jnp.zeros((1,), jnp.int32), jump_masks])
+    coefs = jnp.concatenate([1.0 - 0.5 * jnp.sum(jump_rates, keepdims=True), jnp.sqrt(jump_rates)])
+    sketch, keep, send = stack_products(where, flips, coefs, moved, table)
     part = keep + swap(send)
     part, sketch = lax.optimization_barrier((part, sketch))
     total, other = sum_wide(part, swap(sketch))

time: 117 us -> 116 us (level)
  waiting for transfers between devices: 36.4 us -> 33.7 us
  other arithmetic: 1.82 us -> 3.86 us
  local copies, waits for them, and re-layouts: 1.32 us -> 0.01 us
    all_to_all x1, waiting for transfers between devices: 29.3 us -> 26.6 us  [per_device(): lax.all_to_all(gated, ('wide', 'cols'), split_axis=0, concat_axis=0, tile...]
    unnamed x8 -> x2, local copies, waits for them, and re-layouts: 1.32 us -> 0.01 us
    reduce_sum x0 -> x1, other arithmetic: none -> 1.26 us  [per_device(): jnp.sum(jump_rates, keepdims=True)]
  transfers between devices with their start and end apart: 5 -> 5, of which waited for: 4 -> 4; matrix products, arithmetic and copies ran while one was open for 1% -> 3% of each run, Pallas kernels for 4% -> 4%
where the time goes in v6:
time: 116 us; the launch traced here: 115 us
  waiting for transfers between devices  33.7 us (29%)
  blocking collectives  26.9 us (23%)
  starting transfers between devices  24.7 us (21%)
  Pallas kernels  24.5 us (21%)
  other arithmetic  3.86 us (3%)
  between operations  1.53 us (1%)
    all_to_all x2, blocking collectives, exchange(): lax.all_to_all(pieces, 'wide', split_axis=0, concat_axis=0, axis_index_gr...  26.9 us
    all_to_all x1, waiting for transfers between devices, per_device(): lax.all_to_all(gated, ('wide', 'cols'), split_axis=0, concat_axis=0, tile...  26.6 us
    all_to_all x1, starting transfers between devices, per_device(): lax.all_to_all(gated, ('wide', 'cols'), split_axis=0, concat_axis=0, tile...  15.7 us
    pallas_call x1, Pallas kernels, outputs(): pl.pallas_call(output_kernel, out_shape=(jax.ShapeDtypeStruct((rows // lo...  11.3 us
    ppermute x3, starting transfers between devices, swap(): return lax.ppermute(value, 'cols', [(0, 1), (1, 0)])  5.24 us
    pallas_call x1, Pallas kernels, rotate_sketch(): pl.pallas_call(rotate_kernel, out_shape=jax.ShapeDtypeStruct((2, PADDED,...  4.93 us
    all_to_all x1, waiting for transfers between devices, exchange(): lax.all_to_all(pieces, 'wide', split_axis=0, concat_axis=0, axis_index_gr...  4.04 us
    pallas_call x1, Pallas kernels, stack_products(): pl.pallas_call(stack_kernel, out_shape=(jax.ShapeDtypeStruct((count, lows...  3.82 us
  transfers between devices with their start and end apart: 5, of which 4 were waited for; matrix products, arithmetic and copies ran while one was open for 3% of the time, Pallas kernels for 4%

profile of v6, /device:TPU:1, one launch (start us, length us, event | category | flops | bytes accessed | tf_op | source)
XLA Modules:
  0.0 115.2 jit_solution(10724289151545337427)
XLA Ops:
  0.6 3.5 %gates.1 = f32[2048,128]{1,0:T(8,128)} custom-call(s32[16]{0:T(128)} %refs_0_.1, f32[8,128,128]{2,1,0:T(8,128)} %refs_1_.1, f32[2048,128]{1,0:T(8,128)} %refs_2_.1), custom_call_target="tpu_custom_call" | custom-call | tf_op jit(solution)/shard_map/gates/pallas_call | solution.py:80
  4.2 15.7 %all-to-all-start = ((f32[256,8,128]{2,1,0:T(8,128)}), f32[256,8,128]{2,1,0:T(8,128)S(1)}, u32[]{:S(2)}, u32[]{:S(2)}) async-start(f32[256,8,128]{2,1,0:T(8,128)} %bitcast.6), calls=%async_computation | async-start | bytes 2097152 | tf_op jit(solution)/shard_map/all_to_all | solution.py:382
  19.8 1.3 %fusion.6 = (f32[]{:T(128)}, f32[3]{0:T(128)S(1)}) fusion(f32[3]{0:T(128)} %param.12), kind=kLoop, calls=%fused_computation.19 | loop fusion | flops 2 | bytes 28 | tf_op jit(solution)/shard_map/reduce_sum | solution.py:386
  21.8 0.7 pad_add_fusion.flips
  22.5 0.1 pad_maximum_fusion.coefs
  22.6 0.7 fusion.3
  23.3 0.7 add_select_fusion.2
  24.0 0.3 select_convert_fusion.table
  24.3 26.6 %all-to-all-done = f32[256,8,128]{2,1,0:T(8,128)S(1)} async-done(((f32[256,8,128]{2,1,0:T(8,128)}), f32[256,8,128]{2,1,0:T(8,128)S(1)}, u32[]{:S(2)}, u32[]{:S(2)}) %all-to-all-start) | async-done | bytes 1048608 | tf_op jit(solution)/shard_map/all_to_all | solution.py:382
  50.9 3.8 %stack.1 = (f32[128,8,256]{2,1,0:T(8,128)S(1)}, f32[16,8,8,128]{3,2,1,0:T(8,128)S(1)}, f32[16,8,8,128]{3,2,1,0:T(8,128)S(1)}) custom-call(s32[1]{0:T(128)} %bitcast.where, s32[4]{0:T(128)S(1)} %pad_add_fusion.flips, f32[4]{0:T(128)S(1)} %pad_maximum_fusion.coefs, f32[128,2,8,128]{3,2,1,0:T(8,128)S(1)} %bitcast.5, bf16[1024,256]{1,0:T(8,128)(2,1)S(1)} %select_convert_fusion.table), custom_call_target="tpu_custom_call" | custom-call | tf_op jit(solution)/shard_map/stack/pallas_call | solution.py:137
  54.8 0.0 copy-start
  54.8 0.7 collective-permute-start
  55.5 1.5 %collective-permute-done = f32[16,8,8,128]{3,2,1,0:T(8,128)S(1)} collective-permute-done((f32[16,8,8,128]{3,2,1,0:T(8,128)S(1)}, f32[16,8,8,128]{3,2,1,0:T(8,128)S(1)}, u32[]{:S(2)}, u32[]{:S(2)}) %collective-permute-start) | collective-permute-done | bytes 524320 | tf_op jit(solution)/shard_map/ppermute | solution.py:373
  57.0 0.1 add.16
  57.1 0.5 collective-permute-start.1
  57.6 14.6 %all_to_all.20.parts = f32[16,8,8,128]{3,2,1,0:T(8,128)S(1)} all-to-all(f32[16,8,8,128]{3,2,1,0:T(8,128)S(1)} %add.16), channel_id=1, replica_groups={{0,2,4,6,64,66,68,70,128,130,132,134,192,194,196,198},{8,10,12,14,72,74..., dimensions={0} | all-to-all | bytes 1048576 | tf_op jit(solution)/shard_map/all_to_all | solution.py:177
  72.2 0.0 collective-permute-done.1.other_away
  72.2 12.3 %all_to_all.21.parts = f32[8,8,8,128]{3,2,1,0:T(8,128)S(1)} all-to-all(f32[8,8,8,128]{3,2,1,0:T(8,128)S(1)} %spread.2), channel_id=1, replica_groups={{0,8,16,24,32,40,48,56},{2,10,18,26,34,42,50,58},{4,12,20,28,36,44,52,6..., dimensions={0} | all-to-all | bytes 524288 | tf_op jit(solution)/shard_map/all_to_all | solution.py:177
  84.5 0.9 spread.3
  85.4 3.8 %all-to-all-start.3 = ((f32[16,8,8,128]{3,2,1,0:T(8,128)}), f32[16,8,8,128]{3,2,1,0:T(8,128)S(1)}, u32[]{:S(2)}, u32[]{:S(2)}) async-start(f32[16,8,8,128]{3,2,1,0:T(8,128)} %spread.3), calls=%async_computation.3 | async-start | bytes 1048576 | tf_op jit(solution)/shard_map/all_to_all | solution.py:177
  89.2 0.0 copy-done
  89.2 4.9 %rotate.1.away = bf16[2,16,1024,256]{3,2,1,0:T(8,128)(2,1)} custom-call(s32[1]{0:T(128)} %bitcast.where, s32[1,32]{1,0:T(1,128)} %index.1, f32[128,8,256]{2,1,0:T(8,128)} %copy-done, f32[128,8,256]{2,1,0:T(8,128)} %collective-permute-done.1.other_away, f32[8,64,64]{2,1,0:T(8,128)} %mats_away.1), custom_call_target="tpu_custom_call" | custom-call | tf_op jit(solution)/shard_map/rotate/pallas_call | solution.py:244
  94.1 4.0 %all-to-all-done.3.mine = f32[16,8,8,128]{3,2,1,0:T(8,128)S(1)} async-done(((f32[16,8,8,128]{3,2,1,0:T(8,128)}), f32[16,8,8,128]{3,2,1,0:T(8,128)S(1)}, u32[]{:S(2)}, u32[]{:S(2)}) %all-to-all-start.3) | async-done | bytes 524320 | tf_op jit(solution)/shard_map/all_to_all | solution.py:177
  98.2 4.0 %collective-permute-start.2 = (f32[16,8,8,128]{3,2,1,0:T(8,128)S(1)}, f32[16,8,8,128]{3,2,1,0:T(8,128)S(1)}, u32[]{:S(2)}, u32[]{:S(2)}) collective-permute-start(f32[16,8,8,128]{3,2,1,0:T(8,128)S(1)} %all-to-all-done.3.mine), channel_id=1, source_target_pairs={{0,1},{1,0},{2,3},{3,2},{4,5},{5,4},{6,7},{7,6},{8,9},{9,8},{10,11... | collective-permute-start | bytes 1572872 | tf_op jit(solution)/shard_map/ppermute | solution.py:373
  102.2 1.5 %collective-permute-done.2.other = f32[16,8,8,128]{3,2,1,0:T(8,128)S(1)} collective-permute-done((f32[16,8,8,128]{3,2,1,0:T(8,128)S(1)}, f32[16,8,8,128]{3,2,1,0:T(8,128)S(1)}, u32[]{:S(2)}, u32[]{:S(2)}) %collective-permute-start.2) | collective-permute-done | bytes 524320 | tf_op jit(solution)/shard_map/ppermute | solution.py:373
  103.7 11.3 %outputs.1 = (f32[128,2,8,128]{3,2,1,0:T(8,128)}, f32[1,1024]{1,0:T(1,128)}) custom-call(s32[1]{0:T(128)} %bitcast.where, f32[16,8,8,128]{3,2,1,0:T(8,128)S(1)} %all-to-all-done.3.mine, f32[16,8,8,128]{3,2,1,0:T(8,128)S(1)} %collective-permute-done.2.other, bf16[1024,256]{1,0:T(8,128)(2,1)S(1)} %select_convert_fusion.table, ...), custom_call_target="tpu_custom_call" | custom-call | tf_op jit(solution)/shard_map/outputs/pallas_call | solution.py:346
  (1 shorter events, 0.0 us)
Async XLA Ops:
  4.2 46.8 %all-to-all-start = ((f32[256,8,128]{2,1,0:T(8,128)}), f32[256,8,128]{2,1,0:T(8,128)S(1)}, u32[]{:S(2)}, u32[]{:S(2)}) async-start(f32[256,8,128]{2,1,0:T(8,128)} %bitcast.6), calls=%async_computation | async-start | bytes 2097152 | tf_op jit(solution)/shard_map/all_to_all | solution.py:382
  54.8 34.4 %copy-start = (f32[128,8,256]{2,1,0:T(8,128)}, f32[128,8,256]{2,1,0:T(8,128)S(1)}, u32[]{:S(2)}) copy-start(f32[128,8,256]{2,1,0:T(8,128)S(1)} %get-tuple-element.17.own_away) | copy-start | bytes 3145732
  54.8 2.3 %collective-permute-start = (f32[16,8,8,128]{3,2,1,0:T(8,128)S(1)}, f32[16,8,8,128]{3,2,1,0:T(8,128)S(1)}, u32[]{:S(2)}, u32[]{:S(2)}) collective-permute-start(f32[16,8,8,128]{3,2,1,0:T(8,128)S(1)} %get-tuple-element.14), channel_id=1, source_target_pairs={{0,1},{1,0},{2,3},{3,2},{4,5},{5,4},{6,7},{7,6},{8,9},{9,8},{10,11... | collective-permute-start | bytes 1572872 | tf_op jit(solution)/shard_map/ppermute | solution.py:373
  57.1 15.0 %collective-permute-start.1 = (f32[128,8,256]{2,1,0:T(8,128)S(1)}, f32[128,8,256]{2,1,0:T(8,128)}, u32[]{:S(2)}, u32[]{:S(2)}) collective-permute-start(f32[128,8,256]{2,1,0:T(8,128)S(1)} %get-tuple-element.17.own_away), channel_id=1, source_target_pairs={{0,1},{1,0},{2,3},{3,2},{4,5},{5,4},{6,7},{7,6},{8,9},{9,8},{10,11... | collective-permute-start | bytes 3145736 | tf_op jit(solution)/shard_map/ppermute | solution.py:373
  85.4 12.8 %all-to-all-start.3 = ((f32[16,8,8,128]{3,2,1,0:T(8,128)}), f32[16,8,8,128]{3,2,1,0:T(8,128)S(1)}, u32[]{:S(2)}, u32[]{:S(2)}) async-start(f32[16,8,8,128]{3,2,1,0:T(8,128)} %spread.3), calls=%async_computation.3 | async-start | bytes 1048576 | tf_op jit(solution)/shard_map/all_to_all | solution.py:177
  98.2 5.6 %collective-permute-start.2 = (f32[16,8,8,128]{3,2,1,0:T(8,128)S(1)}, f32[16,8,8,128]{3,2,1,0:T(8,128)S(1)}, u32[]{:S(2)}, u32[]{:S(2)}) collective-permute-start(f32[16,8,8,128]{3,2,1,0:T(8,128)S(1)} %all-to-all-done.3.mine), channel_id=1, source_target_pairs={{0,1},{1,0},{2,3},{3,2},{4,5},{5,4},{6,7},{7,6},{8,9},{9,8},{10,11... | collective-permute-start | bytes 1572872 | tf_op jit(solution)/shard_map/ppermute | solution.py:373

commit v7 on v6

--- a/solution.py
+++ b/solution.py
@@ -146,15 +146,17 @@
 
 
 SIDES = (4, 8, 4)
+DEPTH = 2
 
 
 def groups(count):
     ny, nz, nx = SIDES
     assert ny * nz * nx == count
     at = lambda y, z, x: (y * nz + z) * nx + x
-    planes = [[at(y, z, x) for y in range(ny) for x in range(nx)] for z in range(nz)]
-    lines = [[at(y, z, x) for z in range(nz)] for y in range(ny) for x in range(nx)]
-    return planes, lines
+    inside = [(y, d, x) for y in range(ny) for d in range(DEPTH) for x in range(nx)]
+    slabs = [[at(y, z + d, x) for y, d, x in inside] for z in range(0, nz, DEPTH)]
+    lines = [[at(y, z + d, x) for z in range(0, nz, DEPTH)] for y, d, x in inside]
+    return slabs, lines
 
 
 def spread_kernel(parts, out):
@@ -180,12 +182,14 @@
 
 
 def sum_wide(part, beside):
-    planes, lines = groups(lax.axis_size("wide"))
-    assert len(planes[0]) == part.shape[0]
-    pieces = exchange(part, planes)
+    slabs, lines = groups(lax.axis_size("wide"))
+    members = len(slabs[0])
+    tiles = part.shape[0] * part.shape[1] // members
+    pieces = exchange(part.reshape((members, tiles) + part.shape[2:]), slabs)
     pieces, beside = lax.optimization_barrier((pieces, beside))
     pieces = exchange(sum_and_spread(pieces, len(lines[0])), lines)
-    return exchange(sum_and_spread(pieces, len(planes[0])), planes), beside
+    total = exchange(sum_and_spread(pieces, members), slabs)
+    return total.reshape(part.shape), beside
 
 
 PADDED = 16

time: 116 us -> 114 us (0.983)
  blocking collectives: 26.9 us -> 23.9 us
    all_to_all x2, blocking collectives: 26.9 us -> 23.9 us  [exchange(): lax.all_to_all(pieces, 'wide', split_axis=0, concat_axis=0, axis_index_gr...]
    all_to_all x1, starting transfers between devices: 3.77 us -> 5.65 us  [exchange(): lax.all_to_all(pieces, 'wide', split_axis=0, concat_axis=0, axis_index_gr...]
where the time goes in v7:
time: 114 us
  waiting for transfers between devices  34.2 us (30%)
  starting transfers between devices  25.5 us (22%)
  Pallas kernels  24.5 us (21%)
  blocking collectives  23.9 us (21%)
  other arithmetic  3.86 us (3%)
  between operations  1.52 us (1%)
    all_to_all x1, waiting for transfers between devices, per_device(): lax.all_to_all(gated, ('wide', 'cols'), split_axis=0, concat_axis=0, tile...  26.6 us
    all_to_all x2, blocking collectives, exchange(): lax.all_to_all(pieces, 'wide', split_axis=0, concat_axis=0, axis_index_gr...  23.9 us
    all_to_all x1, starting transfers between devices, per_device(): lax.all_to_all(gated, ('wide', 'cols'), split_axis=0, concat_axis=0, tile...  15.7 us
    pallas_call x1, Pallas kernels, outputs(): pl.pallas_call(output_kernel, out_shape=(jax.ShapeDtypeStruct((rows // lo...  11.3 us
    all_to_all x1, starting transfers between devices, exchange(): lax.all_to_all(pieces, 'wide', split_axis=0, concat_axis=0, axis_index_gr...  5.65 us
    pallas_call x1, Pallas kernels, rotate_sketch(): pl.pallas_call(rotate_kernel, out_shape=jax.ShapeDtypeStruct((2, PADDED,...  4.93 us
    all_to_all x1, waiting for transfers between devices, exchange(): lax.all_to_all(pieces, 'wide', split_axis=0, concat_axis=0, axis_index_gr...  4.53 us
    ppermute x3, starting transfers between devices, swap(): return lax.ppermute(value, 'cols', [(0, 1), (1, 0)])  4.22 us
  transfers between devices with their start and end apart: 5, of which 4 were waited for; matrix products, arithmetic and copies ran while one was open for 3% of the time, Pallas kernels for 4%

profile of v7, /device:TPU:1, one launch (start us, length us, event | category | flops | bytes accessed | tf_op | source)
XLA Modules:
  0.0 113.6 jit_solution(9989731875220388053)
XLA Ops:
  0.6 3.5 %gates.1 = f32[2048,128]{1,0:T(8,128)} custom-call(s32[16]{0:T(128)} %refs_0_.1, f32[8,128,128]{2,1,0:T(8,128)} %refs_1_.1, f32[2048,128]{1,0:T(8,128)} %refs_2_.1), custom_call_target="tpu_custom_call" | custom-call | tf_op jit(solution)/shard_map/gates/pallas_call | solution.py:80
  4.2 15.7 %all-to-all-start = ((f32[256,8,128]{2,1,0:T(8,128)}), f32[256,8,128]{2,1,0:T(8,128)S(1)}, u32[]{:S(2)}, u32[]{:S(2)}) async-start(f32[256,8,128]{2,1,0:T(8,128)} %bitcast.10), calls=%async_computation | async-start | bytes 2097152 | tf_op jit(solution)/shard_map/all_to_all | solution.py:386
  19.8 1.3 %fusion.6 = (f32[]{:T(128)}, f32[3]{0:T(128)S(1)}) fusion(f32[3]{0:T(128)} %param.12), kind=kLoop, calls=%fused_computation.19 | loop fusion | flops 2 | bytes 28 | tf_op jit(solution)/shard_map/reduce_sum | solution.py:390
  21.8 0.7 pad_add_fusion.flips
  22.5 0.1 pad_maximum_fusion.coefs
  22.6 0.7 fusion.3
  23.3 0.7 add_select_fusion.2
  24.0 0.3 select_convert_fusion.table
  24.3 26.6 %all-to-all-done = f32[256,8,128]{2,1,0:T(8,128)S(1)} async-done(((f32[256,8,128]{2,1,0:T(8,128)}), f32[256,8,128]{2,1,0:T(8,128)S(1)}, u32[]{:S(2)}, u32[]{:S(2)}) %all-to-all-start) | async-done | bytes 1048608 | tf_op jit(solution)/shard_map/all_to_all | solution.py:386
  50.9 3.8 %stack.1 = (f32[128,8,256]{2,1,0:T(8,128)S(1)}, f32[16,8,8,128]{3,2,1,0:T(8,128)S(1)}, f32[16,8,8,128]{3,2,1,0:T(8,128)S(1)}) custom-call(s32[1]{0:T(128)} %bitcast.where, s32[4]{0:T(128)S(1)} %pad_add_fusion.flips, f32[4]{0:T(128)S(1)} %pad_maximum_fusion.coefs, f32[128,2,8,128]{3,2,1,0:T(8,128)S(1)} %bitcast.7, bf16[1024,256]{1,0:T(8,128)(2,1)S(1)} %select_convert_fusion.table), custom_call_target="tpu_custom_call" | custom-call | tf_op jit(solution)/shard_map/stack/pallas_call | solution.py:137
  54.8 0.0 copy-start
  54.8 0.8 collective-permute-start
  55.5 1.5 %collective-permute-done = f32[16,8,8,128]{3,2,1,0:T(8,128)S(1)} collective-permute-done((f32[16,8,8,128]{3,2,1,0:T(8,128)S(1)}, f32[16,8,8,128]{3,2,1,0:T(8,128)S(1)}, u32[]{:S(2)}, u32[]{:S(2)}) %collective-permute-start) | collective-permute-done | bytes 524320 | tf_op jit(solution)/shard_map/ppermute | solution.py:377
  57.1 0.1 add.16
  57.1 0.5 collective-permute-start.1
  57.6 14.7 %all_to_all.20.parts = f32[32,4,8,128]{3,2,1,0:T(8,128)S(1)} all-to-all(f32[32,4,8,128]{3,2,1,0:T(8,128)S(1)} %bitcast.11), channel_id=1, replica_groups={{0,2,4,6,8,10,12,14,64,66,68,70,72,74,76,78,128,130,132,134,136,138,140..., dimensions={0} | all-to-all | bytes 1048576 | tf_op jit(solution)/shard_map/all_to_all | solution.py:179
  72.3 0.0 collective-permute-done.1.other_away
  72.3 9.3 %all_to_all.21.parts = f32[4,4,8,128]{3,2,1,0:T(8,128)S(1)} all-to-all(f32[4,4,8,128]{3,2,1,0:T(8,128)S(1)} %spread.2), channel_id=1, replica_groups={{0,16,32,48},{2,18,34,50},{4,20,36,52},{6,22,38,54},{8,24,40,56},{10,26..., dimensions={0} | all-to-all | bytes 131072 | tf_op jit(solution)/shard_map/all_to_all | solution.py:179
  81.6 0.9 spread.3
  82.4 5.7 %all-to-all-start.3 = ((f32[32,4,8,128]{3,2,1,0:T(8,128)}), f32[32,4,8,128]{3,2,1,0:T(8,128)S(1)}, u32[]{:S(2)}, u32[]{:S(2)}) async-start(f32[32,4,8,128]{3,2,1,0:T(8,128)} %spread.3), calls=%async_computation.3 | async-start | bytes 1048576 | tf_op jit(solution)/shard_map/all_to_all | solution.py:179
  88.1 0.0 copy-done
  88.1 4.9 %rotate.1.away = bf16[2,16,1024,256]{3,2,1,0:T(8,128)(2,1)} custom-call(s32[1]{0:T(128)} %bitcast.where, s32[1,32]{1,0:T(1,128)} %index.1, f32[128,8,256]{2,1,0:T(8,128)} %copy-done, f32[128,8,256]{2,1,0:T(8,128)} %collective-permute-done.1.other_away, f32[8,64,64]{2,1,0:T(8,128)} %mats_away.1), custom_call_target="tpu_custom_call" | custom-call | tf_op jit(solution)/shard_map/rotate/pallas_call | solution.py:248
  93.0 4.5 %all-to-all-done.3 = f32[32,4,8,128]{3,2,1,0:T(8,128)S(1)} async-done(((f32[32,4,8,128]{3,2,1,0:T(8,128)}), f32[32,4,8,128]{3,2,1,0:T(8,128)S(1)}, u32[]{:S(2)}, u32[]{:S(2)}) %all-to-all-start.3) | async-done | bytes 524320 | tf_op jit(solution)/shard_map/all_to_all | solution.py:179
  97.6 3.0 %collective-permute-start.2 = (f32[16,8,8,128]{3,2,1,0:T(8,128)S(1)}, f32[16,8,8,128]{3,2,1,0:T(8,128)S(1)}, u32[]{:S(2)}, u32[]{:S(2)}) collective-permute-start(f32[16,8,8,128]{3,2,1,0:T(8,128)S(1)} %bitcast.8), channel_id=1, source_target_pairs={{0,1},{1,0},{2,3},{3,2},{4,5},{5,4},{6,7},{7,6},{8,9},{9,8},{10,11... | collective-permute-start | bytes 1572872 | tf_op jit(solution)/shard_map/ppermute | solution.py:377
  100.6 1.5 %collective-permute-done.2.other = f32[16,8,8,128]{3,2,1,0:T(8,128)S(1)} collective-permute-done((f32[16,8,8,128]{3,2,1,0:T(8,128)S(1)}, f32[16,8,8,128]{3,2,1,0:T(8,128)S(1)}, u32[]{:S(2)}, u32[]{:S(2)}) %collective-permute-start.2) | collective-permute-done | bytes 524320 | tf_op jit(solution)/shard_map/ppermute | solution.py:377
  102.1 11.3 %outputs.1 = (f32[128,2,8,128]{3,2,1,0:T(8,128)}, f32[1,1024]{1,0:T(1,128)}) custom-call(s32[1]{0:T(128)} %bitcast.where, f32[16,8,8,128]{3,2,1,0:T(8,128)S(1)} %bitcast.9, f32[16,8,8,128]{3,2,1,0:T(8,128)S(1)} %collective-permute-done.2.other, bf16[1024,256]{1,0:T(8,128)(2,1)S(1)} %select_convert_fusion.table, bf16[2,16,1024,256]{3,2,1,0:T(8,128)(2,1)} %rotate.1.away), custom_call_target="tpu_custom_call" | custom-call | tf_op jit(solution)/shard_map/outputs/pallas_call | solution.py:350
  (1 shorter events, 0.0 us)
Async XLA Ops:
  4.2 46.8 %all-to-all-start = ((f32[256,8,128]{2,1,0:T(8,128)}), f32[256,8,128]{2,1,0:T(8,128)S(1)}, u32[]{:S(2)}, u32[]{:S(2)}) async-start(f32[256,8,128]{2,1,0:T(8,128)} %bitcast.10), calls=%async_computation | async-start | bytes 2097152 | tf_op jit(solution)/shard_map/all_to_all | solution.py:386
  54.8 33.3 %copy-start = (f32[128,8,256]{2,1,0:T(8,128)}, f32[128,8,256]{2,1,0:T(8,128)S(1)}, u32[]{:S(2)}) copy-start(f32[128,8,256]{2,1,0:T(8,128)S(1)} %get-tuple-element.17.own_away) | copy-start | bytes 3145732
  54.8 2.3 %collective-permute-start = (f32[16,8,8,128]{3,2,1,0:T(8,128)S(1)}, f32[16,8,8,128]{3,2,1,0:T(8,128)S(1)}, u32[]{:S(2)}, u32[]{:S(2)}) collective-permute-start(f32[16,8,8,128]{3,2,1,0:T(8,128)S(1)} %get-tuple-element.14), channel_id=1, source_target_pairs={{0,1},{1,0},{2,3},{3,2},{4,5},{5,4},{6,7},{7,6},{8,9},{9,8},{10,11... | collective-permute-start | bytes 1572872 | tf_op jit(solution)/shard_map/ppermute | solution.py:377
  57.1 15.1 %collective-permute-start.1 = (f32[128,8,256]{2,1,0:T(8,128)S(1)}, f32[128,8,256]{2,1,0:T(8,128)}, u32[]{:S(2)}, u32[]{:S(2)}) collective-permute-start(f32[128,8,256]{2,1,0:T(8,128)S(1)} %get-tuple-element.17.own_away), channel_id=1, source_target_pairs={{0,1},{1,0},{2,3},{3,2},{4,5},{5,4},{6,7},{7,6},{8,9},{9,8},{10,11... | collective-permute-start | bytes 3145736 | tf_op jit(solution)/shard_map/ppermute | solution.py:377
  82.4 15.1 %all-to-all-start.3 = ((f32[32,4,8,128]{3,2,1,0:T(8,128)}), f32[32,4,8,128]{3,2,1,0:T(8,128)S(1)}, u32[]{:S(2)}, u32[]{:S(2)}) async-start(f32[32,4,8,128]{3,2,1,0:T(8,128)} %spread.3), calls=%async_computation.3 | async-start | bytes 1048576 | tf_op jit(solution)/shard_map/all_to_all | solution.py:179
  97.6 4.5 %collective-permute-start.2 = (f32[16,8,8,128]{3,2,1,0:T(8,128)S(1)}, f32[16,8,8,128]{3,2,1,0:T(8,128)S(1)}, u32[]{:S(2)}, u32[]{:S(2)}) collective-permute-start(f32[16,8,8,128]{3,2,1,0:T(8,128)S(1)} %bitcast.8), channel_id=1, source_target_pairs={{0,1},{1,0},{2,3},{3,2},{4,5},{5,4},{6,7},{7,6},{8,9},{9,8},{10,11... | collective-permute-start | bytes 1572872 | tf_op jit(solution)/shard_map/ppermute | solution.py:377

commit v8 on v7

--- a/solution.py
+++ b/solution.py
@@ -26,10 +26,24 @@
     return x[:half], x[half:]
 
 
-def mul3(a, b, dims=NN):
+def joined(a, b, dims=NN):
     left = jnp.concatenate([a[0], a[1], a[0]], axis=dims[0][0][0])
     right = jnp.concatenate([b[0], b[0], b[1]], axis=dims[0][1][0])
-    return jnp.concatenate([dot(rows, right, dims) for rows in halves_of(left)], axis=0)
+    return left, right
+
+
+def mul3(a, b, dims=NN):
+    return dot(*joined(a, b, dims), dims)
+
+
+def mul3_rows(a, b):
+    left, right = joined(a, b)
+    return jnp.concatenate([dot(rows, right) for rows in halves_of(left)], axis=0)
+
+
+def blocks_of(a, size):
+    cuts = range(0, a[0].shape[1], size)
+    return [tuple(part[:, i : i + size] for part in a) for i in cuts]
 
 
 WHOLE = 60
@@ -159,20 +173,27 @@
     return slabs, lines
 
 
-def spread_kernel(parts, out):
-    out[...] = jnp.broadcast_to(jnp.sum(parts[...], axis=0, keepdims=True), out.shape)
-
-
-def sum_and_spread(parts, copies):
+def sum_kernel(parts, out):
+    out[...] = jnp.sum(parts[...], axis=0)
+
+
+def spread_kernel(*refs):
+    total = refs[0][...]
+    for part in refs[1:-1]:
+        total = total + part[...]
+    refs[-1][...] = jnp.broadcast_to(total[None], refs[-1].shape)
+
+
+def local(kernel, shape, name, *args):
     vmem = pl.BlockSpec(memory_space=pltpu.VMEM)
     return pl.pallas_call(
-        spread_kernel,
-        out_shape=jax.ShapeDtypeStruct((copies,) + parts.shape[1:], F32),
-        in_specs=[vmem],
+        kernel,
+        out_shape=jax.ShapeDtypeStruct(shape, F32),
+        in_specs=[vmem] * len(args),
         out_specs=vmem,
         compiler_params=params(4),
-        name="spread",
-    )(parts)
+        name=name,
+    )(*args)
 
 
 def exchange(pieces, members):
@@ -187,8 +208,13 @@
     tiles = part.shape[0] * part.shape[1] // members
     pieces = exchange(part.reshape((members, tiles) + part.shape[2:]), slabs)
     pieces, beside = lax.optimization_barrier((pieces, beside))
-    pieces = exchange(sum_and_spread(pieces, len(lines[0])), lines)
-    total = exchange(sum_and_spread(pieces, members), slabs)
+    mine = local(sum_kernel, pieces.shape[1:], "sum", pieces)
+    terms = [mine]
+    for step in range(1, len(lines[0])):
+        pairs = [(at, line[(i + step) % len(line)]) for line in lines for i, at in enumerate(line)]
+        terms.append(lax.ppermute(mine, "wide", pairs))
+    copies = local(spread_kernel, pieces.shape, "spread", *terms)
+    total = exchange(copies, slabs)
     return total.reshape(part.shape), beside
 
 
@@ -228,7 +254,7 @@
             parts.append(jnp.where(mine, first, second))
             parts.append(jnp.where(mine, second, first))
         data = jnp.concatenate(parts, axis=0)
-        value = mul3(split(mats[index[0, core * blocks + b]]), split(data))
+        value = mul3_rows(split(mats[index[0, core * blocks + b]]), split(data))
         rotated[b * order : (b + 1) * order, :] = value
     for q in range(rotated.shape[0] // rank):
         rows = slice(q * rank, (q + 1) * rank)
@@ -280,14 +306,14 @@
         last = step == NS_ITERS - 1
         right = split(t)
         if step == 0:
-            once = 1.5 * t - 0.5 * mul3(right, right)
+            once = 1.5 * t - 0.5 * mul3_rows(right, right)
             held = 1.5 * eye(t.shape[0]) - 0.5 * t if value is None else once
         else:
             if not last:
-                once = 1.5 * t - 0.5 * mul3(right, right)
-            held = 1.5 * held - 0.5 * mul3(split(held), right)
+                once = 1.5 * t - 0.5 * mul3_rows(right, right)
+            held = 1.5 * held - 0.5 * mul3_rows(split(held), right)
         if not last:
-            t = 1.5 * once - 0.5 * mul3(split(once), right)
+            t = 1.5 * once - 0.5 * mul3_rows(split(once), right)
     return held
 
 
@@ -304,13 +330,17 @@
         proj[first, cols] = mine[:, j].reshape(width, 128)
         proj[second, cols] = other[:, j].reshape(width, 128)
     p = split(proj[...])
-    left = jnp.concatenate(p, axis=1)
-    right = jnp.concatenate([table[...]] * 2, axis=0)
-    gram = jnp.concatenate([dot(part, right) for part in halves_of(left)], axis=0)
+    gram = 0.0
+    for k, part in enumerate(blocks_of(p, rank)):
+        signs = table[k * rank : (k + 1) * rank]
+        left = jnp.concatenate(part, axis=1)
+        gram = gram + dot(left, jnp.concatenate([signs] * 2, axis=0))
     inverse = newton(gram / (frobenius(gram) + 1e-6), None)
     inv = split(inverse)
-    coeff = split(mul3(inv, p))
-    core = mul3(coeff, coeff, NT)
+    core = 0.0
+    for part in blocks_of(p, rank):
+        coeff = split(mul3(inv, part))
+        core = core + mul3(coeff, coeff, NT)
     shift = frobenius(core) + 1e-6
     root = split(newton(core / shift, "approx"))
     scale = jnp.sqrt(shift)

time: 114 us -> 114 us (level)
  blocking collectives: 23.9 us -> 14.7 us
  waiting for transfers between devices: 34.2 us -> 38.8 us
  starting transfers between devices: 25.5 us -> 29.9 us
    all_to_all x2 -> x1, blocking collectives: 23.9 us -> 14.7 us  [exchange(): lax.all_to_all(pieces, 'wide', split_axis=0, concat_axis=0, axis_index_gr...]
    ppermute x0 -> x3, waiting for transfers between devices: none -> 4.99 us  [sum_wide(): terms.append(lax.ppermute(mine, 'wide', pairs))]
    ppermute x0 -> x3, starting transfers between devices: none -> 4.29 us  [sum_wide(): terms.append(lax.ppermute(mine, 'wide', pairs))]
  transfers between devices with their start and end apart: 5 -> 8, of which waited for: 4 -> 6; matrix products, arithmetic and copies ran while one was open for 3% -> 3% of each run, Pallas kernels for 4% -> 4%
where the time goes in v8:
time: 114 us; the launch traced here: 113 us
  waiting for transfers between devices  38.8 us (34%)
  starting transfers between devices  29.9 us (26%)
  Pallas kernels  24.4 us (21%)
  blocking collectives  14.7 us (13%)
  other arithmetic  3.89 us (3%)
  between operations  1.53 us (1%)
    all_to_all x1, waiting for transfers between devices, per_device(): lax.all_to_all(gated, ('wide', 'cols'), split_axis=0, concat_axis=0, tile...  26.6 us
    all_to_all x1, starting transfers between devices, per_device(): lax.all_to_all(gated, ('wide', 'cols'), split_axis=0, concat_axis=0, tile...  15.7 us
    all_to_all x1, blocking collectives, exchange(): lax.all_to_all(pieces, 'wide', split_axis=0, concat_axis=0, axis_index_gr...  14.7 us
    pallas_call x1, Pallas kernels, outputs(): pl.pallas_call(output_kernel, out_shape=(jax.ShapeDtypeStruct((rows // lo...  11.3 us
    all_to_all x1, starting transfers between devices, exchange(): lax.all_to_all(pieces, 'wide', split_axis=0, concat_axis=0, axis_index_gr...  5.15 us
    ppermute x3, waiting for transfers between devices, sum_wide(): terms.append(lax.ppermute(mine, 'wide', pairs))  4.99 us
    pallas_call x1, Pallas kernels, rotate_sketch(): pl.pallas_call(rotate_kernel, out_shape=jax.ShapeDtypeStruct((2, PADDED,...  4.93 us
    ppermute x3, starting transfers between devices, swap(): return lax.ppermute(value, 'cols', [(0, 1), (1, 0)])  4.83 us
  transfers between devices with their start and end apart: 8, of which 6 were waited for; matrix products, arithmetic and copies ran while one was open for 3% of the time, Pallas kernels for 4%

profile of v8, /device:TPU:1, one launch (start us, length us, event | category | flops | bytes accessed | tf_op | source)
XLA Modules:
  0.0 113.2 jit_solution(16128051686806911749)
XLA Ops:
  0.6 3.5 %gates.1 = f32[2048,128]{1,0:T(8,128)} custom-call(s32[16]{0:T(128)} %refs_0_.1, f32[8,128,128]{2,1,0:T(8,128)} %refs_1_.1, f32[2048,128]{1,0:T(8,128)} %refs_2_.1), custom_call_target="tpu_custom_call" | custom-call | tf_op jit(solution)/shard_map/gates/pallas_call | solution.py:94
  4.2 15.7 %all-to-all-start = ((f32[256,8,128]{2,1,0:T(8,128)}), f32[256,8,128]{2,1,0:T(8,128)S(1)}, u32[]{:S(2)}, u32[]{:S(2)}) async-start(f32[256,8,128]{2,1,0:T(8,128)} %bitcast.10), calls=%async_computation | async-start | bytes 2097152 | tf_op jit(solution)/shard_map/all_to_all | solution.py:416
  19.8 1.3 %fusion.6 = (f32[]{:T(128)}, f32[3]{0:T(128)S(1)}) fusion(f32[3]{0:T(128)} %param.12), kind=kLoop, calls=%fused_computation.19 | loop fusion | flops 2 | bytes 28 | tf_op jit(solution)/shard_map/reduce_sum | solution.py:420
  21.8 0.7 pad_add_fusion.flips
  22.5 0.1 pad_maximum_fusion.coefs
  22.6 0.7 fusion.3
  23.3 0.7 add_select_fusion.2
  24.0 0.3 select_convert_fusion.table
  24.3 26.6 %all-to-all-done = f32[256,8,128]{2,1,0:T(8,128)S(1)} async-done(((f32[256,8,128]{2,1,0:T(8,128)}), f32[256,8,128]{2,1,0:T(8,128)S(1)}, u32[]{:S(2)}, u32[]{:S(2)}) %all-to-all-start) | async-done | bytes 1048608 | tf_op jit(solution)/shard_map/all_to_all | solution.py:416
  50.9 3.7 %stack.1 = (f32[128,8,256]{2,1,0:T(8,128)S(1)}, f32[16,8,8,128]{3,2,1,0:T(8,128)S(1)}, f32[16,8,8,128]{3,2,1,0:T(8,128)S(1)}) custom-call(s32[1]{0:T(128)} %bitcast.where, s32[4]{0:T(128)S(1)} %pad_add_fusion.flips, f32[4]{0:T(128)S(1)} %pad_maximum_fusion.coefs, f32[128,2,8,128]{3,2,1,0:T(8,128)S(1)} %bitcast.7, bf16[1024,256]{1,0:T(8,128)(2,1)S(1)} %select_convert_fusion.table), custom_call_target="tpu_custom_call" | custom-call | tf_op jit(solution)/shard_map/stack/pallas_call | solution.py:151
  54.6 0.0 copy-start
  54.6 0.7 collective-permute-start
  55.4 1.5 %collective-permute-done = f32[16,8,8,128]{3,2,1,0:T(8,128)S(1)} collective-permute-done((f32[16,8,8,128]{3,2,1,0:T(8,128)S(1)}, f32[16,8,8,128]{3,2,1,0:T(8,128)S(1)}, u32[]{:S(2)}, u32[]{:S(2)}) %collective-permute-start) | collective-permute-done | bytes 524320 | tf_op jit(solution)/shard_map/ppermute | solution.py:407
  56.9 0.1 add.16
  57.0 0.5 collective-permute-start.1
  57.5 14.7 %all_to_all.15.parts = f32[32,4,8,128]{3,2,1,0:T(8,128)S(1)} all-to-all(f32[32,4,8,128]{3,2,1,0:T(8,128)S(1)} %bitcast.11), channel_id=1, replica_groups={{0,2,4,6,8,10,12,14,64,66,68,70,72,74,76,78,128,130,132,134,136,138,140..., dimensions={0} | all-to-all | bytes 1048576 | tf_op jit(solution)/shard_map/all_to_all | solution.py:200
  72.1 0.0 collective-permute-done.1.other_away
  72.1 0.0 copy-start.1
  72.2 0.5 collective-permute-start.4
  72.7 3.8 %collective-permute-start.3 = (f32[4,8,128]{2,1,0:T(8,128)S(1)}, f32[4,8,128]{2,1,0:T(8,128)S(1)}, u32[]{:S(2)}, u32[]{:S(2)}) collective-permute-start(f32[4,8,128]{2,1,0:T(8,128)S(1)} %sum.1.refs_0_), channel_id=1, source_target_pairs={{0,32},{16,48},{32,0},{48,16},{2,34},{18,50},{34,2},{50,18},{4,36}... | collective-permute-start | bytes 49160 | tf_op jit(solution)/shard_map/ppermute | solution.py:215
  76.5 0.0 collective-permute-start.2
  76.5 0.0 collective-permute-done.4.refs_3_
  76.5 2.7 %collective-permute-done.3.refs_2_ = f32[4,8,128]{2,1,0:T(8,128)S(1)} collective-permute-done((f32[4,8,128]{2,1,0:T(8,128)S(1)}, f32[4,8,128]{2,1,0:T(8,128)S(1)}, u32[]{:S(2)}, u32[]{:S(2)}) %collective-permute-start.3) | collective-permute-done | bytes 16416 | tf_op jit(solution)/shard_map/ppermute | solution.py:215
  79.2 2.2 %collective-permute-done.2.refs_1_ = f32[4,8,128]{2,1,0:T(8,128)S(1)} collective-permute-done((f32[4,8,128]{2,1,0:T(8,128)S(1)}, f32[4,8,128]{2,1,0:T(8,128)S(1)}, u32[]{:S(2)}, u32[]{:S(2)}) %collective-permute-start.2) | collective-permute-done | bytes 16416 | tf_op jit(solution)/shard_map/ppermute | solution.py:215
  81.5 0.9 spread.1
  82.3 5.1 %all-to-all-start.2 = ((f32[32,4,8,128]{3,2,1,0:T(8,128)}), f32[32,4,8,128]{3,2,1,0:T(8,128)S(1)}, u32[]{:S(2)}, u32[]{:S(2)}) async-start(f32[32,4,8,128]{3,2,1,0:T(8,128)} %spread.1), calls=%async_computation.2 | async-start | bytes 1048576 | tf_op jit(solution)/shard_map/all_to_all | solution.py:200
  87.5 0.0 copy-done
  87.5 0.0 copy-done.1
  87.5 4.9 %rotate.1.away = bf16[2,16,1024,256]{3,2,1,0:T(8,128)(2,1)} custom-call(s32[1]{0:T(128)} %bitcast.where, s32[1,32]{1,0:T(1,128)} %index.1, f32[128,8,256]{2,1,0:T(8,128)} %copy-done, f32[128,8,256]{2,1,0:T(8,128)} %copy-done.1, f32[8,64,64]{2,1,0:T(8,128)} %mats_away.1), custom_call_target="tpu_custom_call" | custom-call | tf_op jit(solution)/shard_map/rotate/pallas_call | solution.py:274
  92.5 4.1 %all-to-all-done.2 = f32[32,4,8,128]{3,2,1,0:T(8,128)S(1)} async-done(((f32[32,4,8,128]{3,2,1,0:T(8,128)}), f32[32,4,8,128]{3,2,1,0:T(8,128)S(1)}, u32[]{:S(2)}, u32[]{:S(2)}) %all-to-all-start.2) | async-done | bytes 524320 | tf_op jit(solution)/shard_map/all_to_all | solution.py:200
  96.6 3.6 %collective-permute-start.5 = (f32[16,8,8,128]{3,2,1,0:T(8,128)S(1)}, f32[16,8,8,128]{3,2,1,0:T(8,128)S(1)}, u32[]{:S(2)}, u32[]{:S(2)}) collective-permute-start(f32[16,8,8,128]{3,2,1,0:T(8,128)S(1)} %bitcast.8), channel_id=1, source_target_pairs={{0,1},{1,0},{2,3},{3,2},{4,5},{5,4},{6,7},{7,6},{8,9},{9,8},{10,11... | collective-permute-start | bytes 1572872 | tf_op jit(solution)/shard_map/ppermute | solution.py:407
  100.2 1.5 %collective-permute-done.5.other = f32[16,8,8,128]{3,2,1,0:T(8,128)S(1)} collective-permute-done((f32[16,8,8,128]{3,2,1,0:T(8,128)S(1)}, f32[16,8,8,128]{3,2,1,0:T(8,128)S(1)}, u32[]{:S(2)}, u32[]{:S(2)}) %collective-permute-start.5) | collective-permute-done | bytes 524320 | tf_op jit(solution)/shard_map/ppermute | solution.py:407
  101.7 11.3 %outputs.1 = (f32[128,2,8,128]{3,2,1,0:T(8,128)}, f32[1,1024]{1,0:T(1,128)}) custom-call(s32[1]{0:T(128)} %bitcast.where, f32[16,8,8,128]{3,2,1,0:T(8,128)S(1)} %bitcast.9, f32[16,8,8,128]{3,2,1,0:T(8,128)S(1)} %collective-permute-done.5.other, bf16[1024,256]{1,0:T(8,128)(2,1)S(1)} %select_convert_fusion.table, bf16[2,16,1024,256]{3,2,1,0:T(8,128)(2,1)} %rotate.1.away), custom_call_target="tpu_custom_call" | custom-call | tf_op jit(solution)/shard_map/outputs/pallas_call | solution.py:380
  (1 shorter events, 0.0 us)
Async XLA Ops:
  4.2 46.8 %all-to-all-start = ((f32[256,8,128]{2,1,0:T(8,128)}), f32[256,8,128]{2,1,0:T(8,128)S(1)}, u32[]{:S(2)}, u32[]{:S(2)}) async-start(f32[256,8,128]{2,1,0:T(8,128)} %bitcast.10), calls=%async_computation | async-start | bytes 2097152 | tf_op jit(solution)/shard_map/all_to_all | solution.py:416
  54.6 32.9 %copy-start = (f32[128,8,256]{2,1,0:T(8,128)}, f32[128,8,256]{2,1,0:T(8,128)S(1)}, u32[]{:S(2)}) copy-start(f32[128,8,256]{2,1,0:T(8,128)S(1)} %get-tuple-element.17.own_away) | copy-start | bytes 3145732
  54.6 2.3 %collective-permute-start = (f32[16,8,8,128]{3,2,1,0:T(8,128)S(1)}, f32[16,8,8,128]{3,2,1,0:T(8,128)S(1)}, u32[]{:S(2)}, u32[]{:S(2)}) collective-permute-start(f32[16,8,8,128]{3,2,1,0:T(8,128)S(1)} %get-tuple-element.14), channel_id=1, source_target_pairs={{0,1},{1,0},{2,3},{3,2},{4,5},{5,4},{6,7},{7,6},{8,9},{9,8},{10,11... | collective-permute-start | bytes 1572872 | tf_op jit(solution)/shard_map/ppermute | solution.py:407
  57.0 15.1 %collective-permute-start.1 = (f32[128,8,256]{2,1,0:T(8,128)S(1)}, f32[128,8,256]{2,1,0:T(8,128)S(1)}, u32[]{:S(2)}, u32[]{:S(2)}) collective-permute-start(f32[128,8,256]{2,1,0:T(8,128)S(1)} %get-tuple-element.17.own_away), channel_id=1, source_target_pairs={{0,1},{1,0},{2,3},{3,2},{4,5},{5,4},{6,7},{7,6},{8,9},{9,8},{10,11... | collective-permute-start | bytes 3145736 | tf_op jit(solution)/shard_map/ppermute | solution.py:407
  72.1 15.4 %copy-start.1 = (f32[128,8,256]{2,1,0:T(8,128)}, f32[128,8,256]{2,1,0:T(8,128)S(1)}, u32[]{:S(2)}) copy-start(f32[128,8,256]{2,1,0:T(8,128)S(1)} %collective-permute-done.1.other_away) | copy-start | bytes 3145732
  72.2 4.3 %collective-permute-start.4 = (f32[4,8,128]{2,1,0:T(8,128)S(1)}, f32[4,8,128]{2,1,0:T(8,128)S(1)}, u32[]{:S(2)}, u32[]{:S(2)}) collective-permute-start(f32[4,8,128]{2,1,0:T(8,128)S(1)} %sum.1.refs_0_), channel_id=1, source_target_pairs={{0,48},{16,0},{32,16},{48,32},{2,50},{18,2},{34,18},{50,34},{4,52}... | collective-permute-start | bytes 49160 | tf_op jit(solution)/shard_map/ppermute | solution.py:215
  72.7 6.5 %collective-permute-start.3 = (f32[4,8,128]{2,1,0:T(8,128)S(1)}, f32[4,8,128]{2,1,0:T(8,128)S(1)}, u32[]{:S(2)}, u32[]{:S(2)}) collective-permute-start(f32[4,8,128]{2,1,0:T(8,128)S(1)} %sum.1.refs_0_), channel_id=1, source_target_pairs={{0,32},{16,48},{32,0},{48,16},{2,34},{18,50},{34,2},{50,18},{4,36}... | collective-permute-start | bytes 49160 | tf_op jit(solution)/shard_map/ppermute | solution.py:215
  76.5 5.0 %collective-permute-start.2 = (f32[4,8,128]{2,1,0:T(8,128)S(1)}, f32[4,8,128]{2,1,0:T(8,128)S(1)}, u32[]{:S(2)}, u32[]{:S(2)}) collective-permute-start(f32[4,8,128]{2,1,0:T(8,128)S(1)} %sum.1.refs_0_), channel_id=1, source_target_pairs={{0,16},{16,32},{32,48},{48,0},{2,18},{18,34},{34,50},{50,2},{4,20}... | collective-permute-start | bytes 49160 | tf_op jit(solution)/shard_map/ppermute | solution.py:215
  82.3 14.2 %all-to-all-start.2 = ((f32[32,4,8,128]{3,2,1,0:T(8,128)}), f32[32,4,8,128]{3,2,1,0:T(8,128)S(1)}, u32[]{:S(2)}, u32[]{:S(2)}) async-start(f32[32,4,8,128]{3,2,1,0:T(8,128)} %spread.1), calls=%async_computation.2 | async-start | bytes 1048576 | tf_op jit(solution)/shard_map/all_to_all | solution.py:200
  96.6 5.2 %collective-permute-start.5 = (f32[16,8,8,128]{3,2,1,0:T(8,128)S(1)}, f32[16,8,8,128]{3,2,1,0:T(8,128)S(1)}, u32[]{:S(2)}, u32[]{:S(2)}) collective-permute-start(f32[16,8,8,128]{3,2,1,0:T(8,128)S(1)} %bitcast.8), channel_id=1, source_target_pairs={{0,1},{1,0},{2,3},{3,2},{4,5},{5,4},{6,7},{7,6},{8,9},{9,8},{10,11... | collective-permute-start | bytes 1572872 | tf_op jit(solution)/shard_map/ppermute | solution.py:407

commit v9 on v8

--- a/solution.py
+++ b/solution.py
@@ -90,7 +90,7 @@
 def apply_gates(gates, layout, factor):
     order = gates.shape[1]
     away = pl.BlockSpec(memory_space=pltpu.HBM)
-    steps = 4
+    steps = 2
     return pl.pallas_call(
         lambda *refs: gate_kernel(order, *refs),
         out_shape=jax.ShapeDtypeStruct(factor.shape, F32),
@@ -173,27 +173,20 @@
     return slabs, lines
 
 
-def sum_kernel(parts, out):
-    out[...] = jnp.sum(parts[...], axis=0)
-
-
-def spread_kernel(*refs):
-    total = refs[0][...]
-    for part in refs[1:-1]:
-        total = total + part[...]
-    refs[-1][...] = jnp.broadcast_to(total[None], refs[-1].shape)
-
-
-def local(kernel, shape, name, *args):
+def spread_kernel(parts, out):
+    out[...] = jnp.broadcast_to(jnp.sum(parts[...], axis=0, keepdims=True), out.shape)
+
+
+def sum_and_spread(parts, copies):
     vmem = pl.BlockSpec(memory_space=pltpu.VMEM)
     return pl.pallas_call(
-        kernel,
-        out_shape=jax.ShapeDtypeStruct(shape, F32),
-        in_specs=[vmem] * len(args),
+        spread_kernel,
+        out_shape=jax.ShapeDtypeStruct((copies,) + parts.shape[1:], F32),
+        in_specs=[vmem],
         out_specs=vmem,
         compiler_params=params(4),
-        name=name,
-    )(*args)
+        name="spread",
+    )(parts)
 
 
 def exchange(pieces, members):
@@ -208,80 +201,63 @@
     tiles = part.shape[0] * part.shape[1] // members
     pieces = exchange(part.reshape((members, tiles) + part.shape[2:]), slabs)
     pieces, beside = lax.optimization_barrier((pieces, beside))
-    mine = local(sum_kernel, pieces.shape[1:], "sum", pieces)
-    terms = [mine]
-    for step in range(1, len(lines[0])):
-        pairs = [(at, line[(i + step) % len(line)]) for line in lines for i, at in enumerate(line)]
-        terms.append(lax.ppermute(mine, "wide", pairs))
-    copies = local(spread_kernel, pieces.shape, "spread", *terms)
-    total = exchange(copies, slabs)
+    pieces = exchange(sum_and_spread(pieces, len(lines[0])), lines)
+    total = exchange(sum_and_spread(pieces, members), slabs)
     return total.reshape(part.shape), beside
 
 
 PADDED = 16
 
 
-def rotate_kernel(
-    where, index, own_away, other_away, mats_away, kept,
-    own, other, mats, rotated, near, sems,
-):
+def rotate_kernel(where, index, own, other, mats_away, kept, rows, mats, rotated, turned, sems):
     count, lows, rank = own.shape
     order = mats.shape[1]
     group = order // (2 * lows)
     blocks = rotated.shape[0] // order
     core = where[0]
-    mine = core == 0
-    arrive = [
-        pltpu.make_async_copy(own_away, own, sems.at[0]),
-        pltpu.make_async_copy(other_away, other, sems.at[1]),
+    near = [
+        pltpu.make_async_copy(own, rows.at[core], sems.at[0]),
+        pltpu.make_async_copy(other, rows.at[1 - core], sems.at[1]),
         pltpu.make_async_copy(mats_away, mats, sems.at[2]),
     ]
-    for copy in arrive:
+    through = [pltpu.make_async_copy(rows, kept.at[:2], sems.at[3])]
+    for copy in near:
         copy.start()
-    for copy in arrive:
+    for copy in near:
         copy.wait()
-    for part, value in enumerate(split(own[...].reshape(count * lows, rank))):
-        near[part, core] = value
-    for part, value in enumerate(split(other[...].reshape(count * lows, rank))):
-        near[part, 1 - core] = value
-    leave = pltpu.make_async_copy(near.at[:, :2], kept.at[:, :2], sems.at[3])
-    leave.start()
+    through[0].start()
     for b in range(blocks):
         parts = []
         for g in range(group):
             w = core * (count // 2) + b * group + g
-            first, second = own[w], other[w]
-            parts.append(jnp.where(mine, first, second))
-            parts.append(jnp.where(mine, second, first))
+            parts += [rows[0, w], rows[1, w]]
         data = jnp.concatenate(parts, axis=0)
         value = mul3_rows(split(mats[index[0, core * blocks + b]]), split(data))
         rotated[b * order : (b + 1) * order, :] = value
     for q in range(rotated.shape[0] // rank):
-        rows = slice(q * rank, (q + 1) * rank)
-        for part, value in enumerate(split(rotated[rows, :].T)):
-            near[part, 2, rows] = value
-    last = pltpu.make_async_copy(near.at[:, 2], kept.at[:, 2], sems.at[4])
+        cut = slice(q * rank, (q + 1) * rank)
+        tile = rotated[cut, :].T
+        turned[q * rank // lows : (q + 1) * rank // lows] = tile.reshape(-1, lows, rank)
+    last = pltpu.make_async_copy(turned, kept.at[2], sems.at[4])
     last.start()
-    leave.wait()
-    last.wait()
+    for copy in through + [last]:
+        copy.wait()
 
 
 def rotate_sketch(where, index, own, other, bases):
     count, lows, rank = own.shape
-    rows = count * lows
     smem = pl.BlockSpec(memory_space=pltpu.SMEM)
     away = pl.BlockSpec(memory_space=pl.ANY)
     return pl.pallas_call(
         rotate_kernel,
-        out_shape=jax.ShapeDtypeStruct((2, PADDED, rows, rank), BF16),
+        out_shape=jax.ShapeDtypeStruct((PADDED,) + own.shape, F32),
         in_specs=[smem, smem, away, away, away],
         out_specs=away,
         scratch_shapes=[
+            pltpu.VMEM((2, count, lows, rank), F32),
+            pltpu.VMEM(bases.shape, F32),
+            pltpu.VMEM((count * lows, rank), F32),
             pltpu.VMEM(own.shape, F32),
-            pltpu.VMEM(own.shape, F32),
-            pltpu.VMEM(bases.shape, F32),
-            pltpu.VMEM((rows, rank), F32),
-            pltpu.VMEM((2, 3, rows, rank), BF16),
             pltpu.SemaphoreType.DMA((5,)),
         ],
         compiler_params=params(WHOLE),
@@ -317,11 +293,11 @@
     return held
 
 
-def output_kernel(where, mine, other, table, away, new, weights, proj, kept, new_near, sems):
+def output_kernel(where, mine, other, table, away, new, weights, proj, near, kept, new_near, sems):
     rank = proj.shape[0]
     halves = new.shape[1]
     width = rank // halves
-    fetch = pltpu.make_async_copy(away.at[:, : kept.shape[1]], kept, sems.at[2])
+    fetch = pltpu.make_async_copy(away.at[: near.shape[0]], near, sems.at[2])
     fetch.start()
     first = pl.ds(pl.multiple_of(where[0] * width, width), width)
     second = pl.ds(pl.multiple_of((1 - where[0]) * width, width), width)
@@ -341,6 +317,9 @@
     for part in blocks_of(p, rank):
         coeff = split(mul3(inv, part))
         core = core + mul3(coeff, coeff, NT)
+    fetch.wait()
+    for i in range(near.shape[0]):
+        kept[0, i], kept[1, i] = split(near[i].reshape(kept.shape[2:]))
     shift = frobenius(core) + 1e-6
     root = split(newton(core / shift, "approx"))
     scale = jnp.sqrt(shift)
@@ -354,7 +333,6 @@
         ],
         axis=0,
     )
-    fetch.wait()
     leave = []
     for c in range(halves):
         left = jnp.concatenate([kept[0, c], kept[1, c]], axis=1)
@@ -371,8 +349,9 @@
         copy.wait()
 
 
-def outputs(where, mine, other, table, kept, lows):
-    rows, rank = kept.shape[2:]
+def outputs(where, mine, other, table, kept):
+    count, lows, rank = kept.shape[1:]
+    rows = count * lows
     width = rank // 2
     smem = pl.BlockSpec(memory_space=pltpu.SMEM)
     vmem = pl.BlockSpec(memory_space=pltpu.VMEM)
@@ -387,6 +366,7 @@
         out_specs=(away, vmem),
         scratch_shapes=[
             pltpu.VMEM((rank, table.shape[0]), F32),
+            pltpu.VMEM((3, count, lows, rank), F32),
             pltpu.VMEM((2, 3, rows, rank), BF16),
             pltpu.VMEM((2, rows // lows, lows, width), F32),
             pltpu.SemaphoreType.DMA((3,)),
@@ -424,7 +404,7 @@
     total, other = sum_wide(part, swap(sketch))
     turned = rotate_sketch(where, basis_index, sketch, other, bases)
     total, turned = lax.optimization_barrier((total, turned))
-    new, weights = outputs(where, total, swap(total), table, turned, moved.shape[2])
+    new, weights = outputs(where, total, swap(total), table, turned)
     return new.reshape(rows, width), weights
 
 

time: 114 us -> 114 us (level)
  blocking collectives: 14.7 us -> 23.9 us
  starting transfers between devices: 29.9 us -> 25.5 us
  waiting for transfers between devices: 38.8 us -> 34.7 us
    all_to_all x1 -> x2, blocking collectives: 14.7 us -> 23.9 us  [exchange(): lax.all_to_all(pieces, 'wide', split_axis=0, concat_axis=0, axis_index_gr...]
    ppermute x3 -> x0, waiting for transfers between devices: 4.99 us -> none  [sum_wide(): terms.append(lax.ppermute(mine, 'wide', pairs))]
    ppermute x3 -> x0, starting transfers between devices: 4.29 us -> none  [sum_wide(): terms.append(lax.ppermute(mine, 'wide', pairs))]
  transfers between devices with their start and end apart: 8 -> 5, of which waited for: 6 -> 4; matrix products, arithmetic and copies ran while one was open for 3% -> 3% of each run, Pallas kernels for 4% -> 4%
where the time goes in v9:
time: 114 us; the launch traced here: 113 us
  waiting for transfers between devices  34.7 us (30%)
  starting transfers between devices  25.5 us (22%)
  blocking collectives  23.9 us (21%)
  Pallas kernels  23.7 us (21%)
  other arithmetic  3.86 us (3%)
  between operations  1.52 us (1%)
    all_to_all x1, waiting for transfers between devices, per_device(): lax.all_to_all(gated, ('wide', 'cols'), split_axis=0, concat_axis=0, tile...  26.6 us
    all_to_all x2, blocking collectives, exchange(): lax.all_to_all(pieces, 'wide', split_axis=0, concat_axis=0, axis_index_gr...  23.9 us
    all_to_all x1, starting transfers between devices, per_device(): lax.all_to_all(gated, ('wide', 'cols'), split_axis=0, concat_axis=0, tile...  15.7 us
    pallas_call x1, Pallas kernels, outputs(): pl.pallas_call(output_kernel, out_shape=(jax.ShapeDtypeStruct((rows // lo...  11.3 us
    all_to_all x1, starting transfers between devices, exchange(): lax.all_to_all(pieces, 'wide', split_axis=0, concat_axis=0, axis_index_gr...  5.65 us
    all_to_all x1, waiting for transfers between devices, exchange(): lax.all_to_all(pieces, 'wide', split_axis=0, concat_axis=0, axis_index_gr...  4.97 us
    pallas_call x1, Pallas kernels, rotate_sketch(): pl.pallas_call(rotate_kernel, out_shape=jax.ShapeDtypeStruct((PADDED,) +...  4.5 us
    ppermute x3, starting transfers between devices, swap(): return lax.ppermute(value, 'cols', [(0, 1), (1, 0)])  4.21 us
  transfers between devices with their start and end apart: 5, of which 4 were waited for; matrix products, arithmetic and copies ran while one was open for 3% of the time, Pallas kernels for 4%

profile of v9, /device:TPU:1, one launch (start us, length us, event | category | flops | bytes accessed | tf_op | source)
XLA Modules:
  0.0 113.3 jit_solution(235102676012455928)
XLA Ops:
  0.6 3.3 %gates.1 = f32[2048,128]{1,0:T(8,128)} custom-call(s32[16]{0:T(128)} %refs_0_.1, f32[8,128,128]{2,1,0:T(8,128)} %refs_1_.1, f32[2048,128]{1,0:T(8,128)} %refs_2_.1), custom_call_target="tpu_custom_call" | custom-call | tf_op jit(solution)/shard_map/gates/pallas_call | solution.py:94
  4.0 15.7 %all-to-all-start = ((f32[256,8,128]{2,1,0:T(8,128)}), f32[256,8,128]{2,1,0:T(8,128)S(1)}, u32[]{:S(2)}, u32[]{:S(2)}) async-start(f32[256,8,128]{2,1,0:T(8,128)} %bitcast.10), calls=%async_computation | async-start | bytes 2097152 | tf_op jit(solution)/shard_map/all_to_all | solution.py:396
  19.6 1.3 %fusion.6 = (f32[]{:T(128)}, f32[3]{0:T(128)S(1)}) fusion(f32[3]{0:T(128)} %param.12), kind=kLoop, calls=%fused_computation.19 | loop fusion | flops 2 | bytes 28 | tf_op jit(solution)/shard_map/reduce_sum | solution.py:400
  21.6 0.7 pad_add_fusion.flips
  22.3 0.1 pad_maximum_fusion.coefs
  22.4 0.7 fusion.3
  23.1 0.7 add_select_fusion.2
  23.8 0.3 select_convert_fusion.table
  24.1 26.6 %all-to-all-done = f32[256,8,128]{2,1,0:T(8,128)S(1)} async-done(((f32[256,8,128]{2,1,0:T(8,128)}), f32[256,8,128]{2,1,0:T(8,128)S(1)}, u32[]{:S(2)}, u32[]{:S(2)}) %all-to-all-start) | async-done | bytes 1048608 | tf_op jit(solution)/shard_map/all_to_all | solution.py:396
  50.7 3.7 %stack.1 = (f32[128,8,256]{2,1,0:T(8,128)S(1)}, f32[16,8,8,128]{3,2,1,0:T(8,128)S(1)}, f32[16,8,8,128]{3,2,1,0:T(8,128)S(1)}) custom-call(s32[1]{0:T(128)} %bitcast.where, s32[4]{0:T(128)S(1)} %pad_add_fusion.flips, f32[4]{0:T(128)S(1)} %pad_maximum_fusion.coefs, f32[128,2,8,128]{3,2,1,0:T(8,128)S(1)} %bitcast.7, bf16[1024,256]{1,0:T(8,128)(2,1)S(1)} %select_convert_fusion.table), custom_call_target="tpu_custom_call" | custom-call | tf_op jit(solution)/shard_map/stack/pallas_call | solution.py:151
  54.4 0.0 copy-start
  54.5 0.7 collective-permute-start
  55.2 1.5 %collective-permute-done = f32[16,8,8,128]{3,2,1,0:T(8,128)S(1)} collective-permute-done((f32[16,8,8,128]{3,2,1,0:T(8,128)S(1)}, f32[16,8,8,128]{3,2,1,0:T(8,128)S(1)}, u32[]{:S(2)}, u32[]{:S(2)}) %collective-permute-start) | collective-permute-done | bytes 524320 | tf_op jit(solution)/shard_map/ppermute | solution.py:387
  56.7 0.1 add.16
  56.8 0.5 collective-permute-start.1
  57.3 14.7 %all_to_all.20.parts = f32[32,4,8,128]{3,2,1,0:T(8,128)S(1)} all-to-all(f32[32,4,8,128]{3,2,1,0:T(8,128)S(1)} %bitcast.11), channel_id=1, replica_groups={{0,2,4,6,8,10,12,14,64,66,68,70,72,74,76,78,128,130,132,134,136,138,140..., dimensions={0} | all-to-all | bytes 1048576 | tf_op jit(solution)/shard_map/all_to_all | solution.py:193
  71.9 0.0 collective-permute-done.1.other
  72.0 9.3 %all_to_all.21.parts = f32[4,4,8,128]{3,2,1,0:T(8,128)S(1)} all-to-all(f32[4,4,8,128]{3,2,1,0:T(8,128)S(1)} %spread.2), channel_id=1, replica_groups={{0,16,32,48},{2,18,34,50},{4,20,36,52},{6,22,38,54},{8,24,40,56},{10,26..., dimensions={0} | all-to-all | bytes 131072 | tf_op jit(solution)/shard_map/all_to_all | solution.py:193
  81.2 0.9 spread.3
  82.1 5.7 %all-to-all-start.3 = ((f32[32,4,8,128]{3,2,1,0:T(8,128)}), f32[32,4,8,128]{3,2,1,0:T(8,128)S(1)}, u32[]{:S(2)}, u32[]{:S(2)}) async-start(f32[32,4,8,128]{3,2,1,0:T(8,128)} %spread.3), calls=%async_computation.3 | async-start | bytes 1048576 | tf_op jit(solution)/shard_map/all_to_all | solution.py:193
  87.8 0.0 copy-done
  87.8 4.5 %rotate.1.away = f32[16,128,8,256]{3,2,1,0:T(8,128)} custom-call(s32[1]{0:T(128)} %bitcast.where, s32[1,32]{1,0:T(1,128)} %index.1, f32[128,8,256]{2,1,0:T(8,128)} %copy-done, f32[128,8,256]{2,1,0:T(8,128)} %collective-permute-done.1.other, f32[8,64,64]{2,1,0:T(8,128)} %mats_away.1), custom_call_target="tpu_custom_call" | custom-call | tf_op jit(solution)/shard_map/rotate/pallas_call | solution.py:251
  92.3 5.0 %all-to-all-done.3 = f32[32,4,8,128]{3,2,1,0:T(8,128)S(1)} async-done(((f32[32,4,8,128]{3,2,1,0:T(8,128)}), f32[32,4,8,128]{3,2,1,0:T(8,128)S(1)}, u32[]{:S(2)}, u32[]{:S(2)}) %all-to-all-start.3) | async-done | bytes 524320 | tf_op jit(solution)/shard_map/all_to_all | solution.py:193
  97.2 3.0 %collective-permute-start.2 = (f32[16,8,8,128]{3,2,1,0:T(8,128)S(1)}, f32[16,8,8,128]{3,2,1,0:T(8,128)S(1)}, u32[]{:S(2)}, u32[]{:S(2)}) collective-permute-start(f32[16,8,8,128]{3,2,1,0:T(8,128)S(1)} %bitcast.8), channel_id=1, source_target_pairs={{0,1},{1,0},{2,3},{3,2},{4,5},{5,4},{6,7},{7,6},{8,9},{9,8},{10,11... | collective-permute-start | bytes 1572872 | tf_op jit(solution)/shard_map/ppermute | solution.py:387
  100.2 1.5 %collective-permute-done.2.other = f32[16,8,8,128]{3,2,1,0:T(8,128)S(1)} collective-permute-done((f32[16,8,8,128]{3,2,1,0:T(8,128)S(1)}, f32[16,8,8,128]{3,2,1,0:T(8,128)S(1)}, u32[]{:S(2)}, u32[]{:S(2)}) %collective-permute-start.2) | collective-permute-done | bytes 524320 | tf_op jit(solution)/shard_map/ppermute | solution.py:387
  101.8 11.3 %outputs.1 = (f32[128,2,8,128]{3,2,1,0:T(8,128)}, f32[1,1024]{1,0:T(1,128)}) custom-call(s32[1]{0:T(128)} %bitcast.where, f32[16,8,8,128]{3,2,1,0:T(8,128)S(1)} %bitcast.9, f32[16,8,8,128]{3,2,1,0:T(8,128)S(1)} %collective-permute-done.2.other, bf16[1024,256]{1,0:T(8,128)(2,1)S(1)} %select_convert_fusion.table, f32[16,128,8,256]{3,2,1,0:T(8,128)} %rotate.1.away), custom_call_target="tpu_custom_call" | custom-call | tf_op jit(solution)/shard_map/outputs/pallas_call | solution.py:359
  (1 shorter events, 0.0 us)
Async XLA Ops:
  4.0 46.8 %all-to-all-start = ((f32[256,8,128]{2,1,0:T(8,128)}), f32[256,8,128]{2,1,0:T(8,128)S(1)}, u32[]{:S(2)}, u32[]{:S(2)}) async-start(f32[256,8,128]{2,1,0:T(8,128)} %bitcast.10), calls=%async_computation | async-start | bytes 2097152 | tf_op jit(solution)/shard_map/all_to_all | solution.py:396
  54.4 33.3 %copy-start = (f32[128,8,256]{2,1,0:T(8,128)}, f32[128,8,256]{2,1,0:T(8,128)S(1)}, u32[]{:S(2)}) copy-start(f32[128,8,256]{2,1,0:T(8,128)S(1)} %get-tuple-element.17.own) | copy-start | bytes 3145732
  54.5 2.3 %collective-permute-start = (f32[16,8,8,128]{3,2,1,0:T(8,128)S(1)}, f32[16,8,8,128]{3,2,1,0:T(8,128)S(1)}, u32[]{:S(2)}, u32[]{:S(2)}) collective-permute-start(f32[16,8,8,128]{3,2,1,0:T(8,128)S(1)} %get-tuple-element.14), channel_id=1, source_target_pairs={{0,1},{1,0},{2,3},{3,2},{4,5},{5,4},{6,7},{7,6},{8,9},{9,8},{10,11... | collective-permute-start | bytes 1572872 | tf_op jit(solution)/shard_map/ppermute | solution.py:387
  56.8 15.1 %collective-permute-start.1 = (f32[128,8,256]{2,1,0:T(8,128)S(1)}, f32[128,8,256]{2,1,0:T(8,128)}, u32[]{:S(2)}, u32[]{:S(2)}) collective-permute-start(f32[128,8,256]{2,1,0:T(8,128)S(1)} %get-tuple-element.17.own), channel_id=1, source_target_pairs={{0,1},{1,0},{2,3},{3,2},{4,5},{5,4},{6,7},{7,6},{8,9},{9,8},{10,11... | collective-permute-start | bytes 3145736 | tf_op jit(solution)/shard_map/ppermute | solution.py:387
  82.1 15.1 %all-to-all-start.3 = ((f32[32,4,8,128]{3,2,1,0:T(8,128)}), f32[32,4,8,128]{3,2,1,0:T(8,128)S(1)}, u32[]{:S(2)}, u32[]{:S(2)}) async-start(f32[32,4,8,128]{3,2,1,0:T(8,128)} %spread.3), calls=%async_computation.3 | async-start | bytes 1048576 | tf_op jit(solution)/shard_map/all_to_all | solution.py:193
  97.2 4.5 %collective-permute-start.2 = (f32[16,8,8,128]{3,2,1,0:T(8,128)S(1)}, f32[16,8,8,128]{3,2,1,0:T(8,128)S(1)}, u32[]{:S(2)}, u32[]{:S(2)}) collective-permute-start(f32[16,8,8,128]{3,2,1,0:T(8,128)S(1)} %bitcast.8), channel_id=1, source_target_pairs={{0,1},{1,0},{2,3},{3,2},{4,5},{5,4},{6,7},{7,6},{8,9},{9,8},{10,11... | collective-permute-start | bytes 1572872 | tf_op jit(solution)/shard_map/ppermute | solution.py:387
